TPU v7x, 32 devices: a whole 2x2x4 slice. The times are simulated.
32 devices in a mesh: groups: 2 (over y), seq: 4 (over x, core), head: 4 (over z).
Axes of the slice: x: 2, y: 2, z: 4, core: 2. Of those that a mesh axis runs over, the one named last changes fastest.
Arguments:
- lin_qkv: bfloat16 [8192, 3, 2048], P(('groups', 'seq'), None, 'head'), parts along dimension 0, may hold values from -6 to 6
- level_weights: float32 [16, 16], P(None, 'head'), may hold values from 0.3 to 1.7
- soft_q: bfloat16 [8192, 2048], P(('groups', 'seq'), 'head'), parts along dimension 0, may hold values from -6 to 6
- soft_kv: bfloat16 [8192, 2, 256], P(('groups', 'seq')), parts along dimension 0, may hold values from -6 to 6
Outputs:
- mixed: bfloat16 [8192, 2, 2048], P(('groups', 'seq'), None, 'head'), parts along dimension 0
There are 2 independent parts, one for each index of `groups`. A program takes and returns all parts, laid end to end along the dimension named above; an argument that names none is the same for every part. Nothing has to cross between parts.
All inputs are finite; a program needn't handle non-finite values.
Results may differ from a plain program's by a relative error of at most 0.0049.
Values may be sent and summed in bfloat16 or wider, within the bound.
No kernel may reach another device: no remote copies, remote signals or barrier semaphores. Data moves between devices by JAX's collectives and lax.ppermute only.
A program may use at most 128 MiB of HBM per device.

v0:
```python
import jax
import jax.numpy as jnp
from jax import lax
from jax.sharding import PartitionSpec as P

HD = 128
HEADS_SM = 16
KV_HEADS = 2
WINDOW = 1024
LEVELS = 16


def partner_2(value, axis, distance):
    mask = 2**distance
    pairs = [(source, source ^ mask) for source in range(lax.axis_size(axis))]
    return lax.ppermute(value, axis, pairs)


def passed_along(x, axis, by):
    size = lax.axis_size(axis)
    pairs = [(i, i + by) for i in range(size) if 0 <= i + by < size]
    return lax.ppermute(x, axis, pairs)


def bit_count(values):
    total = jnp.zeros_like(values)
    for power in range(LEVELS):
        total = total + (values >= 2**power).astype(jnp.int32)
    return total


def local(lin_qkv, level_weights, soft_q, soft_kv):
    tok = lin_qkv.shape[0]
    heads = lin_qkv.shape[2] // HD
    local_bits = tok.bit_length() - 1
    block = min(512, tok)
    my_seq = lax.axis_index("seq")
    query = lin_qkv[:, 0].reshape(tok, heads, HD)
    keys = lin_qkv[:, 1].reshape(tok, heads, HD)
    values = lin_qkv[:, 2].reshape(tok, heads, HD)
    state = jnp.einsum("thd,the->hde", keys, values, preferred_element_type=jnp.float32)
    group_sum = state
    cross_state = jnp.zeros((heads, HD, HD), jnp.float32)
    for bit_pos in range(lax.axis_size("seq").bit_length() - 1):
        partner = partner_2(group_sum, "seq", bit_pos)
        upper = jnp.right_shift(my_seq, bit_pos) % 2 == 1
        factor = jnp.where(upper, level_weights[local_bits + bit_pos + 1], 0.0)
        cross_state = cross_state + factor[:, None, None] * partner
        group_sum = group_sum + partner
    cross_state = cross_state.astype(jnp.bfloat16)
    pieces = []
    for index in range(tok // block):
        start = index * block
        end = start + block
        q_block = query[start:end]
        scores = jnp.einsum("ahd,jhd->haj", q_block, keys[:end], preferred_element_type=jnp.float32)
        rows = start + jnp.arange(block, dtype=jnp.int32)[:, None]
        cols = jnp.arange(end, dtype=jnp.int32)[None, :]
        levels = bit_count(jnp.bitwise_xor(rows, cols))
        weight = jnp.zeros((heads, block, end), jnp.float32)
        for lev in range(local_bits + 1):
            weight = (
                weight
                + (levels == lev).astype(jnp.float32)[None] * level_weights[lev][:, None, None]
            )
        weight = jnp.where((cols <= rows)[None], weight, 0.0)
        weighted = (scores * weight).astype(jnp.bfloat16)
        intra = jnp.einsum(
            "haj,jhd->ahd", weighted, values[:end], preferred_element_type=jnp.float32
        )
        cross = jnp.einsum("ahd,hde->ahe", q_block, cross_state, preferred_element_type=jnp.float32)
        pieces.append(intra + cross)
    lin_sum = jnp.concatenate(pieces, axis=0)
    normed = lin_sum * lax.rsqrt(jnp.mean(lin_sum * lin_sum, axis=-1, keepdims=True) + 1e-06)
    lin_out = normed.astype(jnp.bfloat16).reshape(tok, heads * HD)
    q_heads = soft_q.shape[1] // HD
    group = HEADS_SM // KV_HEADS
    kv_index = lax.axis_index("head") * q_heads // group
    own_kv = lax.dynamic_slice_in_dim(soft_kv, kv_index * HD, HD, 2)
    tail = own_kv.reshape(WINDOW, 2 * HD)
    before = passed_along(tail, "seq", 1).reshape(WINDOW, 2, HD)
    extended = jnp.concatenate([before, own_kv], axis=0)
    soft_q_heads = soft_q.reshape(tok, q_heads, HD)
    scale = 1.0 / HD**0.5
    soft_pieces = []
    for index in range(tok // block):
        start = index * block
        q_block = soft_q_heads[start : start + block]
        kv_block = extended[start : start + WINDOW + block]
        scores = (
            jnp.einsum("ahd,jd->haj", q_block, kv_block[:, 0], preferred_element_type=jnp.float32)
            * scale
        )
        rows = jnp.arange(block, dtype=jnp.int32)[:, None]
        cols = jnp.arange(WINDOW + block, dtype=jnp.int32)[None, :]
        valid = (
            (cols >= rows) & (cols <= rows + WINDOW) & (my_seq * tok + start + cols - WINDOW >= 0)
        )
        scores = jnp.where(valid[None], scores, -1e30)
        probs = jax.nn.softmax(scores, axis=-1).astype(jnp.bfloat16)
        out = jnp.einsum("haj,jd->ahd", probs, kv_block[:, 1], preferred_element_type=jnp.float32)
        soft_pieces.append(out.astype(jnp.bfloat16))
    soft_out = jnp.concatenate(soft_pieces, axis=0).reshape(tok, q_heads * HD)
    return jnp.stack([lin_out, soft_out], axis=1)


def solution(mesh):
    in_specs = (
        P(("groups", "seq"), None, "head"),
        P(None, "head"),
        P(("groups", "seq"), "head"),
        P(("groups", "seq"), None, None),
    )
    out_specs = P(("groups", "seq"), None, "head")
    return jax.shard_map(local, mesh=mesh, in_specs=in_specs, out_specs=out_specs, check_vma=False)
```

profile of v0, /device:TPU:1, one launch (start us, length us, event | category | flops | bytes accessed | tf_op | source)
XLA Modules:
  0.0 150.0 jit_solution(18333500294727288441)
XLA Ops:
  0.0 0.0 copy-start
  0.0 3.1 %fusion.86 = (bf16[1024,1,512]{2,0,1:T(8,128)(2,1)}, bf16[1024,1,512]{2,0,1:T(8,128)(2,1)}) fusion(bf16[1024,3,512]{2,0,1:T(8,128)(2,1)} %param.4), kind=kLoop, calls=%fused_computation.152 | loop fusion | bytes 4194304 | tf_op jit(solution)/shard_map/slice | solution.py:39
  3.1 1.5 copy.75
  4.6 2.3 %copy.119 = bf16[1024,1,512]{0,2,1:T(8,128)(2,1)} copy(bf16[1024,1,512]{2,0,1:T(8,128)(2,1)} %get-tuple-element.23) | data formatting | bytes 2097152
  6.9 2.4 %fusion.90 = f32[4,128,128]{2,1,0:T(8,128)} fusion(bf16[1024,4,128]{0,2,1:T(8,128)(2,1)S(1)} %bitcast.88, bf16[1024,4,128]{0,2,1:T(8,128)(2,1)} %bitcast.90), kind=kOutput, calls=%fused_computation.156 | convolution fusion | flops 134217728 | bytes 2359296 | tf_op jit(solution)/shard_map/thd,the->hde/dot_general | solution.py:41
  9.2 0.0 collective-permute-start
  9.3 0.0 copy-done
  9.3 0.4 constant_dynamic-slice_fusion
  9.6 1.1 copy.89
  10.8 4.5 %collective-permute-start.2 = (bf16[1024,256]{0,1:T(8,128)(2,1)}, bf16[1024,256]{0,1:T(8,128)(2,1)}, u32[]{:S(2)}, u32[]{:S(2)}) collective-permute-start(bf16[1024,256]{0,1:T(8,128)(2,1)} %bitcast.13), channel_id=1, source_target_pairs={{0,4},{4,8},{8,12},{1,5},{5,9},{9,13},{2,6},{6,10},{10,14},{3,7},{... | collective-permute-start | bytes 1572872 | tf_op jit(solution)/shard_map/ppermute | solution.py:22
  15.3 2.7 %fusion.85 = (bf16[512,1,512]{2,0,1:T(8,128)(2,1)}, bf16[512,1,512]{2,0,1:T(8,128)(2,1)}, bf16[512,1,512]{2,0,1:T(8,128)(2,1)S(1)}, bf16[512,1,512]{2,0,1:T(8,128)(2,1)}) fusion(bf16[1024,3,512]{2,0,1:T(8,128)(2,1)} %param.4), kind=kLoop, calls=%fused_computation.151 | loop fusion | bytes 4194304 | tf_op jit(solution)/shard_map/slice | solution.py:56
  18.0 1.8 %compare_convert_fusion.12 = (f32[512,512]{1,0:T(8,128)}, f32[512,512]{1,0:T(8,128)}) fusion(), kind=kLoop, calls=%fused_computation.100 | loop fusion | flops 13631488 | bytes 2097152 | tf_op jit(solution)/shard_map/convert_element_type | solution.py:64
  19.7 1.8 %compare_convert_fusion.14 = (f32[512,512]{1,0:T(8,128)}, f32[512,512]{1,0:T(8,128)}) fusion(), kind=kLoop, calls=%fused_computation.102 | loop fusion | flops 13631488 | bytes 2097152 | tf_op jit(solution)/shard_map/convert_element_type | solution.py:64
  21.5 1.7 %compare_convert_fusion.16 = (f32[512,512]{1,0:T(8,128)}, f32[512,512]{1,0:T(8,128)}) fusion(), kind=kLoop, calls=%fused_computation.104 | loop fusion | flops 13631488 | bytes 2097152 | tf_op jit(solution)/shard_map/convert_element_type | solution.py:64
  23.2 1.8 %compare_convert_fusion.18 = (f32[512,512]{1,0:T(8,128)}, f32[512,512]{1,0:T(8,128)}) fusion(), kind=kLoop, calls=%fused_computation.106 | loop fusion | flops 13631488 | bytes 2097152 | tf_op jit(solution)/shard_map/convert_element_type | solution.py:64
  25.0 1.7 %compare_convert_fusion.20 = (f32[512,512]{1,0:T(8,128)}, f32[512,512]{1,0:T(8,128)}) fusion(), kind=kLoop, calls=%fused_computation.108 | loop fusion | flops 13631488 | bytes 2097152 | tf_op jit(solution)/shard_map/convert_element_type | solution.py:64
  26.7 1.4 iota_compare_fusion.3
  28.2 9.7 %iota_compare_fusion.2 = (pred[512,1024]{1,0:T(8,128)(4,1)}, f32[512,1024]{1,0:T(8,128)}, f32[512,1024]{1,0:T(8,128)}, f32[512,1024]{1,0:T(8,128)}, f32[512,1024...) fusion(s32[512]{0:T(512)S(1)} %iota_add_fusion.1), kind=kLoop, calls=%fused_computation.50 | loop fusion | flops 37224448 | bytes 23595008 | tf_op jit(solution)/shard_map/le | solution.py:66
  37.9 0.0 copy-start.7
  37.9 0.0 copy-start.2
  37.9 1.0 copy.120
  38.9 1.3 copy.117
  40.2 0.0 copy-start.4
  40.2 2.2 %copy.118 = bf16[512,1,512]{0,2,1:T(8,128)(2,1)} copy(bf16[512,1,512]{2,0,1:T(8,128)(2,1)} %get-tuple-element.18) | data formatting | bytes 1048576
  42.4 2.1 %copy.74 = bf16[512,1,512]{0,2,1:T(8,128)(2,1)} copy(bf16[512,1,512]{2,0,1:T(8,128)(2,1)} %get-tuple-element.21) | data formatting | bytes 1048576 | tf_op jit(solution)/shard_map/slice | solution.py:69
  44.5 0.0 copy-done.7
  44.5 0.4 select_reduce_fusion.1
  44.9 0.0 copy-done.2
  44.9 13.8 %fusion.40 = f32[512,4,128]{0,2,1:T(8,128)} fusion(bf16[1024,4,128]{0,2,1:T(8,128)(2,1)S(1)} %bitcast.91, f32[4]{0:T(128)S(1)} %get-tuple-element.6, f32[512,1024]{1,0:T(8,128)} %get-tuple-element.36, f32[4]{0:T(128)S(1)} %get-tuple-element.7, f32[512,1024]{1,0:T(8,128)} %get-tuple-element.35, f32[4]{0:T(128)S(1)} %get-tuple-element.8, ...), kind=kOutput, calls=%fused_computation.68 | convolution fusion | flops 1124073472 | bytes 27263152 | tf_op jit(solution)/shard_map/haj,jhd->ahd/dot_general | solution.py:68
  58.7 0.0 copy-done.4
  58.7 10.4 %fusion.37 = f32[512,4,128]{0,2,1:T(8,128)} fusion(bf16[512,4,128]{0,2,1:T(8,128)(2,1)} %bitcast.99, bf16[512,4,128]{0,2,1:T(8,128)(2,1)S(1)} %bitcast.94, bf16[512,4,128]{0,2,1:T(8,128)(2,1)} %bitcast.98, f32[4]{0:T(128)S(1)} %get-tuple-element.6, f32[512,512]{1,0:T(8,128)} %get-tuple-element.47, f32[4]{0:T(128)S(1)} %get-tuple-element.7, ...), kind=kOutput, calls=%fused_computation.63 | convolution fusion | flops 562036736 | bytes 14418096 | tf_op jit(solution)/shard_map/haj,jhd->ahd/dot_general | solution.py:68
  69.2 2.4 %fusion.17 = (pred[512,1536]{0,1:T(8,128)(4,1)}, pred[512,1536]{0,1:T(8,128)(4,1)}) fusion(s32[512]{0:T(512)S(1)} %iota_add_fusion, pred[1536]{0:T(1024)(128)(4,1)S(1)} %get-tuple-element.45, pred[1536]{0:T(1024)(128)(4,1)S(1)} %get-tuple-element.44), kind=kLoop, calls=%fused_computation.26 | loop fusion | flops 3932160 | bytes 1577984 | tf_op jit(solution)/shard_map/and | solution.py:97
  71.6 0.1 copy.121
  71.6 0.0 collective-permute-done
  71.6 1.0 add.1912
  72.6 0.1 collective-permute-start.1
  72.7 1.3 fusion.87
  74.0 1.0 copy.122
  75.0 1.0 copy.123
  76.0 4.1 %collective-permute-done.1 = f32[4,128,128]{2,1,0:T(8,128)S(1)} collective-permute-done((f32[4,128,128]{2,1,0:T(8,128)S(1)}, f32[4,128,128]{2,1,0:T(8,128)S(1)}, u32[]{:S(2)}, u32[]{:S(2)}) %collective-permute-start.1) | collective-permute-done | bytes 262176 | tf_op jit(solution)/shard_map/ppermute | solution.py:16
  80.1 0.1 add_convert_fusion
  80.2 0.0 copy-done.5
  80.2 1.6 %fusion.38 = f32[512,4,128]{0,2,1:T(8,128)S(1)} fusion(f32[512,4,128]{0,2,1:T(8,128)} %fusion.40, bf16[4,128,128]{2,1,0:T(8,128)(2,1)S(1)} %add_convert_fusion, bf16[512,4,128]{0,2,1:T(8,128)(2,1)S(1)} %bitcast.97), kind=kOutput, calls=%fused_computation.65 | convolution fusion | flops 67371008 | bytes 2752512 | tf_op jit(solution)/shard_map/ahd,hde->ahe/dot_general | solution.py:71
  81.8 1.7 %fusion.39 = f32[512,4,128]{0,2,1:T(8,128)S(1)} fusion(f32[512,4,128]{0,2,1:T(8,128)} %fusion.37, bf16[4,128,128]{2,1,0:T(8,128)(2,1)S(1)} %add_convert_fusion, bf16[512,4,128]{0,2,1:T(8,128)(2,1)} %bitcast.95), kind=kOutput, calls=%fused_computation.67 | convolution fusion | flops 67371008 | bytes 2752512 | tf_op jit(solution)/shard_map/ahd,hde->ahe/dot_general | solution.py:71
  83.5 0.2 fusion.19
  83.8 1.0 copy.87
  84.8 1.9 %copy.86 = f32[512,1,512]{2,1,0:T(1,128)} copy(f32[512,1,512]{0,2,1:T(8,128)S(1)} %bitcast.84) | data formatting | bytes 2097152 | tf_op jit(solution)/shard_map/concatenate | solution.py:73
  86.7 2.0 %copy.85 = f32[512,1,512]{2,1,0:T(1,128)} copy(f32[512,1,512]{0,2,1:T(8,128)S(1)} %bitcast.85) | data formatting | bytes 2097152 | tf_op jit(solution)/shard_map/concatenate | solution.py:73
  88.7 0.0 collective-permute-done.2
  88.7 1.3 copy.90
  90.0 0.0 copy-start.3
  90.0 7.4 %fusion.69 = f32[1536,512,4]{1,0,2:T(8,128)} fusion(bf16[512,4,128]{0,2,1:T(8,128)(2,1)} %bitcast.92, bf16[1024,2,128]{2,0,1:T(8,128)(2,1)S(1)} %copy.90, bf16[1024,2,128]{2,0,1:T(8,128)(2,1)S(1)} %copy.121), kind=kOutput, calls=%fused_computation.116 | convolution fusion | flops 806092800 | bytes 14155776 | tf_op jit(solution)/shard_map/ahd,jd->haj/dot_general | solution.py:91
  97.5 0.0 copy-done.3
  97.5 1.8 %fusion.72 = f32[1536,512,4]{1,0,2:T(8,128)S(1)} fusion(bf16[512,4,128]{0,2,1:T(8,128)(2,1)S(1)} %bitcast.93, bf16[1024,2,128]{2,0,1:T(8,128)(2,1)S(1)} %copy.121, bf16[1024,2,128]{2,0,1:T(8,128)(2,1)S(1)} %copy.90), kind=kOutput, calls=%fused_computation.119 | convolution fusion | flops 806092800 | bytes 14155776 | tf_op jit(solution)/shard_map/ahd,jd->haj/dot_general | solution.py:91
  99.3 14.5 %fusion.89 = (f32[4,512]{1,0:T(4,128)S(1)}, f32[4,512,1536]{1,2,0:T(8,128)}) fusion(f32[1536,512,4]{1,0,2:T(8,128)} %fusion.69, pred[512,1536]{0,1:T(8,128)(4,1)} %get-tuple-element.38), kind=kOutput, calls=%fused_computation.155 | output fusion | flops 18875904 | bytes 25960448 | tf_op jit(solution)/shard_map/sub | solution.py:100
  113.8 6.4 %fusion.43 = bf16[512,4,128]{0,2,1:T(8,128)(2,1)} fusion(f32[4,512,1536]{1,2,0:T(8,128)} %get-tuple-element.43, f32[4,512]{1,0:T(4,128)S(1)} %get-tuple-element.42, bf16[1024,2,128]{2,0,1:T(8,128)(2,1)S(1)} %copy.90, bf16[1024,2,128]{2,0,1:T(8,128)(2,1)S(1)} %copy.121), kind=kOutput, calls=%fused_computation.77 | convolution fusion | flops 812646400 | bytes 14163968 | tf_op jit(solution)/shard_map/haj,jd->ahd/dot_general | solution.py:101
  120.2 10.0 %fusion.88 = (f32[4,512]{1,0:T(4,128)S(1)}, f32[4,512,1536]{1,2,0:T(8,128)}) fusion(f32[1536,512,4]{1,0,2:T(8,128)S(1)} %fusion.72, pred[512,1536]{0,1:T(8,128)(4,1)} %get-tuple-element.39), kind=kOutput, calls=%fused_computation.154 | output fusion | flops 18875904 | bytes 25960448 | tf_op jit(solution)/shard_map/sub | solution.py:100
  130.2 5.6 %fusion.44 = bf16[512,4,128]{0,2,1:T(8,128)(2,1)S(1)} fusion(f32[4,512,1536]{1,2,0:T(8,128)} %get-tuple-element.41, f32[4,512]{1,0:T(4,128)S(1)} %get-tuple-element.40, bf16[1024,2,128]{2,0,1:T(8,128)(2,1)S(1)} %copy.90, bf16[1024,2,128]{2,0,1:T(8,128)(2,1)S(1)} %copy.121), kind=kOutput, calls=%fused_computation.78 | convolution fusion | flops 812646400 | bytes 14163968 | tf_op jit(solution)/shard_map/haj,jd->ahd/dot_general | solution.py:101
  135.8 0.1 pad_maximum_fusion.1
  135.9 1.8 %copy.99 = bf16[1024,1,512]{2,1,0:T(2,128)(2,1)S(1)} copy(bf16[1024,1,512]{0,2,1:T(8,128)(2,1)S(1)} %bitcast.87) | data formatting | bytes 2097152 | tf_op jit(solution)/shard_map/stack;reshape | solution.py:104
  137.8 2.2 %mul.456 = f32[1024,4,128]{2,1,0:T(4,128)S(1)} broadcast(f32[1024,4]{1,0:T(8,128)} %copy.87), dimensions={0,1} | broadcast | bytes 2113536 | tf_op jit(solution)/shard_map/mul | solution.py:74
  140.0 0.0 copy-start.1
  140.0 4.4 %fusion.18 = bf16[1024,1,512]{2,1,0:T(2,128)(2,1)S(1)} fusion(f32[1024,1,512]{2,1,0:T(1,128)S(1)} %bitcast.86, f32[512,1,512]{2,1,0:T(1,128)} %copy.86, f32[512,1,512]{2,1,0:T(1,128)} %copy.85), kind=kLoop, calls=%fused_computation.28 | loop fusion | flops 1572864 | bytes 5242880 | tf_op jit(solution)/shard_map/convert_element_type | solution.py:75
  144.4 5.6 %pad_maximum_fusion = bf16[1024,2,512]{2,1,0:T(2,128)(2,1)} fusion(bf16[1024,1,512]{2,1,0:T(2,128)(2,1)S(1)} %copy.99, bf16[1024,1,512]{2,1,0:T(2,128)(2,1)S(1)} %fusion.18), kind=kLoop, calls=%fused_computation.31 | loop fusion | flops 4194304 | bytes 4194304 | tf_op jit(solution)/shard_map/stack | solution.py:104
  (8 shorter events, 0.0 us)
Async XLA Ops:
  0.0 9.3 %copy-start = (bf16[1024,2,256]{2,1,0:T(2,128)(2,1)S(1)}, bf16[1024,2,256]{2,1,0:T(2,128)(2,1)}, u32[]{:S(2)}) copy-start(bf16[1024,2,256]{2,1,0:T(2,128)(2,1)} %param.7) | copy-start | bytes 3145732
  9.2 62.4 %collective-permute-start = (f32[4,128,128]{2,1,0:T(8,128)}, f32[4,128,128]{2,1,0:T(8,128)S(1)}, u32[]{:S(2)}, u32[]{:S(2)}) collective-permute-start(f32[4,128,128]{2,1,0:T(8,128)} %fusion.90), channel_id=1, source_target_pairs={{0,4},{4,0},{8,12},{12,8},{1,5},{5,1},{9,13},{13,9},{2,6},{6,2},{1... | collective-permute-start | bytes 786440 | tf_op jit(solution)/shard_map/ppermute | solution.py:16
  10.8 77.9 %collective-permute-start.2 = (bf16[1024,256]{0,1:T(8,128)(2,1)}, bf16[1024,256]{0,1:T(8,128)(2,1)}, u32[]{:S(2)}, u32[]{:S(2)}) collective-permute-start(bf16[1024,256]{0,1:T(8,128)(2,1)} %bitcast.13), channel_id=1, source_target_pairs={{0,4},{4,8},{8,12},{1,5},{5,9},{9,13},{2,6},{6,10},{10,14},{3,7},{... | collective-permute-start | bytes 1572872 | tf_op jit(solution)/shard_map/ppermute | solution.py:22
  37.9 6.6 %copy-start.7 = (f32[16,4]{0,1:T(4,128)S(1)}, f32[16,4]{0,1:T(4,128)}, u32[]{:S(2)}) copy-start(f32[16,4]{0,1:T(4,128)} %param.5) | copy-start | bytes 772
  37.9 7.0 %copy-start.2 = (bf16[1024,1,512]{0,2,1:T(8,128)(2,1)S(1)}, bf16[1024,1,512]{0,2,1:T(8,128)(2,1)}, u32[]{:S(2)}) copy-start(bf16[1024,1,512]{0,2,1:T(8,128)(2,1)} %copy.119) | copy-start | bytes 3145732
  40.2 18.6 %copy-start.4 = (bf16[512,1,512]{0,2,1:T(8,128)(2,1)}, bf16[512,1,512]{0,2,1:T(8,128)(2,1)S(1)}, u32[]{:S(2)}) copy-start(bf16[512,1,512]{0,2,1:T(8,128)(2,1)S(1)} %copy.117) | copy-start | bytes 1572868
  69.2 11.0 %copy-start.5 = (bf16[512,1,512]{0,2,1:T(8,128)(2,1)S(1)}, bf16[512,1,512]{0,2,1:T(8,128)(2,1)}, u32[]{:S(2)}) copy-start(bf16[512,1,512]{0,2,1:T(8,128)(2,1)} %copy.120) | copy-start | bytes 1572868
  72.6 7.4 %collective-permute-start.1 = (f32[4,128,128]{2,1,0:T(8,128)S(1)}, f32[4,128,128]{2,1,0:T(8,128)S(1)}, u32[]{:S(2)}, u32[]{:S(2)}) collective-permute-start(f32[4,128,128]{2,1,0:T(8,128)S(1)} %add.1912), channel_id=1, source_target_pairs={{0,8},{4,12},{8,0},{12,4},{1,9},{5,13},{9,1},{13,5},{2,10},{6,14},... | collective-permute-start | bytes 786440 | tf_op jit(solution)/shard_map/ppermute | solution.py:16
  90.0 7.5 %copy-start.3 = (bf16[512,512]{0,1:T(8,128)(2,1)S(1)}, bf16[512,512]{0,1:T(8,128)(2,1)}, u32[]{:S(2)}) copy-start(bf16[512,512]{0,1:T(8,128)(2,1)} %copy.123) | copy-start | bytes 1572868
  130.2 5.7 %copy-start.6 = (bf16[512,4,128]{0,2,1:T(8,128)(2,1)S(1)}, bf16[512,4,128]{0,2,1:T(8,128)(2,1)}, u32[]{:S(2)}) copy-start(bf16[512,4,128]{0,2,1:T(8,128)(2,1)} %fusion.43) | copy-start | bytes 1572868
  140.0 10.1 %copy-start.1 = (bf16[1024,2,256]{2,1,0:T(2,128)(2,1)S(1)}, bf16[1024,2,256]{2,1,0:T(2,128)(2,1)}, u32[]{:S(2)}) copy-start(bf16[1024,2,256]{2,1,0:T(2,128)(2,1)} %param.7) | copy-start | bytes 3145732
where the time goes:
time: 151 us; the launch traced here: 150 us
  other arithmetic  58.7 us (39%)
  matrix products  51.2 us (34%)
  local copies, waits for them, and re-layouts  31.3 us (21%)
  starting transfers between devices  4.56 us (3%)
  waiting for transfers between devices  4.06 us (3%)
    sub x2, other arithmetic, local(): probs = jax.nn.softmax(scores, axis=-1).astype(jnp.bfloat16)  24.5 us
    dot_general x2, matrix products, local(): jnp.einsum('haj,jhd->ahd', weighted, values[:end], preferred_element_type...  24.3 us
    dot_general x2, matrix products, local(): jnp.einsum('haj,jd->ahd', probs, kv_block[:, 1], preferred_element_type=j...  12 us
    le x2, other arithmetic, local(): weight = jnp.where((cols <= rows)[None], weight, 0.0)  11.2 us
    dot_general x2, matrix products, local(): jnp.einsum('ahd,jd->haj', q_block, kv_block[:, 0], preferred_element_type...  9.22 us
    unnamed x23, local copies, waits for them, and re-layouts  8.89 us
    convert_element_type x5, other arithmetic, local(): (levels == lev).astype(jnp.float32)[None]  8.75 us
    another operation x1, other arithmetic, local(): return jnp.stack([lin_out, soft_out], axis=1)  5.62 us
  transfers between devices with their start and end apart: 3, of which 1 were waited for; matrix products, arithmetic and copies ran while one was open for 47% of the time, Pallas kernels for 0%

commit v1 on v0

v1 whole, which is shorter than its diff:
```python
import functools

import jax
import jax.numpy as jnp
import numpy as np
from jax import lax
from jax.experimental import pallas as pl
from jax.experimental.pallas import tpu as pltpu
from jax.sharding import PartitionSpec as P

HD = 128
HEADS_SM = 16
KV_HEADS = 2
WINDOW = 1024
CHUNK = 128
NEG = -1e30
F32 = jnp.float32
BF16 = jnp.bfloat16


def partner_2(value, axis, distance):
    mask = 2**distance
    pairs = [(source, source ^ mask) for source in range(lax.axis_size(axis))]
    return lax.ppermute(value, axis, pairs)


def passed_along(x, axis, by):
    size = lax.axis_size(axis)
    pairs = [(i, i + by) for i in range(size) if 0 <= i + by < size]
    return lax.ppermute(x, axis, pairs)


def nt_dot(a, b):
    return lax.dot_general(a, b, (((1,), (1,)), ((), ())), preferred_element_type=F32)


def tn_dot(a, b):
    return lax.dot_general(a, b, (((0,), (0,)), ((), ())), preferred_element_type=F32)


def states_kernel(heads, x_ref, state_ref):
    step = pl.program_id(0)
    for h in range(heads):
        lanes = slice(h * HD, (h + 1) * HD)
        part = tn_dot(x_ref[1, :, lanes], x_ref[2, :, lanes])

        @pl.when(step == 0)
        def _():
            state_ref[h] = part

        @pl.when(step > 0)
        def _():
            state_ref[h] += part


def states_call(planes):
    _, tok, width = planes.shape
    heads = width // HD
    rows = min(256, tok)
    return pl.pallas_call(
        functools.partial(states_kernel, heads),
        grid=(tok // rows,),
        in_specs=[pl.BlockSpec((3, rows, width), lambda i: (0, i, 0))],
        out_specs=pl.BlockSpec((heads, HD, HD), lambda i: (0, 0, 0)),
        out_shape=jax.ShapeDtypeStruct((heads, HD, HD), F32),
    )(planes)


def layer_kernel(
    heads, q_heads, block, first_ref, table_ref, x_ref, cross_ref, sq_ref, kb_ref, ko_ref, out_ref,
    stage, k_all, v_all, states, rows_out,
):
    tok = x_ref.shape[1]
    first = first_ref[0] > 0
    scale = float(np.log2(np.e) / np.sqrt(HD))
    for part, ref in enumerate((kb_ref, ko_ref)):
        here = pl.ds(part * tok, tok)
        stage[...] = ref[...].astype(F32)
        keys = stage[pl.ds(0, tok, stride=2), :] * scale
        high = keys.astype(BF16)
        k_all[here, 0:HD] = high
        k_all[here, HD : 2 * HD] = (keys - high.astype(F32)).astype(BF16)
        v_all[here, 0:HD] = stage[pl.ds(1, tok, stride=2), :].astype(BF16)
    v_all[:, HD : 2 * HD] = jnp.ones((2 * tok, HD), BF16)

    chunks = tok // CHUNK
    chunk_bits = CHUNK.bit_length() - 1
    row = lax.broadcasted_iota(jnp.int32, (CHUNK, CHUNK), 0)
    col = lax.broadcasted_iota(jnp.int32, (CHUNK, CHUNK), 1)
    differ = jnp.bitwise_xor(row, col)
    causal = col <= row
    stride = 2 * q_heads
    for h in range(heads):
        lanes = slice(h * HD, (h + 1) * HD)
        weight = jnp.full((CHUNK, CHUNK), table_ref[h, 0], F32)
        for level in range(1, chunk_bits + 1):
            weight = jnp.where(differ >= 2 ** (level - 1), table_ref[h, level], weight)
        weight = jnp.where(causal, weight, 0.0)
        groups = {}
        for c in range(chunks):
            here = slice(c * CHUNK, (c + 1) * CHUNK)
            q = x_ref[0, here, lanes]
            k = x_ref[1, here, lanes]
            v = x_ref[2, here, lanes]
            prefix = cross_ref[h]
            bit = 0
            while (1 << bit) <= c:
                if (c >> bit) & 1:
                    prefix = prefix + table_ref[h, chunk_bits + bit + 1] * states[groups[bit, (c >> bit) - 1]]
                bit += 1
            tile = (nt_dot(q, k) * weight).astype(BF16)
            total = jnp.dot(
                jnp.concatenate([tile, q], axis=1),
                jnp.concatenate([v, prefix.astype(BF16)], axis=0),
                preferred_element_type=F32,
            )
            norm = total * lax.rsqrt(jnp.mean(total * total, axis=1, keepdims=True) + 1e-06)
            rows_out[pl.ds(c * CHUNK * stride + 2 * h, CHUNK, stride=stride), :] = norm
            if c < chunks - 1:
                state = tn_dot(k, v)
                bit, index = 0, c
                slot = len(groups)
                groups[0, c] = slot
                states[slot] = state
                while index & 1:
                    state = states[groups[bit, index - 1]] + state
                    bit, index = bit + 1, index >> 1
                    slot = len(groups)
                    groups[bit, index] = slot
                    states[slot] = state

    row = lax.broadcasted_iota(jnp.int32, (block, block), 0)
    col = lax.broadcasted_iota(jnp.int32, (block, block), 1)
    low = jnp.where(col >= row, 0.0, NEG).astype(F32)
    high = jnp.where(col <= row, 0.0, NEG).astype(F32)
    for index in range(tok // block):
        start = index * block
        before = tok - start
        for h in range(q_heads):
            q = sq_ref[start : start + block, h * HD : (h + 1) * HD]
            scores = nt_dot(jnp.concatenate([q, q], axis=1), k_all[start : start + tok + block, :])
            left = scores[:, :block] + low
            if before > block:
                left = jnp.concatenate([left, scores[:, block:before]], axis=1)
            right = scores[:, tok:] + high
            if before < tok:
                right = jnp.concatenate([scores[:, before:tok], right], axis=1)
            m_left = jnp.max(left, axis=1, keepdims=True)
            m_right = jnp.max(right, axis=1, keepdims=True)
            m = jnp.where(first, m_right, jnp.maximum(m_left, m_right))
            m_left = jnp.where(first, 1e30, m)
            probs = jnp.concatenate(
                [jnp.exp2(left - m_left).astype(BF16), jnp.exp2(right - m).astype(BF16)], axis=1
            )
            out = jnp.dot(probs, v_all[start : start + tok + block, :], preferred_element_type=F32)
            rows_out[pl.ds(start * stride + 2 * h + 1, block, stride=stride), :] = out[:, :HD] / out[:, HD:]
    out_ref[...] = rows_out[...].astype(BF16)


def layer_call(first, table, planes, cross, soft_q, kb, ko):
    _, tok, width = planes.shape
    heads = width // HD
    q_heads = soft_q.shape[1] // HD
    block = min(256, tok)
    smem = pl.BlockSpec(memory_space=pltpu.SMEM)
    vmem = pl.BlockSpec(memory_space=pltpu.VMEM)
    return pl.pallas_call(
        functools.partial(layer_kernel, heads, q_heads, block),
        in_specs=[smem, smem, vmem, vmem, vmem, vmem, vmem],
        out_specs=vmem,
        out_shape=jax.ShapeDtypeStruct((tok * 2 * q_heads, HD), BF16),
        scratch_shapes=[
            pltpu.VMEM((2 * tok, HD), F32),
            pltpu.VMEM((2 * tok, 2 * HD), BF16),
            pltpu.VMEM((2 * tok, 2 * HD), BF16),
            pltpu.VMEM((2 * (tok // CHUNK), HD, HD), F32),
            pltpu.VMEM((tok * 2 * q_heads, HD), F32),
        ],
    )(first, table, planes, cross, soft_q, kb, ko)


def local(lin_qkv, level_weights, soft_q, soft_kv):
    tok = lin_qkv.shape[0]
    heads = lin_qkv.shape[2] // HD
    q_heads = soft_q.shape[1] // HD
    group = HEADS_SM // KV_HEADS
    local_bits = tok.bit_length() - 1
    my_seq = lax.axis_index("seq")

    kv_index = lax.axis_index("head") * q_heads // group
    own_kv = lax.dynamic_slice_in_dim(soft_kv, kv_index * HD, HD, 2).reshape(2 * tok, HD)
    before = passed_along(own_kv, "seq", 1)

    planes = jnp.transpose(lin_qkv, (1, 0, 2))
    state = states_call(planes)
    group_sum = state
    cross_state = jnp.zeros((heads, HD, HD), F32)
    for bit_pos in range(lax.axis_size("seq").bit_length() - 1):
        partner = partner_2(group_sum, "seq", bit_pos)
        upper = jnp.right_shift(my_seq, bit_pos) % 2 == 1
        factor = jnp.where(upper, level_weights[local_bits + bit_pos + 1], 0.0)
        cross_state = cross_state + factor[:, None, None] * partner
        group_sum = group_sum + partner

    first = (my_seq == 0).astype(jnp.int32).reshape(1)
    table = jnp.transpose(level_weights)
    out = layer_call(first, table, planes, cross_state, soft_q, before, own_kv)
    out = out.reshape(tok, q_heads, 2, HD).transpose(0, 2, 1, 3)
    return out.reshape(tok, 2, q_heads * HD)


def solution(mesh):
    in_specs = (
        P(("groups", "seq"), None, "head"),
        P(None, "head"),
        P(("groups", "seq"), "head"),
        P(("groups", "seq"), None, None),
    )
    out_specs = P(("groups", "seq"), None, "head")
    return jax.shard_map(local, mesh=mesh, in_specs=in_specs, out_specs=out_specs, check_vma=False)
```

time: 151 us -> 40.8 us (0.27)
  other arithmetic: 58.7 us -> 2 us
  matrix products: 51.2 us -> 0 us
  local copies, waits for them, and re-layouts: 31.3 us -> 1.16 us
  Pallas kernels: 0 us -> 22.3 us
  waiting for transfers between devices: 4.06 us -> 10.4 us
    dot_general x9 -> x0, matrix products: 51.2 us -> none  [the longest x2 24.3 us: local(): jnp.einsum('haj,jhd->ahd', weighted, values[:end], preferred_element_type...]
    sub x2 -> x0, other arithmetic: 24.5 us -> none  [local(): probs = jax.nn.softmax(scores, axis=-1).astype(jnp.bfloat16)]
    pallas_call x0 -> x2, Pallas kernels: none -> 22.3 us  [the longest x1 16.7 us: layer_call(): pl.pallas_call(functools.partial(layer_kernel, heads, q_heads, block), in...]
    convert_element_type x7 -> x0, other arithmetic: 13.3 us -> none  [the longest x5 8.75 us: local(): (levels == lev).astype(jnp.float32)[None]]
    le x2 -> x0, other arithmetic: 11.2 us -> none  [local(): weight = jnp.where((cols <= rows)[None], weight, 0.0)]
    slice x5 -> x0, local copies, waits for them, and re-layouts: 10.6 us -> none  [the longest x2 4.58 us: local(): keys = lin_qkv[:, 1].reshape(tok, heads, HD)]
    unnamed x23 -> x8, local copies, waits for them, and re-layouts: 8.89 us -> 0.8 us
    ppermute x2, waiting for transfers between devices: 4.06 us -> 10.4 us  [partner_2(): return lax.ppermute(value, axis, pairs)]
  transfers between devices with their start and end apart: 3 -> 3, of which waited for: 1 -> 1; matrix products, arithmetic and copies ran while one was open for 47% -> 6% of each run, Pallas kernels for 0% -> 0%
where the time goes in v1:
time: 40.8 us; the launch traced here: 40.6 us
  Pallas kernels  22.3 us (55%)
  waiting for transfers between devices  10.4 us (25%)
  starting transfers between devices  4.57 us (11%)
  other arithmetic  2 us (5%)
  local copies, waits for them, and re-layouts  1.16 us (3%)
    pallas_call x1, Pallas kernels, layer_call(): pl.pallas_call(functools.partial(layer_kernel, heads, q_heads, block), in...  16.7 us
    ppermute x2, waiting for transfers between devices, partner_2(): return lax.ppermute(value, axis, pairs)  10.4 us
    pallas_call x1, Pallas kernels, states_call(): pl.pallas_call(functools.partial(states_kernel, heads), grid=(tok // rows...  5.63 us
    ppermute x1, starting transfers between devices, passed_along(): return lax.ppermute(x, axis, pairs)  4.49 us
    add x1, other arithmetic, local(): group_sum = group_sum + partner  0.98 us
  transfers between devices with their start and end apart: 3, of which 1 were waited for; matrix products, arithmetic and copies ran while one was open for 6% of the time, Pallas kernels for 0%

profile of v1, /device:TPU:1, one launch (start us, length us, event | category | flops | bytes accessed | tf_op | source)
XLA Modules:
  0.0 40.6 jit_solution(10090746972958642413)
XLA Ops:
  0.0 0.0 copy-start
  0.0 0.0 copy-start.3
  0.0 5.6 %shard_map.46 = f32[4,128,128]{2,1,0:T(8,128)} custom-call(bf16[3,1024,512]{2,1,0:T(8,128)(2,1)} %bitcast.9), custom_call_target="tpu_custom_call" | custom-call | tf_op jit(solution)/shard_map/pallas_call | solution.py:60
  5.6 0.0 collective-permute-start
  5.6 0.0 copy-done
  5.6 0.4 constant_dynamic-slice_fusion
  6.0 0.0 copy-start.1
  6.0 4.5 %collective-permute-start.2 = (bf16[2048,128]{1,0:T(8,128)(2,1)S(1)}, bf16[2048,128]{1,0:T(8,128)(2,1)S(1)}, u32[]{:S(2)}, u32[]{:S(2)}) collective-permute-start(bf16[2048,128]{1,0:T(8,128)(2,1)S(1)} %bitcast.11), channel_id=1, source_target_pairs={{0,4},{4,8},{8,12},{1,5},{5,9},{9,13},{2,6},{6,10},{10,14},{3,7},{... | collective-permute-start | bytes 1572872 | tf_op jit(solution)/shard_map/ppermute | solution.py:30
  10.5 0.0 collective-permute-done
  10.5 1.0 %add.19 = f32[4,128,128]{2,1,0:T(8,128)S(1)} add(f32[4,128,128]{2,1,0:T(8,128)} %shard_map.46, f32[4,128,128]{2,1,0:T(8,128)S(1)} %collective-permute-done) | non-fusion elementwise | flops 65536 | bytes 786432 | tf_op jit(solution)/shard_map/add | solution.py:203
  11.5 0.1 collective-permute-start.1
  11.6 0.0 copy-done.3
  11.6 0.2 select_reduce_fusion.1
  11.8 10.4 %collective-permute-done.1 = f32[4,128,128]{2,1,0:T(8,128)S(1)} collective-permute-done((f32[4,128,128]{2,1,0:T(8,128)S(1)}, f32[4,128,128]{2,1,0:T(8,128)S(1)}, u32[]{:S(2)}, u32[]{:S(2)}) %collective-permute-start.1) | collective-permute-done | bytes 262176 | tf_op jit(solution)/shard_map/ppermute | solution.py:24
  22.2 0.8 %multiply_add_fusion.cross_ref = f32[4,128,128]{2,1,0:T(8,128)} fusion(f32[4,128,128]{2,1,0:T(8,128)S(1)} %collective-permute-done.1, f32[4,128,128]{2,1,0:T(8,128)S(1)} %collective-permute-done, f32[4]{0:T(128)S(1)} %get-tuple-element.6, f32[4]{0:T(128)S(1)} %get-tuple-element.5), kind=kLoop, calls=%fused_computation | loop fusion | flops 196608 | bytes 786464 | tf_op jit(solution)/shard_map/add | solution.py:202
  23.0 0.0 collective-permute-done.2.kb_ref
  23.1 0.0 copy-start.2
  23.1 0.0 copy-done.1
  23.1 0.8 %copy-done.2 = bf16[2048,128]{1,0:T(8,128)(2,1)} copy-done((bf16[2048,128]{1,0:T(8,128)(2,1)}, bf16[2048,128]{1,0:T(8,128)(2,1)S(1)}, u32[]{:S(2)}) %copy-start.2) | copy-done | bytes 524312
  23.8 16.7 %shard_map.47 = bf16[8192,128]{1,0:T(8,128)(2,1)} custom-call(s32[1]{0:T(128)} %bitcast.first_ref, f32[4,16]{1,0:T(4,128)} %bitcast.13, bf16[3,1024,512]{2,1,0:T(8,128)(2,1)} %bitcast.10, f32[4,128,128]{2,1,0:T(8,128)} %multiply_add_fusion.cross_ref, bf16[1024,512]{1,0:T(8,128)(2,1)} %sq_ref.1, bf16[2048,128]{1,0:T(8,128)(2,1)} %copy-done.2, ...), custom_call_target="tpu_custom_call" | custom-call | tf_op jit(solution)/shard_map/pallas_call | solution.py:167
Async XLA Ops:
  0.0 5.6 %copy-start = (bf16[1024,2,256]{2,1,0:T(2,128)(2,1)S(1)}, bf16[1024,2,256]{2,1,0:T(2,128)(2,1)}, u32[]{:S(2)}) copy-start(bf16[1024,2,256]{2,1,0:T(2,128)(2,1)} %param.7) | copy-start | bytes 3145732
  0.0 11.6 %copy-start.3 = (f32[16,4]{0,1:T(4,128)S(1)}, f32[16,4]{0,1:T(4,128)}, u32[]{:S(2)}) copy-start(f32[16,4]{0,1:T(4,128)} %param.5) | copy-start | bytes 772
  5.6 4.9 %collective-permute-start = (f32[4,128,128]{2,1,0:T(8,128)}, f32[4,128,128]{2,1,0:T(8,128)S(1)}, u32[]{:S(2)}, u32[]{:S(2)}) collective-permute-start(f32[4,128,128]{2,1,0:T(8,128)} %shard_map.46), channel_id=1, source_target_pairs={{0,4},{4,0},{8,12},{12,8},{1,5},{5,1},{9,13},{13,9},{2,6},{6,2},{1... | collective-permute-start | bytes 786440 | tf_op jit(solution)/shard_map/ppermute | solution.py:24
  6.0 17.0 %copy-start.1 = (bf16[1024,2,128]{2,1,0:T(2,128)(2,1)}, bf16[1024,2,128]{2,1,0:T(2,128)(2,1)S(1)}, u32[]{:S(2)}) copy-start(bf16[1024,2,128]{2,1,0:T(2,128)(2,1)S(1)} %constant_dynamic-slice_fusion) | copy-start | bytes 1572868
  6.0 17.0 %collective-permute-start.2 = (bf16[2048,128]{1,0:T(8,128)(2,1)S(1)}, bf16[2048,128]{1,0:T(8,128)(2,1)S(1)}, u32[]{:S(2)}, u32[]{:S(2)}) collective-permute-start(bf16[2048,128]{1,0:T(8,128)(2,1)S(1)} %bitcast.11), channel_id=1, source_target_pairs={{0,4},{4,8},{8,12},{1,5},{5,9},{9,13},{2,6},{6,10},{10,14},{3,7},{... | collective-permute-start | bytes 1572872 | tf_op jit(solution)/shard_map/ppermute | solution.py:30
  11.5 10.7 %collective-permute-start.1 = (f32[4,128,128]{2,1,0:T(8,128)S(1)}, f32[4,128,128]{2,1,0:T(8,128)S(1)}, u32[]{:S(2)}, u32[]{:S(2)}) collective-permute-start(f32[4,128,128]{2,1,0:T(8,128)S(1)} %add.19), channel_id=1, source_target_pairs={{0,8},{4,12},{8,0},{12,4},{1,9},{5,13},{9,1},{13,5},{2,10},{6,14},... | collective-permute-start | bytes 786440 | tf_op jit(solution)/shard_map/ppermute | solution.py:24
  23.1 0.8 %copy-start.2 = (bf16[2048,128]{1,0:T(8,128)(2,1)}, bf16[2048,128]{1,0:T(8,128)(2,1)S(1)}, u32[]{:S(2)}) copy-start(bf16[2048,128]{1,0:T(8,128)(2,1)S(1)} %collective-permute-done.2.kb_ref) | copy-start | bytes 1572868

commit v2 on v1

v2 whole, which is shorter than its diff:
```python
import functools

import jax
import jax.numpy as jnp
import numpy as np
from jax import lax
from jax.experimental import pallas as pl
from jax.experimental.pallas import tpu as pltpu
from jax.sharding import PartitionSpec as P


HD = 128
HEADS_SM = 16
KV_HEADS = 2
CHUNK = 256
NEG = -1e30
FAR = 1e30
F32 = jnp.float32
BF16 = jnp.bfloat16
SCALE = float(np.log2(np.e) / np.sqrt(HD))
ANY = pl.BlockSpec(memory_space=pl.ANY)
SMEM = pl.BlockSpec(memory_space=pltpu.SMEM)
PARAMS = pltpu.CompilerParams(vmem_limit_bytes=32 * 2**20)


def partner_2(value, axis, distance):
    mask = 2**distance
    pairs = [(source, source ^ mask) for source in range(lax.axis_size(axis))]
    return lax.ppermute(value, axis, pairs)


def passed_along(x, axis, by):
    size = lax.axis_size(axis)
    pairs = [(i, i + by) for i in range(size) if 0 <= i + by < size]
    return lax.ppermute(x, axis, pairs)


def nt_dot(a, b):
    return lax.dot_general(a, b, (((1,), (1,)), ((), ())), preferred_element_type=F32)


def tn_dot(a, b):
    return lax.dot_general(a, b, (((0,), (0,)), ((), ())), preferred_element_type=F32)


def lanes(h):
    return slice(h * HD, (h + 1) * HD)


def states_kernel(heads, k_ref, v_ref, state_ref):
    @pl.when(pl.program_id(0) == 0)
    def _():
        state_ref[...] = jnp.zeros_like(state_ref)

    for h in range(heads):
        state_ref[h] += tn_dot(k_ref[0, :, lanes(h)], v_ref[0, :, lanes(h)])


def states_call(planes):
    _, tok, width = planes.shape
    heads = width // HD
    rows = tok // 2
    return pl.pallas_call(
        functools.partial(states_kernel, heads),
        grid=(tok // rows,),
        in_specs=[
            pl.BlockSpec((1, rows, width), lambda i: (1, i, 0)),
            pl.BlockSpec((1, rows, width), lambda i: (2, i, 0)),
        ],
        out_specs=pl.BlockSpec((heads, HD, HD), lambda i: (0, 0, 0)),
        out_shape=jax.ShapeDtypeStruct((heads, HD, HD), F32),
        compiler_params=PARAMS,
        cost_estimate=pl.CostEstimate(
            flops=2 * tok * width * HD, bytes_accessed=4 * tok * width, transcendentals=0
        ),
    )(planes, planes)


def linear_kernel(heads, table_ref, x_hbm, out_hbm, x_ref, out_ref, states, in_sems, out_sems):
    tok = x_ref.shape[1]
    chunks = tok // CHUNK
    bits = CHUNK.bit_length() - 1
    rows = [pl.ds(c * CHUNK, CHUNK) for c in range(chunks)]
    loads = [
        pltpu.make_async_copy(x_hbm.at[:, rows[c], :], x_ref.at[:, rows[c], :], in_sems.at[c])
        for c in range(chunks)
    ]
    for load in loads:
        load.start()
    row = lax.broadcasted_iota(jnp.int32, (CHUNK, CHUNK), 0)
    col = lax.broadcasted_iota(jnp.int32, (CHUNK, CHUNK), 1)
    differ = jnp.bitwise_xor(row, col)
    weights = []
    for h in range(heads):
        weight = jnp.full((CHUNK, CHUNK), table_ref[h, 0], F32)
        for level in range(1, bits + 1):
            weight = jnp.where(differ >= 2 ** (level - 1), table_ref[h, level], weight)
        weights.append(jnp.where(col <= row, weight, 0.0))
    groups = [{} for _ in range(heads)]
    stores = []
    for c in range(chunks):
        loads[c].wait()
        for h in range(heads):
            base = h * 2 * chunks
            q, k, v = (x_ref[part, rows[c], lanes(h)] for part in range(3))
            tile = (nt_dot(q, k) * weights[h]).astype(BF16)
            prefix, bit = None, 0
            while (1 << bit) <= c:
                if (c >> bit) & 1:
                    term = table_ref[h, bits + bit + 1] * states[base + groups[h][bit, (c >> bit) - 1]]
                    prefix = term if prefix is None else prefix + term
                bit += 1
            if prefix is None:
                total = jnp.dot(tile, v, preferred_element_type=F32)
            else:
                total = jnp.dot(
                    jnp.concatenate([tile, q], axis=1),
                    jnp.concatenate([v, prefix.astype(BF16)], axis=0),
                    preferred_element_type=F32,
                )
            out_ref[rows[c], lanes(h)] = total
            if c < chunks - 1:
                state, bit, index = tn_dot(k, v), 0, c
                slot = len(groups[h])
                groups[h][0, c] = slot
                states[base + slot] = state
                while index & 1:
                    state = states[base + groups[h][bit, index - 1]] + state
                    bit, index = bit + 1, index >> 1
                    slot = len(groups[h])
                    groups[h][bit, index] = slot
                    states[base + slot] = state
        store = pltpu.make_async_copy(out_ref.at[rows[c], :], out_hbm.at[rows[c], :], out_sems.at[c])
        store.start()
        stores.append(store)
    for store in stores:
        store.wait()


def linear_call(table, planes):
    _, tok, width = planes.shape
    heads = width // HD
    chunks = tok // CHUNK
    return pl.pallas_call(
        functools.partial(linear_kernel, heads),
        in_specs=[SMEM, ANY],
        out_specs=ANY,
        out_shape=jax.ShapeDtypeStruct((tok, width), F32),
        scratch_shapes=[
            pltpu.VMEM((3, tok, width), BF16),
            pltpu.VMEM((tok, width), F32),
            pltpu.VMEM((heads * 2 * chunks, HD, HD), F32),
            pltpu.SemaphoreType.DMA((chunks,)),
            pltpu.SemaphoreType.DMA((chunks,)),
        ],
        compiler_params=PARAMS,
        cost_estimate=pl.CostEstimate(
            flops=8 * tok * width * CHUNK, bytes_accessed=10 * tok * width, transcendentals=0
        ),
    )(table, planes)


def take_apart(pairs, stage, k_all, v_all, at, count):
    here = pl.ds(at, count)
    rows = pl.ds(2 * at, 2 * count)
    stage[rows, :] = pairs.astype(F32)
    keys = stage[pl.ds(2 * at, count, stride=2), :] * SCALE
    high = keys.astype(BF16)
    k_all[here, 0:HD] = high
    k_all[here, HD : 2 * HD] = (keys - high.astype(F32)).astype(BF16)
    v_all[here, 0:HD] = stage[pl.ds(2 * at + 1, count, stride=2), :].astype(BF16)
    v_all[here, HD : 2 * HD] = jnp.ones((count, HD), BF16)


def edge_masks(block):
    row = lax.broadcasted_iota(jnp.int32, (block, block), 0)
    col = lax.broadcasted_iota(jnp.int32, (block, block), 1)
    low = jnp.where(col >= row, 0.0, NEG).astype(F32)
    high = jnp.where(col <= row, 0.0, NEG).astype(F32)
    return low, high


def softmax_block(q, keys, values, before, masks, first):
    low, high = masks
    block, width = q.shape[0], keys.shape[0]
    scores = nt_dot(jnp.concatenate([q, q], axis=1), keys)
    left = scores[:, :block] + low
    if before > block:
        left = jnp.concatenate([left, scores[:, block:before]], axis=1)
    right = scores[:, width - block :] + high
    if before < width - block:
        right = jnp.concatenate([scores[:, before : width - block], right], axis=1)
    m_left = jnp.max(left, axis=1, keepdims=True)
    m_right = jnp.max(right, axis=1, keepdims=True)
    m = jnp.where(first, m_right, jnp.maximum(m_left, m_right))
    m_left = jnp.where(first, FAR, m)
    probs = jnp.concatenate([jnp.exp2(left - m_left).astype(BF16), jnp.exp2(right - m).astype(BF16)], axis=1)
    out = jnp.dot(probs, values, preferred_element_type=F32)
    return out[:, :HD] / out[:, HD:]


def late_kernel(q_heads, block, first_ref, q_ref, before_ref, own_ref, out_ref, stage, k_all, v_all):
    half = q_ref.shape[0]
    tok = 2 * half
    first = first_ref[0] > 0
    take_apart(before_ref[...], stage, k_all, v_all, 0, half)
    take_apart(own_ref[...], stage, k_all, v_all, half, tok)
    masks = edge_masks(block)
    for start in range(0, half, block):
        keys = k_all[start : start + tok + block, :]
        values = v_all[start : start + tok + block, :]
        for h in range(q_heads):
            q = q_ref[start : start + block, lanes(h)]
            out = softmax_block(q, keys, values, half - start, masks, first)
            out_ref[start : start + block, lanes(h)] = out.astype(BF16)


def late_call(first, soft_q, before_late, own_kv, block):
    tok, width = soft_q.shape
    half = tok // 2
    q_heads = width // HD
    whole = lambda i: (0, 0)
    return pl.pallas_call(
        functools.partial(late_kernel, q_heads, block),
        grid=(1,),
        in_specs=[
            SMEM,
            pl.BlockSpec((half, width), lambda i: (1, 0)),
            pl.BlockSpec(before_late.shape, whole),
            pl.BlockSpec(own_kv.shape, whole),
        ],
        out_specs=pl.BlockSpec((half, width), whole),
        out_shape=jax.ShapeDtypeStruct((half, width), BF16),
        scratch_shapes=[
            pltpu.VMEM((3 * tok, HD), F32),
            pltpu.VMEM((tok + half, 2 * HD), BF16),
            pltpu.VMEM((tok + half, 2 * HD), BF16),
        ],
        compiler_params=PARAMS,
        cost_estimate=pl.CostEstimate(
            flops=6 * half * tok * width, bytes_accessed=6 * tok * width, transcendentals=half * tok * q_heads
        ),
    )(first, soft_q, before_late, own_kv)


def last_kernel(
    heads, block, first_ref, q_hbm, lin_hbm, x_hbm, cross_hbm, early_hbm, late_hbm, own_hbm, soft_hbm, out_hbm,
    q_ref, lin_ref, x_ref, cross_ref, early_ref, late_ref, own_ref, soft_ref, mixed, packed,
    stage, k_all, v_all, in_sems, out_sems,
):
    half = q_ref.shape[0]
    tok = 2 * half
    first = first_ref[0] > 0
    stride = 2 * heads
    copies = [
        (late_hbm, late_ref),
        (early_hbm, early_ref),
        (own_hbm.at[pl.ds(0, tok), :], own_ref),
        (q_hbm.at[pl.ds(0, half), :], q_ref),
        (cross_hbm, cross_ref),
        (x_hbm.at[0], x_ref),
        (lin_hbm, lin_ref),
        (soft_hbm, soft_ref),
    ]
    loads = [pltpu.make_async_copy(src, dst, in_sems.at[i]) for i, (src, dst) in enumerate(copies)]
    for load in loads:
        load.start()
    masks = edge_masks(block)
    stores = []

    def linear_rows(start):
        rows = slice(start, start + block)
        for h in range(heads):
            total = lin_ref[rows, lanes(h)] + jnp.dot(
                x_ref[rows, lanes(h)], cross_ref[h].astype(BF16), preferred_element_type=F32
            )
            norm = total * lax.rsqrt(jnp.mean(total * total, axis=1, keepdims=True) + 1e-06)
            mixed[pl.ds(start * stride + 2 * h, block, stride=stride), :] = norm

    def send(start):
        rows = pl.ds(start * stride, block * stride)
        packed[rows, :] = mixed[rows, :].astype(BF16)
        store = pltpu.make_async_copy(packed.at[rows, :], out_hbm.at[rows, :], out_sems.at[start // block])
        store.start()
        stores.append(store)

    loads[0].wait()
    loads[1].wait()
    take_apart(early_ref[...], stage, k_all, v_all, 0, half)
    take_apart(late_ref[...], stage, k_all, v_all, half, half)
    loads[2].wait()
    take_apart(own_ref[...], stage, k_all, v_all, tok, half)
    loads[3].wait()
    for start in range(0, half, block):
        keys = k_all[start : start + tok + block, :]
        values = v_all[start : start + tok + block, :]
        for h in range(heads):
            out = softmax_block(q_ref[start : start + block, lanes(h)], keys, values, tok - start, masks, first)
            mixed[pl.ds(start * stride + 2 * h + 1, block, stride=stride), :] = out
        if start == 0:
            for load in loads[4:]:
                load.wait()
        linear_rows(start)
        send(start)
    for start in range(half, tok, block):
        for h in range(heads):
            mixed[pl.ds(start * stride + 2 * h + 1, block, stride=stride), :] = soft_ref[
                start - half : start - half + block, lanes(h)
            ].astype(F32)
        linear_rows(start)
        send(start)
    for store in stores:
        store.wait()


def last_call(first, soft_q, partial, planes, cross, early, late, own_kv, soft_late, block):
    tok, width = soft_q.shape
    half = tok // 2
    heads = width // HD
    return pl.pallas_call(
        functools.partial(last_kernel, heads, block),
        in_specs=[SMEM] + [ANY] * 8,
        out_specs=ANY,
        out_shape=jax.ShapeDtypeStruct((tok * 2 * heads, HD), BF16),
        scratch_shapes=[
            pltpu.VMEM((half, width), BF16),
            pltpu.VMEM((tok, width), F32),
            pltpu.VMEM((tok, width), BF16),
            pltpu.VMEM((heads, HD, HD), F32),
            pltpu.VMEM((tok, HD), BF16),
            pltpu.VMEM((tok, HD), BF16),
            pltpu.VMEM((tok, HD), BF16),
            pltpu.VMEM((half, width), BF16),
            pltpu.VMEM((tok * 2 * heads, HD), F32),
            pltpu.VMEM((tok * 2 * heads, HD), BF16),
            pltpu.VMEM((3 * tok, HD), F32),
            pltpu.VMEM((tok + half, 2 * HD), BF16),
            pltpu.VMEM((tok + half, 2 * HD), BF16),
            pltpu.SemaphoreType.DMA((8,)),
            pltpu.SemaphoreType.DMA((tok // block,)),
        ],
        compiler_params=PARAMS,
        cost_estimate=pl.CostEstimate(
            flops=8 * half * tok * width, bytes_accessed=14 * tok * width, transcendentals=half * tok * heads
        ),
    )(first, soft_q, partial, planes, cross, early, late, own_kv, soft_late)


def local(lin_qkv, level_weights, soft_q, soft_kv):
    tok = lin_qkv.shape[0]
    heads = lin_qkv.shape[2] // HD
    q_heads = soft_q.shape[1] // HD
    group = HEADS_SM // KV_HEADS
    local_bits = tok.bit_length() - 1
    block = min(256, tok // 2)
    my_seq = lax.axis_index("seq")

    kv_index = lax.axis_index("head") * q_heads // group
    own_kv = lax.dynamic_slice_in_dim(soft_kv, kv_index * HD, HD, 2).reshape(2 * tok, HD)
    late = passed_along(own_kv[tok:], "seq", 1)
    early = passed_along(own_kv[:tok], "seq", 1)

    planes = jnp.transpose(lin_qkv, (1, 0, 2))
    state = states_call(planes)
    group_sum = state
    cross_state = jnp.zeros((heads, HD, HD), F32)
    for bit_pos in range(lax.axis_size("seq").bit_length() - 1):
        sent = group_sum if bit_pos == 0 else group_sum.astype(BF16)
        partner = partner_2(sent, "seq", bit_pos)
        partner = partner.astype(F32)
        upper = jnp.right_shift(my_seq, bit_pos) % 2 == 1
        factor = jnp.where(upper, level_weights[local_bits + bit_pos + 1], 0.0)
        cross_state = cross_state + factor[:, None, None] * partner
        group_sum = group_sum + partner

    first = (my_seq == 0).astype(jnp.int32).reshape(1)
    table = jnp.transpose(level_weights)
    partial = linear_call(table, planes)
    soft_late = late_call(first, soft_q, late, own_kv, block)
    out = last_call(first, soft_q, partial, planes, cross_state, early, late, own_kv, soft_late, block)
    out = out.reshape(tok, q_heads, 2, HD).transpose(0, 2, 1, 3)
    return out.reshape(tok, 2, q_heads * HD)


def solution(mesh):
    in_specs = (
        P(("groups", "seq"), None, "head"),
        P(None, "head"),
        P(("groups", "seq"), "head"),
        P(("groups", "seq"), None, None),
    )
    out_specs = P(("groups", "seq"), None, "head")
    return jax.shard_map(local, mesh=mesh, in_specs=in_specs, out_specs=out_specs, check_vma=False)
```

time: 40.8 us -> 38.8 us (0.951)
  the two profiles are of different devices: /device:TPU:1 before, /device:TPU:0 now
where the time goes in v2:
time: 38.8 us; the launch traced here: 38.4 us
  Pallas kernels  18.1 us (47%)
  local copies, waits for them, and re-layouts  9.84 us (25%)
  starting transfers between devices  7.88 us (20%)
  other arithmetic  2.25 us (6%)
    pallas_call x1, Pallas kernels, last_call(): pl.pallas_call(functools.partial(last_kernel, heads, block), in_specs=[SM...  7.49 us
    ppermute x2, starting transfers between devices, passed_along(): return lax.ppermute(x, axis, pairs)  7.25 us
    unnamed x14, local copies, waits for them, and re-layouts  5.47 us
    pallas_call x1, Pallas kernels, late_call(): pl.pallas_call(functools.partial(late_kernel, q_heads, block), grid=(1,),...  5.23 us
    pallas_call x1, Pallas kernels, linear_call(): pl.pallas_call(functools.partial(linear_kernel, heads), in_specs=[SMEM, A...  4.67 us
    dynamic_slice x1, local copies, waits for them, and re-layouts, local(): lax.dynamic_slice_in_dim(soft_kv, kv_index * HD, HD, 2).reshape(2 * tok, HD)  2.2 us
    slice x1, local copies, waits for them, and re-layouts, local(): late = passed_along(own_kv[tok:], 'seq', 1)  2.17 us
    add x1, other arithmetic, local(): cross_state = cross_state + factor[:, None, None] * partner  1.06 us
  transfers between devices with their start and end apart: 4, of which 0 were waited for; matrix products, arithmetic and copies ran while one was open for 17% of the time, Pallas kernels for 26%

profile of v2, /device:TPU:0, one launch (start us, length us, event | category | flops | bytes accessed | tf_op | source)
XLA Modules:
  0.0 38.4 jit_solution(16177471810424748051)
XLA Ops:
  0.0 0.0 copy-start
  0.0 1.9 %copy-done = bf16[1024,3,512]{2,0,1:T(8,128)(2,1)S(1)} copy-done((bf16[1024,3,512]{2,0,1:T(8,128)(2,1)S(1)}, bf16[1024,3,512]{2,0,1:T(8,128)(2,1)}, u32[]{:S(2)}) %copy-start) | copy-done | bytes 3145752
  1.9 0.0 copy-start.6
  1.9 0.0 copy-start.1
  1.9 0.7 %shard_map.47 = f32[4,128,128]{2,1,0:T(8,128)S(1)} custom-call(bf16[3,1024,512]{2,1,0:T(8,128)(2,1)S(1)} %bitcast.11, bf16[3,1024,512]{2,1,0:T(8,128)(2,1)S(1)} %bitcast.12), custom_call_target="tpu_custom_call" | custom-call | flops 134217728 | bytes 2097152 | tf_op jit(solution)/shard_map/pallas_call | solution.py:63
  2.6 0.6 %collective-permute-start = (f32[4,128,128]{2,1,0:T(8,128)S(1)}, f32[4,128,128]{2,1,0:T(8,128)}, u32[]{:S(2)}, u32[]{:S(2)}) collective-permute-start(f32[4,128,128]{2,1,0:T(8,128)S(1)} %shard_map.47), channel_id=1, source_target_pairs={{0,4},{4,0},{8,12},{12,8},{1,5},{5,1},{9,13},{13,9},{2,6},{6,2},{1... | collective-permute-start | bytes 786440 | tf_op jit(solution)/shard_map/ppermute | solution.py:29
  3.2 2.2 %constant_dynamic-slice_fusion = (bf16[512,2,128]{2,1,0:T(2,128)(2,1)}, bf16[512,2,128]{2,1,0:T(2,128)(2,1)}) fusion(bf16[1024,2,256]{2,1,0:T(2,128)(2,1)} %param.7, s32[]{:T(128)S(6)} %add.24, s32[]{:T(128)S(6)} %select_n.55), kind=kLoop, calls=%fused_computation.4 | loop fusion | bytes 1048584 | tf_op jit(solution)/shard_map/slice | solution.py:360
  5.4 2.7 %collective-permute-start.2 = (bf16[1024,128]{1,0:T(8,128)(2,1)}, bf16[1024,128]{1,0:T(8,128)(2,1)}, u32[]{:S(2)}, u32[]{:S(2)}) collective-permute-start(bf16[1024,128]{1,0:T(8,128)(2,1)} %bitcast.3), channel_id=1, source_target_pairs={{0,4},{4,8},{8,12},{1,5},{5,9},{9,13},{2,6},{6,10},{10,14},{3,7},{... | collective-permute-start | bytes 786440 | tf_op jit(solution)/shard_map/ppermute | solution.py:35
  8.1 4.5 %collective-permute-start.3 = (bf16[1024,128]{1,0:T(8,128)(2,1)}, bf16[1024,128]{1,0:T(8,128)(2,1)}, u32[]{:S(2)}, u32[]{:S(2)}) collective-permute-start(bf16[1024,128]{1,0:T(8,128)(2,1)} %bitcast.4), channel_id=1, source_target_pairs={{0,4},{4,8},{8,12},{1,5},{5,9},{9,13},{2,6},{6,10},{10,14},{3,7},{... | collective-permute-start | bytes 786440 | tf_op jit(solution)/shard_map/ppermute | solution.py:35
  12.6 0.0 copy-done.6
  12.6 0.2 select_reduce_fusion.1
  12.8 2.2 %constant_dynamic-slice_fusion.2 = bf16[1024,2,128]{2,1,0:T(2,128)(2,1)} fusion(bf16[1024,2,256]{2,1,0:T(2,128)(2,1)} %param.7, s32[]{:T(128)S(6)} %select_n.55), kind=kLoop, calls=%fused_computation.6 | loop fusion | bytes 1048580 | tf_op jit(solution)/shard_map/dynamic_slice | solution.py:359
  15.0 0.0 copy-done.1
  15.0 4.7 %shard_map.46.lin_hbm = f32[1024,512]{1,0:T(8,128)S(1)} custom-call(f32[4,16]{1,0:T(4,128)S(1)} %bitcast.17, bf16[3,1024,512]{2,1,0:T(8,128)(2,1)S(1)} %bitcast.13), custom_call_target="tpu_custom_call" | custom-call | flops 1073741824 | bytes 5242880 | tf_op jit(solution)/shard_map/pallas_call | solution.py:144
  19.7 0.0 copy-start.2
  19.7 1.3 %copy-done.2 = f32[1024,512]{1,0:T(8,128)} copy-done((f32[1024,512]{1,0:T(8,128)}, f32[1024,512]{1,0:T(8,128)S(1)}, u32[]{:S(2)}) %copy-start.2) | copy-done | bytes 2097176
  21.0 0.0 collective-permute-done
  21.0 1.0 %add_convert_fusion = bf16[4,128,128]{2,1,0:T(8,128)(2,1)S(1)} fusion(f32[4,128,128]{2,1,0:T(8,128)S(1)} %shard_map.47, f32[4,128,128]{2,1,0:T(8,128)} %collective-permute-done), kind=kLoop, calls=%fused_computation.1 | loop fusion | flops 131072 | bytes 655360 | tf_op jit(solution)/shard_map/convert_element_type | solution.py:368
  22.0 0.1 collective-permute-start.1
  22.1 0.0 collective-permute-done.3.before_ref.late_hbm
  22.1 0.0 copy-start.4
  22.1 1.0 %copy-done.4 = bf16[1024,2,128]{2,1,0:T(2,128)(2,1)S(1)} copy-done((bf16[1024,2,128]{2,1,0:T(2,128)(2,1)S(1)}, bf16[1024,2,128]{2,1,0:T(2,128)(2,1)}, u32[]{:S(2)}) %copy-start.4) | copy-done | bytes 524312
  23.1 0.0 copy-start.5
  23.1 1.2 %copy-done.5 = bf16[1024,512]{1,0:T(8,128)(2,1)S(1)} copy-done((bf16[1024,512]{1,0:T(8,128)(2,1)S(1)}, bf16[1024,512]{1,0:T(8,128)(2,1)}, u32[]{:S(2)}) %copy-start.5) | copy-done | bytes 1048600
  24.4 0.0 copy-start.3
  24.4 5.2 %shard_map.48.soft_hbm = bf16[512,512]{1,0:T(8,128)(2,1)S(1)} custom-call(s32[1]{0:T(128)} %bitcast.first_ref, bf16[1024,512]{1,0:T(8,128)(2,1)S(1)} %copy-done.5, bf16[1024,128]{1,0:T(8,128)(2,1)} %collective-permute-done.3.before_ref.late_hbm, bf16[2048,128]{1,0:T(8,128)(2,1)S(1)} %bitcast.15), custom_call_target="tpu_custom_call" | custom-call | flops 1610612736 | bytes 3145728 | tf_op jit(solution)/shard_map/pallas_call | solution.py:223
  29.6 0.0 collective-permute-done.1
  29.6 1.1 %multiply_add_fusion.cross_hbm = f32[4,128,128]{2,1,0:T(8,128)S(1)} fusion(bf16[4,128,128]{2,1,0:T(8,128)(2,1)S(1)} %collective-permute-done.1, f32[4,128,128]{2,1,0:T(8,128)} %collective-permute-done, f32[4]{0:T(128)S(1)} %get-tuple-element.6, f32[4]{0:T(128)S(1)} %get-tuple-element.5), kind=kLoop, calls=%fused_computation | loop fusion | flops 262144 | bytes 655392 | tf_op jit(solution)/shard_map/add | solution.py:373
  30.7 0.0 collective-permute-done.2.early_hbm
  30.7 0.0 copy-done.3
  30.7 7.5 %shard_map.49 = bf16[8192,128]{1,0:T(8,128)(2,1)} custom-call(s32[1]{0:T(128)} %bitcast.first_ref, bf16[1024,512]{1,0:T(8,128)(2,1)S(1)} %copy-done.5, f32[1024,512]{1,0:T(8,128)S(1)} %copy-done.3, bf16[3,1024,512]{2,1,0:T(8,128)(2,1)S(1)} %bitcast.14, f32[4,128,128]{2,1,0:T(8,128)S(1)} %multiply_add_fusion.cross_hbm, ...), custom_call_target="tpu_custom_call" | custom-call | flops 2147483648 | bytes 7340032 | tf_op jit(solution)/shard_map/pallas_call | solution.py:320
Async XLA Ops:
  0.0 1.9 %copy-start = (bf16[1024,3,512]{2,0,1:T(8,128)(2,1)S(1)}, bf16[1024,3,512]{2,0,1:T(8,128)(2,1)}, u32[]{:S(2)}) copy-start(bf16[1024,3,512]{2,0,1:T(8,128)(2,1)} %param.4) | copy-start | bytes 9437188
  1.9 10.7 %copy-start.6 = (f32[16,4]{0,1:T(4,128)S(1)}, f32[16,4]{0,1:T(4,128)}, u32[]{:S(2)}) copy-start(f32[16,4]{0,1:T(4,128)} %param.5) | copy-start | bytes 772
  1.9 13.1 %copy-start.1 = (bf16[1024,3,512]{2,0,1:T(8,128)(2,1)S(1)}, bf16[1024,3,512]{2,0,1:T(8,128)(2,1)}, u32[]{:S(2)}) copy-start(bf16[1024,3,512]{2,0,1:T(8,128)(2,1)} %param.4) | copy-start | bytes 9437188
  2.6 18.4 %collective-permute-start = (f32[4,128,128]{2,1,0:T(8,128)S(1)}, f32[4,128,128]{2,1,0:T(8,128)}, u32[]{:S(2)}, u32[]{:S(2)}) collective-permute-start(f32[4,128,128]{2,1,0:T(8,128)S(1)} %shard_map.47), channel_id=1, source_target_pairs={{0,4},{4,0},{8,12},{12,8},{1,5},{5,1},{9,13},{13,9},{2,6},{6,2},{1... | collective-permute-start | bytes 786440 | tf_op jit(solution)/shard_map/ppermute | solution.py:29
  5.4 25.3 %collective-permute-start.2 = (bf16[1024,128]{1,0:T(8,128)(2,1)}, bf16[1024,128]{1,0:T(8,128)(2,1)}, u32[]{:S(2)}, u32[]{:S(2)}) collective-permute-start(bf16[1024,128]{1,0:T(8,128)(2,1)} %bitcast.3), channel_id=1, source_target_pairs={{0,4},{4,8},{8,12},{1,5},{5,9},{9,13},{2,6},{6,10},{10,14},{3,7},{... | collective-permute-start | bytes 786440 | tf_op jit(solution)/shard_map/ppermute | solution.py:35
  8.1 14.0 %collective-permute-start.3 = (bf16[1024,128]{1,0:T(8,128)(2,1)}, bf16[1024,128]{1,0:T(8,128)(2,1)}, u32[]{:S(2)}, u32[]{:S(2)}) collective-permute-start(bf16[1024,128]{1,0:T(8,128)(2,1)} %bitcast.4), channel_id=1, source_target_pairs={{0,4},{4,8},{8,12},{1,5},{5,9},{9,13},{2,6},{6,10},{10,14},{3,7},{... | collective-permute-start | bytes 786440 | tf_op jit(solution)/shard_map/ppermute | solution.py:35
  19.7 1.3 %copy-start.2 = (f32[1024,512]{1,0:T(8,128)}, f32[1024,512]{1,0:T(8,128)S(1)}, u32[]{:S(2)}) copy-start(f32[1024,512]{1,0:T(8,128)S(1)} %shard_map.46.lin_hbm) | copy-start | bytes 6291460
  22.0 7.6 %collective-permute-start.1 = (bf16[4,128,128]{2,1,0:T(8,128)(2,1)S(1)}, bf16[4,128,128]{2,1,0:T(8,128)(2,1)S(1)}, u32[]{:S(2)}, u32[]{:S(2)}) collective-permute-start(bf16[4,128,128]{2,1,0:T(8,128)(2,1)S(1)} %add_convert_fusion), channel_id=1, source_target_pairs={{0,8},{4,12},{8,0},{12,4},{1,9},{5,13},{9,1},{13,5},{2,10},{6,14},... | collective-permute-start | bytes 393224 | tf_op jit(solution)/shard_map/ppermute | solution.py:29
  22.1 1.0 %copy-start.4 = (bf16[1024,2,128]{2,1,0:T(2,128)(2,1)S(1)}, bf16[1024,2,128]{2,1,0:T(2,128)(2,1)}, u32[]{:S(2)}) copy-start(bf16[1024,2,128]{2,1,0:T(2,128)(2,1)} %constant_dynamic-slice_fusion.2) | copy-start | bytes 1572868
  23.1 1.2 %copy-start.5 = (bf16[1024,512]{1,0:T(8,128)(2,1)S(1)}, bf16[1024,512]{1,0:T(8,128)(2,1)}, u32[]{:S(2)}) copy-start(bf16[1024,512]{1,0:T(8,128)(2,1)} %q_hbm.1) | copy-start | bytes 3145732
  24.4 6.3 %copy-start.3 = (f32[1024,512]{1,0:T(8,128)S(1)}, f32[1024,512]{1,0:T(8,128)}, u32[]{:S(2)}) copy-start(f32[1024,512]{1,0:T(8,128)} %copy-done.2) | copy-start | bytes 6291460

commit v3 on v2

v3 whole, which is shorter than its diff:
```python
import functools

import jax
import jax.numpy as jnp
import numpy as np
from jax import lax
from jax.experimental import pallas as pl
from jax.experimental.pallas import tpu as pltpu
from jax.sharding import PartitionSpec as P


HD = 128
HEADS_SM = 16
KV_HEADS = 2
CHUNK = 256
NEG = -1e30
FAR = 1e30
F32 = jnp.float32
BF16 = jnp.bfloat16
SCALE = float(np.log2(np.e) / np.sqrt(HD))
ANY = pl.BlockSpec(memory_space=pl.ANY)
SMEM = pl.BlockSpec(memory_space=pltpu.SMEM)
VMEM = pl.BlockSpec(memory_space=pltpu.VMEM)
HBM = pl.BlockSpec(memory_space=pltpu.HBM)
PARAMS = pltpu.CompilerParams(vmem_limit_bytes=24 * 2**20)


def partner_2(value, axis, distance):
    mask = 2**distance
    pairs = [(source, source ^ mask) for source in range(lax.axis_size(axis))]
    return lax.ppermute(value, axis, pairs)


def passed_along(x, axis, by):
    size = lax.axis_size(axis)
    pairs = [(i, (i + by) % size) for i in range(size)]
    return lax.ppermute(x, axis, pairs)


def nt_dot(a, b):
    return lax.dot_general(a, b, (((1,), (1,)), ((), ())), preferred_element_type=F32)


def tn_dot(a, b):
    return lax.dot_general(a, b, (((0,), (0,)), ((), ())), preferred_element_type=F32)


def lanes(h):
    return slice(h * HD, (h + 1) * HD)


def pick_kernel(index_ref, kv_hbm, out_hbm, sem):
    copy = pltpu.make_async_copy(kv_hbm.at[:, index_ref[0]], out_hbm, sem)
    copy.start()
    copy.wait()


def pick_call(index, kv):
    tok, _, two, hd = kv.shape
    return pl.pallas_call(
        pick_kernel,
        in_specs=[SMEM, HBM],
        out_specs=VMEM,
        out_shape=jax.ShapeDtypeStruct((tok, two, hd), BF16),
        scratch_shapes=[pltpu.SemaphoreType.DMA(())],
        compiler_params=PARAMS,
        cost_estimate=pl.CostEstimate(flops=0, bytes_accessed=8 * tok * hd, transcendentals=0),
    )(index, pltpu.with_memory_space_constraint(kv, pltpu.HBM))


def states_kernel(heads, x_hbm, state_ref, kv_ref, sums, sems):
    half = kv_ref.shape[1] // 2
    pieces = [pl.ds(0, half), pl.ds(half, half)]
    loads = [
        pltpu.make_async_copy(x_hbm.at[pl.ds(1, 2), rows, :], kv_ref.at[:, rows, :], sems.at[i])
        for i, rows in enumerate(pieces)
    ]
    for load in loads:
        load.start()
    loads[0].wait()
    for h in range(heads):
        sums[h] = tn_dot(kv_ref[0, pieces[0], lanes(h)], kv_ref[1, pieces[0], lanes(h)])
    loads[1].wait()
    for h in range(heads):
        total = sums[h] + tn_dot(kv_ref[0, pieces[1], lanes(h)], kv_ref[1, pieces[1], lanes(h)])
        state_ref[h] = total.astype(BF16)


def states_call(planes):
    _, tok, width = planes.shape
    heads = width // HD
    return pl.pallas_call(
        functools.partial(states_kernel, heads),
        in_specs=[HBM],
        out_specs=VMEM,
        out_shape=jax.ShapeDtypeStruct((heads, HD, HD), BF16),
        scratch_shapes=[
            pltpu.VMEM((2, tok, width), BF16),
            pltpu.VMEM((heads, HD, HD), F32),
            pltpu.SemaphoreType.DMA((2,)),
        ],
        compiler_params=PARAMS,
        cost_estimate=pl.CostEstimate(
            flops=2 * tok * width * HD, bytes_accessed=4 * tok * width, transcendentals=0
        ),
    )(pltpu.with_memory_space_constraint(planes, pltpu.HBM))


def linear_kernel(heads, table_ref, x_ref, out_ref, states):
    tok = x_ref.shape[1]
    chunks = tok // CHUNK
    bits = CHUNK.bit_length() - 1
    rows = [pl.ds(c * CHUNK, CHUNK) for c in range(chunks)]
    row = lax.broadcasted_iota(jnp.int32, (CHUNK, CHUNK), 0)
    col = lax.broadcasted_iota(jnp.int32, (CHUNK, CHUNK), 1)
    differ = jnp.bitwise_xor(row, col)
    weights = []
    for h in range(heads):
        weight = jnp.full((CHUNK, CHUNK), table_ref[h, 0], F32)
        for level in range(1, bits + 1):
            weight = jnp.where(differ >= 2 ** (level - 1), table_ref[h, level], weight)
        weights.append(jnp.where(col <= row, weight, 0.0))
    groups = [{} for _ in range(heads)]
    for c in range(chunks):
        for h in range(heads):
            base = h * 2 * chunks
            q, k, v = (x_ref[part, rows[c], lanes(h)] for part in range(3))
            tile = (nt_dot(q, k) * weights[h]).astype(BF16)
            prefix, bit = None, 0
            while (1 << bit) <= c:
                if (c >> bit) & 1:
                    term = table_ref[h, bits + bit + 1] * states[base + groups[h][bit, (c >> bit) - 1]]
                    prefix = term if prefix is None else prefix + term
                bit += 1
            if prefix is None:
                total = jnp.dot(tile, v, preferred_element_type=F32)
            else:
                total = jnp.dot(
                    jnp.concatenate([tile, q], axis=1),
                    jnp.concatenate([v, prefix.astype(BF16)], axis=0),
                    preferred_element_type=F32,
                )
            out_ref[rows[c], lanes(h)] = total
            if c < chunks - 1:
                state, bit, index = tn_dot(k, v), 0, c
                slot = len(groups[h])
                groups[h][0, c] = slot
                states[base + slot] = state
                while index & 1:
                    state = states[base + groups[h][bit, index - 1]] + state
                    bit, index = bit + 1, index >> 1
                    slot = len(groups[h])
                    groups[h][bit, index] = slot
                    states[base + slot] = state


def linear_call(table, planes):
    _, tok, width = planes.shape
    heads = width // HD
    return pl.pallas_call(
        functools.partial(linear_kernel, heads),
        in_specs=[SMEM, VMEM],
        out_specs=VMEM,
        out_shape=jax.ShapeDtypeStruct((tok, width), F32),
        scratch_shapes=[pltpu.VMEM((heads * 2 * (tok // CHUNK), HD, HD), F32)],
        compiler_params=PARAMS,
        cost_estimate=pl.CostEstimate(
            flops=8 * tok * width * CHUNK, bytes_accessed=10 * tok * width, transcendentals=0
        ),
    )(table, planes)


def take_apart(pairs, stage, k_all, v_all, at, count):
    here = pl.ds(at, count)
    rows = pl.ds(2 * at, 2 * count)
    stage[rows, :] = pairs.astype(F32)
    keys = stage[pl.ds(2 * at, count, stride=2), :] * SCALE
    high = keys.astype(BF16)
    k_all[here, 0:HD] = high
    k_all[here, HD : 2 * HD] = (keys - high.astype(F32)).astype(BF16)
    v_all[here, 0:HD] = stage[pl.ds(2 * at + 1, count, stride=2), :].astype(BF16)
    v_all[here, HD : 2 * HD] = jnp.ones((count, HD), BF16)


def edge_masks(block):
    row = lax.broadcasted_iota(jnp.int32, (block, block), 0)
    col = lax.broadcasted_iota(jnp.int32, (block, block), 1)
    low = jnp.where(col >= row, 0.0, NEG).astype(F32)
    high = jnp.where(col <= row, 0.0, NEG).astype(F32)
    return low, high


def softmax_block(q, keys, values, before, masks, first):
    low, high = masks
    block, width = q.shape[0], keys.shape[0]
    scores = nt_dot(jnp.concatenate([q, q], axis=1), keys)
    left = scores[:, :block] + low
    if before > block:
        left = jnp.concatenate([left, scores[:, block:before]], axis=1)
    right = scores[:, width - block :] + high
    if before < width - block:
        right = jnp.concatenate([scores[:, before : width - block], right], axis=1)
    m_left = jnp.max(left, axis=1, keepdims=True)
    m_right = jnp.max(right, axis=1, keepdims=True)
    m = jnp.where(first, m_right, jnp.maximum(m_left, m_right))
    m_left = jnp.where(first, FAR, m)
    probs = jnp.concatenate([jnp.exp2(left - m_left).astype(BF16), jnp.exp2(right - m).astype(BF16)], axis=1)
    out = jnp.dot(probs, values, preferred_element_type=F32)
    return out[:, :HD] / out[:, HD:]


def late_kernel(heads, block, place_ref, q_ref, before_ref, own_ref, out_ref, k_all, v_all, stage):
    half = out_ref.shape[0]
    tok = 2 * half
    first = place_ref[0] == 0
    take_apart(before_ref[...], stage, k_all, v_all, 0, tok)
    take_apart(own_ref[...], stage, k_all, v_all, tok, tok)
    masks = edge_masks(block)
    for start in range(half, tok, block):
        keys = k_all[start : start + tok + block, :]
        values = v_all[start : start + tok + block, :]
        for h in range(heads):
            out = softmax_block(q_ref[start : start + block, lanes(h)], keys, values, tok - start, masks, first)
            out_ref[start - half : start - half + block, lanes(h)] = out.astype(BF16)


def late_call(place, soft_q, before, own_kv, block):
    tok, width = soft_q.shape
    half = tok // 2
    heads = width // HD
    both = jax.ShapeDtypeStruct((2 * tok, 2 * HD), BF16)
    return pl.pallas_call(
        functools.partial(late_kernel, heads, block),
        in_specs=[SMEM, VMEM, VMEM, VMEM],
        out_specs=[VMEM, VMEM, VMEM],
        out_shape=[jax.ShapeDtypeStruct((half, width), BF16), both, both],
        scratch_shapes=[pltpu.VMEM((4 * tok, HD), F32)],
        compiler_params=PARAMS,
        cost_estimate=pl.CostEstimate(
            flops=6 * half * tok * width, bytes_accessed=6 * tok * width, transcendentals=half * tok * heads
        ),
    )(place, soft_q, before, own_kv)


def last_kernel(
    heads, block, others, place_ref, table_ref, q_ref, lin_ref, x_ref, k_all, v_all, soft_ref, *refs
):
    state_refs = refs[: len(others)]
    out_hbm, mixed, packed, cross, out_sems = refs[len(others) :]
    tok = q_ref.shape[0]
    half = tok // 2
    place = place_ref[0]
    first = place == 0
    stride = 2 * heads
    local_bits = tok.bit_length() - 1
    masks = edge_masks(block)
    stores = []
    for h in range(heads):
        total = jnp.zeros((HD, HD), F32)
        for distance, ref in zip(others, state_refs):
            bits = distance.bit_length()
            earlier = jnp.bitwise_and(jnp.right_shift(place, bits - 1), 1) == 1
            factor = jnp.where(earlier, table_ref[h, local_bits + bits], 0.0)
            total = total + factor * ref[h].astype(F32)
        cross[h] = total.astype(BF16)

    def linear_rows(start):
        rows = slice(start, start + block)
        for h in range(heads):
            total = lin_ref[rows, lanes(h)] + jnp.dot(
                x_ref[0, rows, lanes(h)], cross[h], preferred_element_type=F32
            )
            norm = total * lax.rsqrt(jnp.mean(total * total, axis=1, keepdims=True) + 1e-06)
            mixed[pl.ds(start * stride + 2 * h, block, stride=stride), :] = norm

    def send(start):
        rows = pl.ds(start * stride, block * stride)
        packed[rows, :] = mixed[rows, :].astype(BF16)
        store = pltpu.make_async_copy(packed.at[rows, :], out_hbm.at[rows, :], out_sems.at[start // block])
        store.start()
        stores.append(store)

    for start in range(half, tok, block):
        for h in range(heads):
            mixed[pl.ds(start * stride + 2 * h + 1, block, stride=stride), :] = soft_ref[
                start - half : start - half + block, lanes(h)
            ].astype(F32)
        linear_rows(start)
        send(start)
    for start in range(0, half, block):
        keys = k_all[start : start + tok + block, :]
        values = v_all[start : start + tok + block, :]
        linear_rows(start)
        for h in range(heads):
            out = softmax_block(q_ref[start : start + block, lanes(h)], keys, values, tok - start, masks, first)
            mixed[pl.ds(start * stride + 2 * h + 1, block, stride=stride), :] = out
        send(start)
    for store in stores:
        store.wait()


def last_call(place, table, soft_q, partial, planes, k_all, v_all, soft_late, states, block):
    tok, width = soft_q.shape
    heads = width // HD
    others = tuple(distance for distance, _ in states)
    return pl.pallas_call(
        functools.partial(last_kernel, heads, block, others),
        in_specs=[SMEM, SMEM] + [VMEM] * (6 + len(others)),
        out_specs=ANY,
        out_shape=jax.ShapeDtypeStruct((tok * 2 * heads, HD), BF16),
        scratch_shapes=[
            pltpu.VMEM((tok * 2 * heads, HD), F32),
            pltpu.VMEM((tok * 2 * heads, HD), BF16),
            pltpu.VMEM((heads, HD, HD), BF16),
            pltpu.SemaphoreType.DMA((tok // block,)),
        ],
        compiler_params=PARAMS,
        cost_estimate=pl.CostEstimate(
            flops=8 * tok * tok * width // 2, bytes_accessed=14 * tok * width, transcendentals=tok * tok * heads // 2
        ),
    )(place, table, soft_q, partial, planes, k_all, v_all, soft_late, *[state for _, state in states])


def all_states(own):
    have = [(0, own)]
    for bit in reversed(range(lax.axis_size("seq").bit_length() - 1)):
        for distance, state in list(have):
            further = distance + (1 << bit)
            have.append((further, partner_2(state, "seq", bit)))
    return have[1:]


def local(lin_qkv, level_weights, soft_q, soft_kv):
    tok = lin_qkv.shape[0]
    q_heads = soft_q.shape[1] // HD
    group = HEADS_SM // KV_HEADS
    block = min(256, tok // 2)
    my_seq = lax.axis_index("seq")

    kv_index = lax.axis_index("head") * q_heads // group
    kv = soft_kv.reshape(tok, 2, KV_HEADS, HD).transpose(0, 2, 1, 3)
    own_kv = pick_call(kv_index.reshape(1), kv).reshape(2 * tok, HD)
    before = passed_along(own_kv, "seq", 1)

    planes = jnp.transpose(lin_qkv, (1, 0, 2))
    state = states_call(planes)
    states = all_states(state)

    place = my_seq.reshape(1)
    table = jnp.transpose(level_weights)
    partial = linear_call(table, planes)
    soft_late, k_all, v_all = late_call(place, soft_q, before, own_kv, block)
    out = last_call(place, table, soft_q, partial, planes, k_all, v_all, soft_late, states, block)
    out = out.reshape(tok, q_heads, 2, HD).transpose(0, 2, 1, 3)
    return out.reshape(tok, 2, q_heads * HD)


def solution(mesh):
    in_specs = (
        P(("groups", "seq"), None, "head"),
        P(None, "head"),
        P(("groups", "seq"), "head"),
        P(("groups", "seq"), None, None),
    )
    out_specs = P(("groups", "seq"), None, "head")
    return jax.shard_map(local, mesh=mesh, in_specs=in_specs, out_specs=out_specs, check_vma=False)
```

time: 38.8 us -> 27.6 us (0.71)
  local copies, waits for them, and re-layouts: 9.84 us -> 0.01 us
  other arithmetic: 2.25 us -> 0 us
  Pallas kernels: 18.1 us -> 20.1 us
  starting transfers between devices: 7.88 us -> 6.15 us
  waiting for transfers between devices: 0.01 us -> 1.18 us
    ppermute x2 -> x1, starting transfers between devices: 7.25 us -> 0.54 us  [passed_along(): return lax.ppermute(x, axis, pairs)]
    unnamed x14 -> x6, local copies, waits for them, and re-layouts: 5.47 us -> 0.01 us
    ppermute x2 -> x3, starting transfers between devices: 0.63 us -> 5.61 us  [partner_2(): return lax.ppermute(value, axis, pairs)]
    dynamic_slice x1 -> x0, local copies, waits for them, and re-layouts: 2.2 us -> none  [local(): lax.dynamic_slice_in_dim(soft_kv, kv_index * HD, HD, 2).reshape(2 * tok, HD)]
    slice x1 -> x0, local copies, waits for them, and re-layouts: 2.17 us -> none  [local(): late = passed_along(own_kv[tok:], 'seq', 1)]
    pallas_call x4 -> x5, Pallas kernels: 18.1 us -> 20.1 us  [the longest x1 7.2 us: last_call(): pl.pallas_call(functools.partial(last_kernel, heads, block, others), in_s...]
    ppermute x2 -> x3, waiting for transfers between devices: 0.01 us -> 1.18 us  [partner_2(): return lax.ppermute(value, axis, pairs)]
    add x1 -> x0, other arithmetic: 1.06 us -> none  [local(): cross_state = cross_state + factor[:, None, None] * partner]
  transfers between devices with their start and end apart: 4 -> 4, of which waited for: 0 -> 1; matrix products, arithmetic and copies ran while one was open for 17% -> 0% of each run, Pallas kernels for 26% -> 40%
where the time goes in v3:
time: 27.6 us; the launch traced here: 27.5 us
  Pallas kernels  20.1 us (73%)
  starting transfers between devices  6.15 us (22%)
  waiting for transfers between devices  1.18 us (4%)
    pallas_call x1, Pallas kernels, last_call(): pl.pallas_call(functools.partial(last_kernel, heads, block, others), in_s...  7.2 us
    pallas_call x1, Pallas kernels, late_call(): pl.pallas_call(functools.partial(late_kernel, heads, block), in_specs=[SM...  5.96 us
    ppermute x3, starting transfers between devices, partner_2(): return lax.ppermute(value, axis, pairs)  5.61 us
    pallas_call x1, Pallas kernels, linear_call(): pl.pallas_call(functools.partial(linear_kernel, heads), in_specs=[SMEM, V...  2.98 us
    pallas_call x1, Pallas kernels, pick_call(): pl.pallas_call(pick_kernel, in_specs=[SMEM, HBM], out_specs=VMEM, out_sha...  1.99 us
    pallas_call x1, Pallas kernels, states_call(): pl.pallas_call(functools.partial(states_kernel, heads), in_specs=[HBM], o...  1.94 us
    ppermute x3, waiting for transfers between devices, partner_2(): return lax.ppermute(value, axis, pairs)  1.18 us
  transfers between devices with their start and end apart: 4, of which 1 were waited for; matrix products, arithmetic and copies ran while one was open for 0% of the time, Pallas kernels for 40%

profile of v3, /device:TPU:0, one launch (start us, length us, event | category | flops | bytes accessed | tf_op | source)
XLA Modules:
  0.0 27.5 jit_solution(7549557656360409611)
XLA Ops:
  0.0 0.0 copy-start
  0.0 0.0 copy-start.2
  0.0 2.0 %shard_map.47 = bf16[1024,2,128]{2,1,0:T(2,128)(2,1)} custom-call(s32[1]{0:T(128)} %bitcast.3.index_ref, bf16[1024,2,2,128]{3,2,1,0:T(2,128)(2,1)} %bitcast.18), custom_call_target="tpu_custom_call" | custom-call | bytes 1048576 | tf_op jit(solution)/shard_map/pallas_call | solution.py:60
  2.0 0.5 %collective-permute-start = (bf16[2048,128]{1,0:T(8,128)(2,1)}, bf16[2048,128]{1,0:T(8,128)(2,1)}, u32[]{:S(2)}, u32[]{:S(2)}) collective-permute-start(bf16[2048,128]{1,0:T(8,128)(2,1)} %bitcast.6.own_ref), channel_id=1, source_target_pairs={{0,4},{4,8},{8,12},{12,0},{1,5},{5,9},{9,13},{13,1},{2,6},{6,10},{... | collective-permute-start | bytes 1572872 | tf_op jit(solution)/shard_map/ppermute | solution.py:37
  2.5 1.9 %shard_map.49 = bf16[4,128,128]{2,1,0:T(8,128)(2,1)S(1)} custom-call(bf16[3,1024,512]{2,1,0:T(8,128)(2,1)} %bitcast.13), custom_call_target="tpu_custom_call" | custom-call | flops 134217728 | bytes 2097152 | tf_op jit(solution)/shard_map/pallas_call | solution.py:92
  4.5 2.6 %collective-permute-start.1 = (bf16[4,128,128]{2,1,0:T(8,128)(2,1)S(1)}, bf16[4,128,128]{2,1,0:T(8,128)(2,1)S(1)}, u32[]{:S(2)}, u32[]{:S(2)}) collective-permute-start(bf16[4,128,128]{2,1,0:T(8,128)(2,1)S(1)} %shard_map.49), channel_id=1, source_target_pairs={{0,8},{4,12},{8,0},{12,4},{1,9},{5,13},{9,1},{13,5},{2,10},{6,14},... | collective-permute-start | bytes 393224 | tf_op jit(solution)/shard_map/ppermute | solution.py:31
  7.1 0.2 collective-permute-start.2
  7.2 0.0 copy-done
  7.2 0.0 copy-done.2
  7.2 0.0 copy-start.1
  7.2 3.0 %shard_map.46.lin_ref = f32[1024,512]{1,0:T(8,128)S(1)} custom-call(f32[4,16]{1,0:T(4,128)S(1)} %bitcast.16, bf16[3,1024,512]{2,1,0:T(8,128)(2,1)S(1)} %bitcast.14), custom_call_target="tpu_custom_call" | custom-call | flops 1073741824 | bytes 5242880 | tf_op jit(solution)/shard_map/pallas_call | solution.py:160
  10.2 1.2 %collective-permute-done.1.refs_0_ = bf16[4,128,128]{2,1,0:T(8,128)(2,1)S(1)} collective-permute-done((bf16[4,128,128]{2,1,0:T(8,128)(2,1)S(1)}, bf16[4,128,128]{2,1,0:T(8,128)(2,1)S(1)}, u32[]{:S(2)}, u32[]{:S(2)}) %collective-permute-start.1) | collective-permute-done | bytes 131104 | tf_op jit(solution)/shard_map/ppermute | solution.py:31
  11.4 2.9 %collective-permute-start.3 = (bf16[4,128,128]{2,1,0:T(8,128)(2,1)S(1)}, bf16[4,128,128]{2,1,0:T(8,128)(2,1)S(1)}, u32[]{:S(2)}, u32[]{:S(2)}) collective-permute-start(bf16[4,128,128]{2,1,0:T(8,128)(2,1)S(1)} %collective-permute-done.1.refs_0_), channel_id=1, source_target_pairs={{0,4},{4,0},{8,12},{12,8},{1,5},{5,1},{9,13},{13,9},{2,6},{6,2},{1... | collective-permute-start | bytes 393224 | tf_op jit(solution)/shard_map/ppermute | solution.py:31
  14.3 0.0 collective-permute-done.before_ref
  14.3 0.0 copy-done.1
  14.3 6.0 %shard_map.48 = (bf16[512,512]{1,0:T(8,128)(2,1)S(1)}, bf16[2048,256]{1,0:T(8,128)(2,1)S(1)}, bf16[2048,256]{1,0:T(8,128)(2,1)S(1)}) custom-call(s32[1]{0:T(128)} %bitcast.place_ref, bf16[1024,512]{1,0:T(8,128)(2,1)S(1)} %copy-done.1, bf16[2048,128]{1,0:T(8,128)(2,1)} %collective-permute-done.before_ref, bf16[2048,128]{1,0:T(8,128)(2,1)} %bitcast.6.own_ref), custom_call_target="tpu_custom_call" | custom-call | flops 1610612736 | bytes 3145728 | tf_op jit(solution)/shard_map/pallas_call | solution.py:232
  20.3 0.0 collective-permute-done.2.refs_1_
  20.3 0.0 collective-permute-done.3.refs_2_
  20.3 7.2 %shard_map.50 = bf16[8192,128]{1,0:T(8,128)(2,1)} custom-call(s32[1]{0:T(128)} %bitcast.place_ref, f32[4,16]{1,0:T(4,128)S(1)} %bitcast.17, bf16[1024,512]{1,0:T(8,128)(2,1)S(1)} %copy-done.1, f32[1024,512]{1,0:T(8,128)S(1)} %shard_map.46.lin_ref, bf16[3,1024,512]{2,1,0:T(8,128)(2,1)S(1)} %bitcast.15, bf16[2048,256]{1,0:T(8,128)(2,1)S(1)} %get-tuple-element.8.k_all, ...), custom_call_target="tpu_custom_call" | custom-call | flops 2147483648 | bytes 7340032 | tf_op jit(solution)/shard_map/pallas_call | solution.py:306
Async XLA Ops:
  0.0 7.2 %copy-start = (bf16[1024,3,512]{2,0,1:T(8,128)(2,1)S(1)}, bf16[1024,3,512]{2,0,1:T(8,128)(2,1)}, u32[]{:S(2)}) copy-start(bf16[1024,3,512]{2,0,1:T(8,128)(2,1)} %param.4) | copy-start | bytes 9437188
  0.0 7.2 %copy-start.2 = (f32[16,4]{0,1:T(4,128)S(1)}, f32[16,4]{0,1:T(4,128)}, u32[]{:S(2)}) copy-start(f32[16,4]{0,1:T(4,128)} %param.5) | copy-start | bytes 772
  2.0 12.3 %collective-permute-start = (bf16[2048,128]{1,0:T(8,128)(2,1)}, bf16[2048,128]{1,0:T(8,128)(2,1)}, u32[]{:S(2)}, u32[]{:S(2)}) collective-permute-start(bf16[2048,128]{1,0:T(8,128)(2,1)} %bitcast.6.own_ref), channel_id=1, source_target_pairs={{0,4},{4,8},{8,12},{12,0},{1,5},{5,9},{9,13},{13,1},{2,6},{6,10},{... | collective-permute-start | bytes 1572872 | tf_op jit(solution)/shard_map/ppermute | solution.py:37
  4.5 6.9 %collective-permute-start.1 = (bf16[4,128,128]{2,1,0:T(8,128)(2,1)S(1)}, bf16[4,128,128]{2,1,0:T(8,128)(2,1)S(1)}, u32[]{:S(2)}, u32[]{:S(2)}) collective-permute-start(bf16[4,128,128]{2,1,0:T(8,128)(2,1)S(1)} %shard_map.49), channel_id=1, source_target_pairs={{0,8},{4,12},{8,0},{12,4},{1,9},{5,13},{9,1},{13,5},{2,10},{6,14},... | collective-permute-start | bytes 393224 | tf_op jit(solution)/shard_map/ppermute | solution.py:31
  7.1 13.2 %collective-permute-start.2 = (bf16[4,128,128]{2,1,0:T(8,128)(2,1)S(1)}, bf16[4,128,128]{2,1,0:T(8,128)(2,1)S(1)}, u32[]{:S(2)}, u32[]{:S(2)}) collective-permute-start(bf16[4,128,128]{2,1,0:T(8,128)(2,1)S(1)} %shard_map.49), channel_id=1, source_target_pairs={{0,4},{4,0},{8,12},{12,8},{1,5},{5,1},{9,13},{13,9},{2,6},{6,2},{1... | collective-permute-start | bytes 393224 | tf_op jit(solution)/shard_map/ppermute | solution.py:31
  7.2 7.1 %copy-start.1 = (bf16[1024,512]{1,0:T(8,128)(2,1)S(1)}, bf16[1024,512]{1,0:T(8,128)(2,1)}, u32[]{:S(2)}) copy-start(bf16[1024,512]{1,0:T(8,128)(2,1)} %q_ref.3) | copy-start | bytes 3145732
  11.4 8.9 %collective-permute-start.3 = (bf16[4,128,128]{2,1,0:T(8,128)(2,1)S(1)}, bf16[4,128,128]{2,1,0:T(8,128)(2,1)S(1)}, u32[]{:S(2)}, u32[]{:S(2)}) collective-permute-start(bf16[4,128,128]{2,1,0:T(8,128)(2,1)S(1)} %collective-permute-done.1.refs_0_), channel_id=1, source_target_pairs={{0,4},{4,0},{8,12},{12,8},{1,5},{5,1},{9,13},{13,9},{2,6},{6,2},{1... | collective-permute-start | bytes 393224 | tf_op jit(solution)/shard_map/ppermute | solution.py:31

commit v4 on v3

v4 whole, which is shorter than its diff:
```python
import functools

import jax
import jax.numpy as jnp
import numpy as np
from jax import lax
from jax.experimental import pallas as pl
from jax.experimental.pallas import tpu as pltpu
from jax.sharding import PartitionSpec as P


HD = 128
HEADS_SM = 16
KV_HEADS = 2
CHUNK = 256
NEG = -1e30
FAR = 1e30
F32 = jnp.float32
BF16 = jnp.bfloat16
SCALE = float(np.log2(np.e) / np.sqrt(HD))
ANY = pl.BlockSpec(memory_space=pl.ANY)
SMEM = pl.BlockSpec(memory_space=pltpu.SMEM)
VMEM = pl.BlockSpec(memory_space=pltpu.VMEM)
HBM = pl.BlockSpec(memory_space=pltpu.HBM)
PARAMS = pltpu.CompilerParams(vmem_limit_bytes=24 * 2**20)


def partner_2(value, axis, distance):
    mask = 2**distance
    pairs = [(source, source ^ mask) for source in range(lax.axis_size(axis))]
    return lax.ppermute(value, axis, pairs)


def passed_along(x, axis, by):
    size = lax.axis_size(axis)
    pairs = [(i, (i + by) % size) for i in range(size)]
    return lax.ppermute(x, axis, pairs)


def nt_dot(a, b):
    return lax.dot_general(a, b, (((1,), (1,)), ((), ())), preferred_element_type=F32)


def tn_dot(a, b):
    return lax.dot_general(a, b, (((0,), (0,)), ((), ())), preferred_element_type=F32)


def lanes(h):
    return slice(h * HD, (h + 1) * HD)


def take_apart(pairs, stage, k_out, v_out):
    count = k_out.shape[0]
    stage[...] = pairs.astype(F32)
    keys = stage[pl.ds(0, count, stride=2), :] * SCALE
    high = keys.astype(BF16)
    k_out[:, 0:HD] = high
    k_out[:, HD : 2 * HD] = (keys - high.astype(F32)).astype(BF16)
    v_out[:, 0:HD] = stage[pl.ds(1, count, stride=2), :].astype(BF16)
    v_out[:, HD : 2 * HD] = jnp.ones((count, HD), BF16)


def first_kernel(heads, index_ref, kv_hbm, x_hbm, own_ref, state_ref, x_ref, sums, sems):
    half = x_ref.shape[1] // 2
    pieces = [pl.ds(0, half), pl.ds(half, half)]
    pick = pltpu.make_async_copy(kv_hbm.at[:, index_ref[0]], own_ref, sems.at[2])
    pick.start()
    loads = [
        pltpu.make_async_copy(x_hbm.at[pl.ds(1, 2), rows, :], x_ref.at[:, rows, :], sems.at[i])
        for i, rows in enumerate(pieces)
    ]
    for load in loads:
        load.start()
    loads[0].wait()
    for h in range(heads):
        sums[h] = tn_dot(x_ref[0, pieces[0], lanes(h)], x_ref[1, pieces[0], lanes(h)])
    loads[1].wait()
    for h in range(heads):
        total = sums[h] + tn_dot(x_ref[0, pieces[1], lanes(h)], x_ref[1, pieces[1], lanes(h)])
        state_ref[h] = total.astype(BF16)
    pick.wait()


def first_call(index, kv, planes):
    tok, _, two, hd = kv.shape
    width = planes.shape[2]
    heads = width // HD
    return pl.pallas_call(
        functools.partial(first_kernel, heads),
        in_specs=[SMEM, HBM, HBM],
        out_specs=[VMEM, VMEM],
        out_shape=[pltpu.VMEM((tok, two, hd), BF16), pltpu.VMEM((heads, HD, HD), BF16)],
        scratch_shapes=[
            pltpu.VMEM((2, tok, width), BF16),
            pltpu.VMEM((heads, HD, HD), F32),
            pltpu.SemaphoreType.DMA((3,)),
        ],
        compiler_params=PARAMS,
        cost_estimate=pl.CostEstimate(
            flops=2 * tok * width * HD, bytes_accessed=4 * tok * width, transcendentals=0
        ),
    )(index, pltpu.with_memory_space_constraint(kv, pltpu.HBM), pltpu.with_memory_space_constraint(planes, pltpu.HBM))


def linear_kernel(
    heads, table_ref, x_ref, own_ref, mine_ref, near_ref, out_ref, pair_ref, k_own, v_own, states, stage,
    raw, sem,
):
    load = pltpu.make_async_copy(own_ref, raw, sem)
    load.start()
    tok = x_ref.shape[1]
    chunks = tok // CHUNK
    bits = CHUNK.bit_length() - 1
    rows = [pl.ds(c * CHUNK, CHUNK) for c in range(chunks)]
    row = lax.broadcasted_iota(jnp.int32, (CHUNK, CHUNK), 0)
    col = lax.broadcasted_iota(jnp.int32, (CHUNK, CHUNK), 1)
    differ = jnp.bitwise_xor(row, col)
    weights = []
    for h in range(heads):
        weight = jnp.full((CHUNK, CHUNK), table_ref[h, 0], F32)
        for level in range(1, bits + 1):
            weight = jnp.where(differ >= 2 ** (level - 1), table_ref[h, level], weight)
        weights.append(jnp.where(col <= row, weight, 0.0))
    pair_ref[...] = (mine_ref[...].astype(F32) + near_ref[...].astype(F32)).astype(BF16)
    groups = [{} for _ in range(heads)]
    for c in range(chunks):
        for h in range(heads):
            base = h * 2 * chunks
            q, k, v = (x_ref[part, rows[c], lanes(h)] for part in range(3))
            tile = (nt_dot(q, k) * weights[h]).astype(BF16)
            prefix, bit = None, 0
            while (1 << bit) <= c:
                if (c >> bit) & 1:
                    term = table_ref[h, bits + bit + 1] * states[base + groups[h][bit, (c >> bit) - 1]]
                    prefix = term if prefix is None else prefix + term
                bit += 1
            if prefix is None:
                total = jnp.dot(tile, v, preferred_element_type=F32)
            else:
                total = jnp.dot(
                    jnp.concatenate([tile, q], axis=1),
                    jnp.concatenate([v, prefix.astype(BF16)], axis=0),
                    preferred_element_type=F32,
                )
            out_ref[rows[c], lanes(h)] = total
            if c < chunks - 1:
                state, bit, index = tn_dot(k, v), 0, c
                slot = len(groups[h])
                groups[h][0, c] = slot
                states[base + slot] = state
                while index & 1:
                    state = states[base + groups[h][bit, index - 1]] + state
                    bit, index = bit + 1, index >> 1
                    slot = len(groups[h])
                    groups[h][bit, index] = slot
                    states[base + slot] = state
    load.wait()
    take_apart(raw[...], stage, k_own, v_own)


def linear_call(table, planes, own_kv, mine, near):
    _, tok, width = planes.shape
    heads = width // HD
    keys = pltpu.VMEM((tok, 2 * HD), BF16)
    return pl.pallas_call(
        functools.partial(linear_kernel, heads),
        in_specs=[SMEM, VMEM, ANY, VMEM, VMEM],
        out_specs=[VMEM] * 4,
        out_shape=[pltpu.VMEM((tok, width), F32), pltpu.VMEM(mine.shape, BF16), keys, keys],
        scratch_shapes=[
            pltpu.VMEM((heads * 2 * (tok // CHUNK), HD, HD), F32),
            pltpu.VMEM((2 * tok, HD), F32),
            pltpu.VMEM((2 * tok, HD), BF16),
            pltpu.SemaphoreType.DMA(()),
        ],
        compiler_params=PARAMS,
        cost_estimate=pl.CostEstimate(
            flops=8 * tok * width * CHUNK, bytes_accessed=10 * tok * width, transcendentals=0
        ),
    )(table, planes, own_kv, mine, near)


def edge_masks(block):
    row = lax.broadcasted_iota(jnp.int32, (block, block), 0)
    col = lax.broadcasted_iota(jnp.int32, (block, block), 1)
    low = jnp.where(col >= row, 0.0, NEG).astype(F32)
    high = jnp.where(col <= row, 0.0, NEG).astype(F32)
    return low, high


def softmax_block(q, start, before, own, masks, first):
    low, high = masks
    block = q.shape[0]
    end = start + block
    twice = jnp.concatenate([q, q], axis=1)
    left = nt_dot(twice, before[0][start:, :])
    right = nt_dot(twice, own[0][:end, :])
    edge = left[:, :block] + low
    left = jnp.concatenate([edge, left[:, block:]], axis=1) if left.shape[1] > block else edge
    edge = right[:, start:] + high
    right = jnp.concatenate([right[:, :start], edge], axis=1) if start else edge
    m_left = jnp.max(left, axis=1, keepdims=True)
    m_right = jnp.max(right, axis=1, keepdims=True)
    m = jnp.where(first, m_right, jnp.maximum(m_left, m_right))
    m_left = jnp.where(first, FAR, m)
    out = jnp.dot(jnp.exp2(left - m_left).astype(BF16), before[1][start:, :], preferred_element_type=F32)
    out = out + jnp.dot(jnp.exp2(right - m).astype(BF16), own[1][:end, :], preferred_element_type=F32)
    return out[:, :HD] / out[:, HD:]


def late_kernel(
    heads, block, place_ref, q_ref, before_ref, k_own, v_own, out_ref, k_before, v_before, stage, raw, sem
):
    load = pltpu.make_async_copy(before_ref, raw, sem)
    load.start()
    half = out_ref.shape[0]
    tok = 2 * half
    first = place_ref[0] == 0
    masks = edge_masks(block)
    load.wait()
    take_apart(raw[...], stage, k_before, v_before)
    for start in range(half, tok, block):
        for h in range(heads):
            q = q_ref[start : start + block, lanes(h)]
            out = softmax_block(q, start, (k_before, v_before), (k_own, v_own), masks, first)
            out_ref[start - half : start - half + block, lanes(h)] = out.astype(BF16)


def late_call(place, soft_q, before, k_own, v_own, block):
    tok, width = soft_q.shape
    half = tok // 2
    heads = width // HD
    keys = pltpu.VMEM((tok, 2 * HD), BF16)
    return pl.pallas_call(
        functools.partial(late_kernel, heads, block),
        in_specs=[SMEM, VMEM, ANY, VMEM, VMEM],
        out_specs=[VMEM] * 3,
        out_shape=[pltpu.VMEM((half, width), BF16), keys, keys],
        scratch_shapes=[
            pltpu.VMEM((2 * tok, HD), F32),
            pltpu.VMEM((2 * tok, HD), BF16),
            pltpu.SemaphoreType.DMA(()),
        ],
        compiler_params=PARAMS,
        cost_estimate=pl.CostEstimate(
            flops=6 * half * tok * width, bytes_accessed=6 * tok * width, transcendentals=half * tok * heads
        ),
    )(place, soft_q, before, k_own, v_own)


def last_kernel(
    heads, block, rounds, place_ref, table_ref, q_ref, lin_ref, x_ref, k_before, v_before, k_own, v_own, soft_ref, *refs
):
    state_refs = refs[:rounds]
    out_hbm, mixed, packed, cross, out_sems = refs[rounds:]
    tok = q_ref.shape[0]
    half = tok // 2
    place = place_ref[0]
    first = place == 0
    stride = 2 * heads
    local_bits = tok.bit_length() - 1
    masks = edge_masks(block)
    stores = []
    for h in range(heads):
        total = jnp.zeros((HD, HD), F32)
        for bit, ref in enumerate(state_refs):
            earlier = jnp.bitwise_and(jnp.right_shift(place, bit), 1) == 1
            factor = jnp.where(earlier, table_ref[h, local_bits + bit + 1], 0.0)
            total = total + factor * ref[h].astype(F32)
        cross[h] = total.astype(BF16)

    def linear_rows(start):
        rows = slice(start, start + block)
        for h in range(heads):
            total = lin_ref[rows, lanes(h)] + jnp.dot(
                x_ref[0, rows, lanes(h)], cross[h], preferred_element_type=F32
            )
            norm = total * lax.rsqrt(jnp.mean(total * total, axis=1, keepdims=True) + 1e-06)
            mixed[pl.ds(start * stride + 2 * h, block, stride=stride), :] = norm

    def send(start):
        rows = pl.ds(start * stride, block * stride)
        packed[rows, :] = mixed[rows, :].astype(BF16)
        store = pltpu.make_async_copy(packed.at[rows, :], out_hbm.at[rows, :], out_sems.at[start // block])
        store.start()
        stores.append(store)

    for start in range(half, tok, block):
        for h in range(heads):
            mixed[pl.ds(start * stride + 2 * h + 1, block, stride=stride), :] = soft_ref[
                start - half : start - half + block, lanes(h)
            ].astype(F32)
        linear_rows(start)
        send(start)
    for start in range(0, half, block):
        linear_rows(start)
        for h in range(heads):
            q = q_ref[start : start + block, lanes(h)]
            out = softmax_block(q, start, (k_before, v_before), (k_own, v_own), masks, first)
            mixed[pl.ds(start * stride + 2 * h + 1, block, stride=stride), :] = out
        send(start)
    for store in stores:
        store.wait()


def last_call(place, table, soft_q, partial, planes, before, own, soft_late, states, block):
    tok, width = soft_q.shape
    heads = width // HD
    return pl.pallas_call(
        functools.partial(last_kernel, heads, block, len(states)),
        in_specs=[SMEM, SMEM] + [VMEM] * (8 + len(states)),
        out_specs=ANY,
        out_shape=jax.ShapeDtypeStruct((tok * 2 * heads, HD), BF16),
        scratch_shapes=[
            pltpu.VMEM((tok * 2 * heads, HD), F32),
            pltpu.VMEM((tok * 2 * heads, HD), BF16),
            pltpu.VMEM((heads, HD, HD), BF16),
            pltpu.SemaphoreType.DMA((tok // block,)),
        ],
        compiler_params=PARAMS,
        cost_estimate=pl.CostEstimate(
            flops=8 * tok * tok * width // 2, bytes_accessed=14 * tok * width, transcendentals=tok * tok * heads // 2
        ),
    )(place, table, soft_q, partial, planes, *before, *own, soft_late, *states)


def local(lin_qkv, level_weights, soft_q, soft_kv):
    tok = lin_qkv.shape[0]
    q_heads = soft_q.shape[1] // HD
    group = HEADS_SM // KV_HEADS
    block = min(256, tok // 2)
    my_seq = lax.axis_index("seq")

    kv_index = lax.axis_index("head") * q_heads // group
    kv = soft_kv.reshape(tok, 2, KV_HEADS, HD).transpose(0, 2, 1, 3)
    planes = jnp.transpose(lin_qkv, (1, 0, 2))
    place = my_seq.reshape(1)
    table = jnp.transpose(level_weights)
    own_kv, state = first_call(kv_index.reshape(1), kv, planes)
    own_kv = own_kv.reshape(2 * tok, HD)
    before = passed_along(own_kv, "seq", 1)
    near = partner_2(state, "seq", 0)
    partial, group_sum, *own = linear_call(table, planes, own_kv, state, near)
    states = [near]
    for bit in range(1, lax.axis_size("seq").bit_length() - 1):
        if bit > 1:
            group_sum = (group_sum.astype(F32) + states[-1].astype(F32)).astype(BF16)
        states.append(partner_2(group_sum, "seq", bit))
    soft_late, *earlier = late_call(place, soft_q, before, *own, block)
    out = last_call(place, table, soft_q, partial, planes, earlier, own, soft_late, states, block)
    out = out.reshape(tok, q_heads, 2, HD).transpose(0, 2, 1, 3)
    return out.reshape(tok, 2, q_heads * HD)


def solution(mesh):
    in_specs = (
        P(("groups", "seq"), None, "head"),
        P(None, "head"),
        P(("groups", "seq"), "head"),
        P(("groups", "seq"), None, None),
    )
    out_specs = P(("groups", "seq"), None, "head")
    return jax.shard_map(local, mesh=mesh, in_specs=in_specs, out_specs=out_specs, check_vma=False)
```

time: 27.6 us -> 25.3 us (0.917)
  starting transfers between devices: 6.15 us -> 4.03 us
  Pallas kernels: 20.1 us -> 18.8 us
  waiting for transfers between devices: 1.18 us -> 2.19 us
    ppermute x3 -> x2, starting transfers between devices: 5.61 us -> 3.49 us  [partner_2(): return lax.ppermute(value, axis, pairs)]
    ppermute x1, waiting for transfers between devices: 0.01 us -> 1.21 us  [passed_along(): return lax.ppermute(x, axis, pairs)]
    pallas_call x3 -> x2, Pallas kernels: 11.1 us -> 10.1 us  [the longest x1 7.01 us: last_call(): pl.pallas_call(functools.partial(last_kernel, heads, block, len(states)),...]
    pallas_call x1, Pallas kernels: 5.96 us -> 5.34 us  [late_call(): pl.pallas_call(functools.partial(late_kernel, heads, block), in_specs=[SM...]
    pallas_call x1, Pallas kernels: 2.98 us -> 3.4 us  [linear_call(): pl.pallas_call(functools.partial(linear_kernel, heads), in_specs=[SMEM, V...]
    ppermute x3 -> x2, waiting for transfers between devices: 1.18 us -> 0.99 us  [partner_2(): return lax.ppermute(value, axis, pairs)]
  transfers between devices with their start and end apart: 4 -> 3, of which waited for: 1 -> 2; matrix products, arithmetic and copies ran while one was open for 0% -> 0% of each run, Pallas kernels for 40% -> 35%
where the time goes in v4:
time: 25.3 us; the launch traced here: 25.1 us
  Pallas kernels  18.8 us (74%)
  starting transfers between devices  4.03 us (16%)
  waiting for transfers between devices  2.19 us (9%)
    pallas_call x1, Pallas kernels, last_call(): pl.pallas_call(functools.partial(last_kernel, heads, block, len(states)),...  7.01 us
    pallas_call x1, Pallas kernels, late_call(): pl.pallas_call(functools.partial(late_kernel, heads, block), in_specs=[SM...  5.34 us
    ppermute x2, starting transfers between devices, partner_2(): return lax.ppermute(value, axis, pairs)  3.49 us
    pallas_call x1, Pallas kernels, linear_call(): pl.pallas_call(functools.partial(linear_kernel, heads), in_specs=[SMEM, V...  3.4 us
    pallas_call x1, Pallas kernels, first_call(): pl.pallas_call(functools.partial(first_kernel, heads), in_specs=[SMEM, HB...  3.06 us
    ppermute x1, waiting for transfers between devices, passed_along(): return lax.ppermute(x, axis, pairs)  1.21 us
    ppermute x2, waiting for transfers between devices, partner_2(): return lax.ppermute(value, axis, pairs)  0.99 us
    ppermute x1, starting transfers between devices, passed_along(): return lax.ppermute(x, axis, pairs)  0.54 us
  transfers between devices with their start and end apart: 3, of which 2 were waited for; matrix products, arithmetic and copies ran while one was open for 0% of the time, Pallas kernels for 35%

profile of v4, /device:TPU:0, one launch (start us, length us, event | category | flops | bytes accessed | tf_op | source)
XLA Modules:
  0.0 25.1 jit_solution(12867185878533938219)
XLA Ops:
  0.0 0.0 copy-start
  0.0 0.0 copy-start.2
  0.0 3.1 %shard_map.46 = (bf16[1024,2,128]{2,1,0:T(2,128)(2,1)}, bf16[4,128,128]{2,1,0:T(8,128)(2,1)S(1)}) custom-call(s32[1]{0:T(128)} %bitcast.3.index_ref, bf16[1024,2,2,128]{3,2,1,0:T(2,128)(2,1)} %bitcast.18, bf16[3,1024,512]{2,1,0:T(8,128)(2,1)} %bitcast.13), custom_call_target="tpu_custom_call" | custom-call | flops 134217728 | bytes 2097152 | tf_op jit(solution)/shard_map/pallas_call | solution.py:88
  3.1 0.5 %collective-permute-start.1 = (bf16[2048,128]{1,0:T(8,128)(2,1)}, bf16[2048,128]{1,0:T(8,128)(2,1)}, u32[]{:S(2)}, u32[]{:S(2)}) collective-permute-start(bf16[2048,128]{1,0:T(8,128)(2,1)} %bitcast.6.own_ref), channel_id=1, source_target_pairs={{0,4},{4,8},{8,12},{12,0},{1,5},{5,9},{9,13},{13,1},{2,6},{6,10},{... | collective-permute-start | bytes 1572872 | tf_op jit(solution)/shard_map/ppermute | solution.py:37
  3.6 2.6 %collective-permute-start = (bf16[4,128,128]{2,1,0:T(8,128)(2,1)S(1)}, bf16[4,128,128]{2,1,0:T(8,128)(2,1)S(1)}, u32[]{:S(2)}, u32[]{:S(2)}) collective-permute-start(bf16[4,128,128]{2,1,0:T(8,128)(2,1)S(1)} %get-tuple-element.15.mine_ref), channel_id=1, source_target_pairs={{0,4},{4,0},{8,12},{12,8},{1,5},{5,1},{9,13},{13,9},{2,6},{6,2},{1... | collective-permute-start | bytes 393224 | tf_op jit(solution)/shard_map/ppermute | solution.py:31
  6.2 0.0 copy-start.1
  6.2 1.0 %collective-permute-done.near_ref.refs_0_ = bf16[4,128,128]{2,1,0:T(8,128)(2,1)S(1)} collective-permute-done((bf16[4,128,128]{2,1,0:T(8,128)(2,1)S(1)}, bf16[4,128,128]{2,1,0:T(8,128)(2,1)S(1)}, u32[]{:S(2)}, u32[]{:S(2)}) %collective-permute-start) | collective-permute-done | bytes 131104 | tf_op jit(solution)/shard_map/ppermute | solution.py:31
  7.2 0.0 copy-done
  7.2 0.0 copy-done.2
  7.2 3.4 %shard_map.47 = (f32[1024,512]{1,0:T(8,128)S(1)}, bf16[4,128,128]{2,1,0:T(8,128)(2,1)S(1)}, bf16[1024,256]{1,0:T(8,128)(2,1)S(1)}, bf16[1024,256]{1,0:T(8,128)(2,1)S(1)}) custom-call(f32[4,16]{1,0:T(4,128)S(1)} %bitcast.16, bf16[3,1024,512]{2,1,0:T(8,128)(2,1)S(1)} %bitcast.14, bf16[2048,128]{1,0:T(8,128)(2,1)} %bitcast.6.own_ref, ...), custom_call_target="tpu_custom_call" | custom-call | flops 1073741824 | bytes 5242880 | tf_op jit(solution)/shard_map/pallas_call | solution.py:165
  10.6 0.9 %collective-permute-start.2 = (bf16[4,128,128]{2,1,0:T(8,128)(2,1)S(1)}, bf16[4,128,128]{2,1,0:T(8,128)(2,1)S(1)}, u32[]{:S(2)}, u32[]{:S(2)}) collective-permute-start(bf16[4,128,128]{2,1,0:T(8,128)(2,1)S(1)} %get-tuple-element.22), channel_id=1, source_target_pairs={{0,8},{4,12},{8,0},{12,4},{1,9},{5,13},{9,1},{13,5},{2,10},{6,14},... | collective-permute-start | bytes 393224 | tf_op jit(solution)/shard_map/ppermute | solution.py:31
  11.5 1.2 %collective-permute-done.1.before_ref = bf16[2048,128]{1,0:T(8,128)(2,1)} collective-permute-done((bf16[2048,128]{1,0:T(8,128)(2,1)}, bf16[2048,128]{1,0:T(8,128)(2,1)}, u32[]{:S(2)}, u32[]{:S(2)}) %collective-permute-start.1) | collective-permute-done | bytes 524320 | tf_op jit(solution)/shard_map/ppermute | solution.py:37
  12.7 0.0 copy-done.1
  12.7 5.3 %shard_map.48 = (bf16[512,512]{1,0:T(8,128)(2,1)S(1)}, bf16[1024,256]{1,0:T(8,128)(2,1)S(1)}, bf16[1024,256]{1,0:T(8,128)(2,1)S(1)}) custom-call(s32[1]{0:T(128)} %bitcast.place_ref, bf16[1024,512]{1,0:T(8,128)(2,1)S(1)} %copy-done.1, bf16[2048,128]{1,0:T(8,128)(2,1)} %collective-permute-done.1.before_ref, bf16[1024,256]{1,0:T(8,128)(2,1)S(1)} %get-tuple-element.17.k_own, ...), custom_call_target="tpu_custom_call" | custom-call | flops 1610612736 | bytes 3145728 | tf_op jit(solution)/shard_map/pallas_call | solution.py:234
  18.1 0.0 collective-permute-done.2.refs_1_
  18.1 7.0 %shard_map.49 = bf16[8192,128]{1,0:T(8,128)(2,1)} custom-call(s32[1]{0:T(128)} %bitcast.place_ref, f32[4,16]{1,0:T(4,128)S(1)} %bitcast.17, bf16[1024,512]{1,0:T(8,128)(2,1)S(1)} %copy-done.1, f32[1024,512]{1,0:T(8,128)S(1)} %get-tuple-element.16.lin_ref, bf16[3,1024,512]{2,1,0:T(8,128)(2,1)S(1)} %bitcast.15, ...), custom_call_target="tpu_custom_call" | custom-call | flops 2147483648 | bytes 7340032 | tf_op jit(solution)/shard_map/pallas_call | solution.py:309
Async XLA Ops:
  0.0 7.2 %copy-start = (bf16[1024,3,512]{2,0,1:T(8,128)(2,1)S(1)}, bf16[1024,3,512]{2,0,1:T(8,128)(2,1)}, u32[]{:S(2)}) copy-start(bf16[1024,3,512]{2,0,1:T(8,128)(2,1)} %param.4) | copy-start | bytes 9437188
  0.0 7.2 %copy-start.2 = (f32[16,4]{0,1:T(4,128)S(1)}, f32[16,4]{0,1:T(4,128)}, u32[]{:S(2)}) copy-start(f32[16,4]{0,1:T(4,128)} %param.5) | copy-start | bytes 772
  3.1 9.6 %collective-permute-start.1 = (bf16[2048,128]{1,0:T(8,128)(2,1)}, bf16[2048,128]{1,0:T(8,128)(2,1)}, u32[]{:S(2)}, u32[]{:S(2)}) collective-permute-start(bf16[2048,128]{1,0:T(8,128)(2,1)} %bitcast.6.own_ref), channel_id=1, source_target_pairs={{0,4},{4,8},{8,12},{12,0},{1,5},{5,9},{9,13},{13,1},{2,6},{6,10},{... | collective-permute-start | bytes 1572872 | tf_op jit(solution)/shard_map/ppermute | solution.py:37
  3.6 3.6 %collective-permute-start = (bf16[4,128,128]{2,1,0:T(8,128)(2,1)S(1)}, bf16[4,128,128]{2,1,0:T(8,128)(2,1)S(1)}, u32[]{:S(2)}, u32[]{:S(2)}) collective-permute-start(bf16[4,128,128]{2,1,0:T(8,128)(2,1)S(1)} %get-tuple-element.15.mine_ref), channel_id=1, source_target_pairs={{0,4},{4,0},{8,12},{12,8},{1,5},{5,1},{9,13},{13,9},{2,6},{6,2},{1... | collective-permute-start | bytes 393224 | tf_op jit(solution)/shard_map/ppermute | solution.py:31
  6.2 6.5 %copy-start.1 = (bf16[1024,512]{1,0:T(8,128)(2,1)S(1)}, bf16[1024,512]{1,0:T(8,128)(2,1)}, u32[]{:S(2)}) copy-start(bf16[1024,512]{1,0:T(8,128)(2,1)} %q_ref.3) | copy-start | bytes 3145732
  10.6 7.5 %collective-permute-start.2 = (bf16[4,128,128]{2,1,0:T(8,128)(2,1)S(1)}, bf16[4,128,128]{2,1,0:T(8,128)(2,1)S(1)}, u32[]{:S(2)}, u32[]{:S(2)}) collective-permute-start(bf16[4,128,128]{2,1,0:T(8,128)(2,1)S(1)} %get-tuple-element.22), channel_id=1, source_target_pairs={{0,8},{4,12},{8,0},{12,4},{1,9},{5,13},{9,1},{13,5},{2,10},{6,14},... | collective-permute-start | bytes 393224 | tf_op jit(solution)/shard_map/ppermute | solution.py:31

commit v5 on v4

--- a/solution.py
+++ b/solution.py
@@ -66,19 +66,21 @@
     pick = pltpu.make_async_copy(kv_hbm.at[:, index_ref[0]], own_ref, sems.at[2])
     pick.start()
     loads = [
-        pltpu.make_async_copy(x_hbm.at[pl.ds(1, 2), rows, :], x_ref.at[:, rows, :], sems.at[i])
+        pltpu.make_async_copy(x_hbm.at[pl.ds(1, 2), rows, :], x_ref.at[pl.ds(1, 2), rows, :], sems.at[i])
         for i, rows in enumerate(pieces)
     ]
+    loads.append(pltpu.make_async_copy(x_hbm.at[0], x_ref.at[0], sems.at[3]))
     for load in loads:
         load.start()
     loads[0].wait()
     for h in range(heads):
-        sums[h] = tn_dot(x_ref[0, pieces[0], lanes(h)], x_ref[1, pieces[0], lanes(h)])
+        sums[h] = tn_dot(x_ref[1, pieces[0], lanes(h)], x_ref[2, pieces[0], lanes(h)])
     loads[1].wait()
     for h in range(heads):
-        total = sums[h] + tn_dot(x_ref[0, pieces[1], lanes(h)], x_ref[1, pieces[1], lanes(h)])
+        total = sums[h] + tn_dot(x_ref[1, pieces[1], lanes(h)], x_ref[2, pieces[1], lanes(h)])
         state_ref[h] = total.astype(BF16)
     pick.wait()
+    loads[2].wait()
 
 
 def first_call(index, kv, planes):
@@ -88,12 +90,15 @@
     return pl.pallas_call(
         functools.partial(first_kernel, heads),
         in_specs=[SMEM, HBM, HBM],
-        out_specs=[VMEM, VMEM],
-        out_shape=[pltpu.VMEM((tok, two, hd), BF16), pltpu.VMEM((heads, HD, HD), BF16)],
+        out_specs=[VMEM] * 3,
+        out_shape=[
+            pltpu.VMEM((tok, two, hd), BF16),
+            pltpu.VMEM((heads, HD, HD), BF16),
+            pltpu.VMEM(planes.shape, BF16),
+        ],
         scratch_shapes=[
-            pltpu.VMEM((2, tok, width), BF16),
             pltpu.VMEM((heads, HD, HD), F32),
-            pltpu.SemaphoreType.DMA((3,)),
+            pltpu.SemaphoreType.DMA((4,)),
         ],
         compiler_params=PARAMS,
         cost_estimate=pl.CostEstimate(
@@ -253,6 +258,9 @@
 ):
     state_refs = refs[:rounds]
     out_hbm, mixed, packed, cross, out_sems = refs[rounds:]
+    pairs = heads // 2 if heads % 2 == 0 else heads
+    together = heads // pairs
+    cross[...] = jnp.zeros_like(cross)
     tok = q_ref.shape[0]
     half = tok // 2
     place = place_ref[0]
@@ -267,37 +275,36 @@
             earlier = jnp.bitwise_and(jnp.right_shift(place, bit), 1) == 1
             factor = jnp.where(earlier, table_ref[h, local_bits + bit + 1], 0.0)
             total = total + factor * ref[h].astype(F32)
-        cross[h] = total.astype(BF16)
+        at = slice(h % together * HD, (h % together + 1) * HD)
+        cross[h // together, at, at] = total.astype(BF16)
 
     def linear_rows(start):
         rows = slice(start, start + block)
-        for h in range(heads):
-            total = lin_ref[rows, lanes(h)] + jnp.dot(
-                x_ref[0, rows, lanes(h)], cross[h], preferred_element_type=F32
-            )
-            norm = total * lax.rsqrt(jnp.mean(total * total, axis=1, keepdims=True) + 1e-06)
-            mixed[pl.ds(start * stride + 2 * h, block, stride=stride), :] = norm
+        for pair in range(pairs):
+            wide = slice(pair * together * HD, (pair + 1) * together * HD)
+            both = jnp.dot(x_ref[0, rows, wide], cross[pair], preferred_element_type=F32) + lin_ref[rows, wide]
+            for i in range(together):
+                total = both[:, lanes(i)]
+                norm = total * lax.rsqrt(jnp.mean(total * total, axis=1, keepdims=True) + 1e-06)
+                mixed[2 * (pair * together + i)] = norm
 
     def send(start):
         rows = pl.ds(start * stride, block * stride)
-        packed[rows, :] = mixed[rows, :].astype(BF16)
+        packed[rows, :] = jnp.swapaxes(mixed[...], 0, 1).reshape(block * stride, HD).astype(BF16)
         store = pltpu.make_async_copy(packed.at[rows, :], out_hbm.at[rows, :], out_sems.at[start // block])
         store.start()
         stores.append(store)
 
     for start in range(half, tok, block):
         for h in range(heads):
-            mixed[pl.ds(start * stride + 2 * h + 1, block, stride=stride), :] = soft_ref[
-                start - half : start - half + block, lanes(h)
-            ].astype(F32)
+            mixed[2 * h + 1] = soft_ref[start - half : start - half + block, lanes(h)].astype(F32)
         linear_rows(start)
         send(start)
     for start in range(0, half, block):
         linear_rows(start)
         for h in range(heads):
             q = q_ref[start : start + block, lanes(h)]
-            out = softmax_block(q, start, (k_before, v_before), (k_own, v_own), masks, first)
-            mixed[pl.ds(start * stride + 2 * h + 1, block, stride=stride), :] = out
+            mixed[2 * h + 1] = softmax_block(q, start, (k_before, v_before), (k_own, v_own), masks, first)
         send(start)
     for store in stores:
         store.wait()
@@ -312,9 +319,9 @@
         out_specs=ANY,
         out_shape=jax.ShapeDtypeStruct((tok * 2 * heads, HD), BF16),
         scratch_shapes=[
-            pltpu.VMEM((tok * 2 * heads, HD), F32),
+            pltpu.VMEM((2 * heads, block, HD), F32),
             pltpu.VMEM((tok * 2 * heads, HD), BF16),
-            pltpu.VMEM((heads, HD, HD), BF16),
+            pltpu.VMEM((heads // 2, 2 * HD, 2 * HD) if heads % 2 == 0 else (heads, HD, HD), BF16),
             pltpu.SemaphoreType.DMA((tok // block,)),
         ],
         compiler_params=PARAMS,
@@ -336,7 +343,7 @@
     planes = jnp.transpose(lin_qkv, (1, 0, 2))
     place = my_seq.reshape(1)
     table = jnp.transpose(level_weights)
-    own_kv, state = first_call(kv_index.reshape(1), kv, planes)
+    own_kv, state, planes = first_call(kv_index.reshape(1), kv, planes)
     own_kv = own_kv.reshape(2 * tok, HD)
     before = passed_along(own_kv, "seq", 1)
     near = partner_2(state, "seq", 0)

time: 25.3 us -> 25.4 us (level)
  transfers between devices with their start and end apart: 3 -> 3, of which waited for: 2 -> 2; matrix products, arithmetic and copies ran while one was open for 0% -> 0% of each run, Pallas kernels for 35% -> 36%
where the time goes in v5:
time: 25.4 us; the launch traced here: 25.2 us
  Pallas kernels  18.9 us (74%)
  starting transfers between devices  4.04 us (16%)
  waiting for transfers between devices  2.2 us (9%)
    pallas_call x1, Pallas kernels, last_call(): pl.pallas_call(functools.partial(last_kernel, heads, block, len(states)),...  7.01 us
    pallas_call x1, Pallas kernels, late_call(): pl.pallas_call(functools.partial(late_kernel, heads, block), in_specs=[SM...  5.56 us
    ppermute x2, starting transfers between devices, partner_2(): return lax.ppermute(value, axis, pairs)  3.49 us
    pallas_call x1, Pallas kernels, linear_call(): pl.pallas_call(functools.partial(linear_kernel, heads), in_specs=[SMEM, V...  3.39 us
    pallas_call x1, Pallas kernels, first_call(): pl.pallas_call(functools.partial(first_kernel, heads), in_specs=[SMEM, HB...  2.93 us
    ppermute x1, waiting for transfers between devices, passed_along(): return lax.ppermute(x, axis, pairs)  1.21 us
    ppermute x2, waiting for transfers between devices, partner_2(): return lax.ppermute(value, axis, pairs)  0.99 us
    ppermute x1, starting transfers between devices, passed_along(): return lax.ppermute(x, axis, pairs)  0.54 us
  transfers between devices with their start and end apart: 3, of which 2 were waited for; matrix products, arithmetic and copies ran while one was open for 0% of the time, Pallas kernels for 36%

profile of v5, /device:TPU:0, one launch (start us, length us, event | category | flops | bytes accessed | tf_op | source)
XLA Modules:
  0.0 25.2 jit_solution(1267615854195460153)
XLA Ops:
  0.0 0.0 copy-start.1
  0.0 2.9 %shard_map.46 = (bf16[1024,2,128]{2,1,0:T(2,128)(2,1)}, bf16[4,128,128]{2,1,0:T(8,128)(2,1)S(1)}, bf16[3,1024,512]{2,1,0:T(8,128)(2,1)S(1)}) custom-call(s32[1]{0:T(128)} %bitcast.2.index_ref, bf16[1024,2,2,128]{3,2,1,0:T(2,128)(2,1)} %bitcast.16, bf16[3,1024,512]{2,1,0:T(8,128)(2,1)} %bitcast.15), custom_call_target="tpu_custom_call" | custom-call | flops 134217728 | bytes 2097152 | tf_op jit(solution)/shard_map/pallas_call | solution.py:90
  2.9 0.5 %collective-permute-start.1 = (bf16[2048,128]{1,0:T(8,128)(2,1)}, bf16[2048,128]{1,0:T(8,128)(2,1)}, u32[]{:S(2)}, u32[]{:S(2)}) collective-permute-start(bf16[2048,128]{1,0:T(8,128)(2,1)} %bitcast.6.own_ref), channel_id=1, source_target_pairs={{0,4},{4,8},{8,12},{12,0},{1,5},{5,9},{9,13},{13,1},{2,6},{6,10},{... | collective-permute-start | bytes 1572872 | tf_op jit(solution)/shard_map/ppermute | solution.py:37
  3.5 2.6 %collective-permute-start = (bf16[4,128,128]{2,1,0:T(8,128)(2,1)S(1)}, bf16[4,128,128]{2,1,0:T(8,128)(2,1)S(1)}, u32[]{:S(2)}, u32[]{:S(2)}) collective-permute-start(bf16[4,128,128]{2,1,0:T(8,128)(2,1)S(1)} %get-tuple-element.17.mine_ref), channel_id=1, source_target_pairs={{0,4},{4,0},{8,12},{12,8},{1,5},{5,1},{9,13},{13,9},{2,6},{6,2},{1... | collective-permute-start | bytes 393224 | tf_op jit(solution)/shard_map/ppermute | solution.py:31
  6.1 0.0 copy-start
  6.1 1.0 %collective-permute-done.near_ref.refs_0_ = bf16[4,128,128]{2,1,0:T(8,128)(2,1)S(1)} collective-permute-done((bf16[4,128,128]{2,1,0:T(8,128)(2,1)S(1)}, bf16[4,128,128]{2,1,0:T(8,128)(2,1)S(1)}, u32[]{:S(2)}, u32[]{:S(2)}) %collective-permute-start) | collective-permute-done | bytes 131104 | tf_op jit(solution)/shard_map/ppermute | solution.py:31
  7.1 0.0 copy-done.1
  7.1 3.4 %shard_map.47 = (f32[1024,512]{1,0:T(8,128)S(1)}, bf16[4,128,128]{2,1,0:T(8,128)(2,1)S(1)}, bf16[1024,256]{1,0:T(8,128)(2,1)S(1)}, bf16[1024,256]{1,0:T(8,128)(2,1)S(1)}) custom-call(f32[4,16]{1,0:T(4,128)S(1)} %bitcast.13, bf16[3,1024,512]{2,1,0:T(8,128)(2,1)S(1)} %get-tuple-element.15.x_ref, bf16[2048,128]{1,0:T(8,128)(2,1)} %bitcast.6.own_ref, ...), custom_call_target="tpu_custom_call" | custom-call | flops 1073741824 | bytes 5242880 | tf_op jit(solution)/shard_map/pallas_call | solution.py:170
  10.5 0.9 %collective-permute-start.2 = (bf16[4,128,128]{2,1,0:T(8,128)(2,1)S(1)}, bf16[4,128,128]{2,1,0:T(8,128)(2,1)S(1)}, u32[]{:S(2)}, u32[]{:S(2)}) collective-permute-start(bf16[4,128,128]{2,1,0:T(8,128)(2,1)S(1)} %get-tuple-element.24), channel_id=1, source_target_pairs={{0,8},{4,12},{8,0},{12,4},{1,9},{5,13},{9,1},{13,5},{2,10},{6,14},... | collective-permute-start | bytes 393224 | tf_op jit(solution)/shard_map/ppermute | solution.py:31
  11.4 1.2 %collective-permute-done.1.before_ref = bf16[2048,128]{1,0:T(8,128)(2,1)} collective-permute-done((bf16[2048,128]{1,0:T(8,128)(2,1)}, bf16[2048,128]{1,0:T(8,128)(2,1)}, u32[]{:S(2)}, u32[]{:S(2)}) %collective-permute-start.1) | collective-permute-done | bytes 524320 | tf_op jit(solution)/shard_map/ppermute | solution.py:37
  12.6 0.0 copy-done
  12.6 5.6 %shard_map.48 = (bf16[512,512]{1,0:T(8,128)(2,1)S(1)}, bf16[1024,256]{1,0:T(8,128)(2,1)S(1)}, bf16[1024,256]{1,0:T(8,128)(2,1)S(1)}) custom-call(s32[1]{0:T(128)} %bitcast.place_ref, bf16[1024,512]{1,0:T(8,128)(2,1)S(1)} %copy-done, bf16[2048,128]{1,0:T(8,128)(2,1)} %collective-permute-done.1.before_ref, bf16[1024,256]{1,0:T(8,128)(2,1)S(1)} %get-tuple-element.19.k_own, ...), custom_call_target="tpu_custom_call" | custom-call | flops 1610612736 | bytes 3145728 | tf_op jit(solution)/shard_map/pallas_call | solution.py:239
  18.2 0.0 collective-permute-done.2.refs_1_
  18.2 7.0 %shard_map.49 = bf16[8192,128]{1,0:T(8,128)(2,1)} custom-call(s32[1]{0:T(128)} %bitcast.place_ref, f32[4,16]{1,0:T(4,128)S(1)} %bitcast.14, bf16[1024,512]{1,0:T(8,128)(2,1)S(1)} %copy-done, f32[1024,512]{1,0:T(8,128)S(1)} %get-tuple-element.18.lin_ref, bf16[3,1024,512]{2,1,0:T(8,128)(2,1)S(1)} %get-tuple-element.15.x_ref, ...), custom_call_target="tpu_custom_call" | custom-call | flops 2147483648 | bytes 7340032 | tf_op jit(solution)/shard_map/pallas_call | solution.py:316
Async XLA Ops:
  0.0 7.1 %copy-start.1 = (f32[16,4]{0,1:T(4,128)S(1)}, f32[16,4]{0,1:T(4,128)}, u32[]{:S(2)}) copy-start(f32[16,4]{0,1:T(4,128)} %param.5) | copy-start | bytes 772
  2.9 9.6 %collective-permute-start.1 = (bf16[2048,128]{1,0:T(8,128)(2,1)}, bf16[2048,128]{1,0:T(8,128)(2,1)}, u32[]{:S(2)}, u32[]{:S(2)}) collective-permute-start(bf16[2048,128]{1,0:T(8,128)(2,1)} %bitcast.6.own_ref), channel_id=1, source_target_pairs={{0,4},{4,8},{8,12},{12,0},{1,5},{5,9},{9,13},{13,1},{2,6},{6,10},{... | collective-permute-start | bytes 1572872 | tf_op jit(solution)/shard_map/ppermute | solution.py:37
  3.5 3.6 %collective-permute-start = (bf16[4,128,128]{2,1,0:T(8,128)(2,1)S(1)}, bf16[4,128,128]{2,1,0:T(8,128)(2,1)S(1)}, u32[]{:S(2)}, u32[]{:S(2)}) collective-permute-start(bf16[4,128,128]{2,1,0:T(8,128)(2,1)S(1)} %get-tuple-element.17.mine_ref), channel_id=1, source_target_pairs={{0,4},{4,0},{8,12},{12,8},{1,5},{5,1},{9,13},{13,9},{2,6},{6,2},{1... | collective-permute-start | bytes 393224 | tf_op jit(solution)/shard_map/ppermute | solution.py:31
  6.1 6.5 %copy-start = (bf16[1024,512]{1,0:T(8,128)(2,1)S(1)}, bf16[1024,512]{1,0:T(8,128)(2,1)}, u32[]{:S(2)}) copy-start(bf16[1024,512]{1,0:T(8,128)(2,1)} %q_ref.3) | copy-start | bytes 3145732
  10.5 7.7 %collective-permute-start.2 = (bf16[4,128,128]{2,1,0:T(8,128)(2,1)S(1)}, bf16[4,128,128]{2,1,0:T(8,128)(2,1)S(1)}, u32[]{:S(2)}, u32[]{:S(2)}) collective-permute-start(bf16[4,128,128]{2,1,0:T(8,128)(2,1)S(1)} %get-tuple-element.24), channel_id=1, source_target_pairs={{0,8},{4,12},{8,0},{12,4},{1,9},{5,13},{9,1},{13,5},{2,10},{6,14},... | collective-permute-start | bytes 393224 | tf_op jit(solution)/shard_map/ppermute | solution.py:31

commit v6 on v5

--- a/solution.py
+++ b/solution.py
@@ -185,100 +185,64 @@
     )(table, planes, own_kv, mine, near)
 
 
-def edge_masks(block):
+def own_kernel(heads, block, q_ref, k_own, v_own, sums_ref, top_ref):
+    tok = q_ref.shape[0]
     row = lax.broadcasted_iota(jnp.int32, (block, block), 0)
     col = lax.broadcasted_iota(jnp.int32, (block, block), 1)
-    low = jnp.where(col >= row, 0.0, NEG).astype(F32)
-    high = jnp.where(col <= row, 0.0, NEG).astype(F32)
-    return low, high
-
-
-def softmax_block(q, start, before, own, masks, first):
-    low, high = masks
-    block = q.shape[0]
-    end = start + block
-    twice = jnp.concatenate([q, q], axis=1)
-    left = nt_dot(twice, before[0][start:, :])
-    right = nt_dot(twice, own[0][:end, :])
-    edge = left[:, :block] + low
-    left = jnp.concatenate([edge, left[:, block:]], axis=1) if left.shape[1] > block else edge
-    edge = right[:, start:] + high
-    right = jnp.concatenate([right[:, :start], edge], axis=1) if start else edge
-    m_left = jnp.max(left, axis=1, keepdims=True)
-    m_right = jnp.max(right, axis=1, keepdims=True)
-    m = jnp.where(first, m_right, jnp.maximum(m_left, m_right))
-    m_left = jnp.where(first, FAR, m)
-    out = jnp.dot(jnp.exp2(left - m_left).astype(BF16), before[1][start:, :], preferred_element_type=F32)
-    out = out + jnp.dot(jnp.exp2(right - m).astype(BF16), own[1][:end, :], preferred_element_type=F32)
-    return out[:, :HD] / out[:, HD:]
-
-
-def late_kernel(
-    heads, block, place_ref, q_ref, before_ref, k_own, v_own, out_ref, k_before, v_before, stage, raw, sem
-):
-    load = pltpu.make_async_copy(before_ref, raw, sem)
-    load.start()
-    half = out_ref.shape[0]
-    tok = 2 * half
-    first = place_ref[0] == 0
-    masks = edge_masks(block)
-    load.wait()
-    take_apart(raw[...], stage, k_before, v_before)
-    for start in range(half, tok, block):
+    mask = jnp.where(col <= row, 0.0, NEG).astype(F32)
+    for start in range(0, tok, block):
+        end = start + block
         for h in range(heads):
-            q = q_ref[start : start + block, lanes(h)]
-            out = softmax_block(q, start, (k_before, v_before), (k_own, v_own), masks, first)
-            out_ref[start - half : start - half + block, lanes(h)] = out.astype(BF16)
-
-
-def late_call(place, soft_q, before, k_own, v_own, block):
+            q = q_ref[start:end, lanes(h)]
+            scores = nt_dot(jnp.concatenate([q, q], axis=1), k_own[:end, :])
+            edge = scores[:, start:] + mask
+            scores = jnp.concatenate([scores[:, :start], edge], axis=1) if start else edge
+            top = jnp.max(scores, axis=1, keepdims=True)
+            sums_ref[h, start:end, :] = jnp.dot(
+                jnp.exp2(scores - top).astype(BF16), v_own[:end, :], preferred_element_type=F32
+            )
+            top_ref[h, start:end, :] = jnp.broadcast_to(top, (block, HD))
+
+
+def own_call(soft_q, k_own, v_own, block):
     tok, width = soft_q.shape
-    half = tok // 2
     heads = width // HD
-    keys = pltpu.VMEM((tok, 2 * HD), BF16)
     return pl.pallas_call(
-        functools.partial(late_kernel, heads, block),
-        in_specs=[SMEM, VMEM, ANY, VMEM, VMEM],
-        out_specs=[VMEM] * 3,
-        out_shape=[pltpu.VMEM((half, width), BF16), keys, keys],
-        scratch_shapes=[
-            pltpu.VMEM((2 * tok, HD), F32),
-            pltpu.VMEM((2 * tok, HD), BF16),
-            pltpu.SemaphoreType.DMA(()),
-        ],
+        functools.partial(own_kernel, heads, block),
+        in_specs=[VMEM] * 3,
+        out_specs=[VMEM] * 2,
+        out_shape=[pltpu.VMEM((heads, tok, 2 * HD), F32), pltpu.VMEM((heads, tok, HD), F32)],
         compiler_params=PARAMS,
         cost_estimate=pl.CostEstimate(
-            flops=6 * half * tok * width, bytes_accessed=6 * tok * width, transcendentals=half * tok * heads
+            flops=3 * tok * tok * width, bytes_accessed=6 * tok * width, transcendentals=tok * tok * heads // 2
         ),
-    )(place, soft_q, before, k_own, v_own)
+    )(soft_q, k_own, v_own)
 
 
 def last_kernel(
-    heads, block, rounds, place_ref, table_ref, q_ref, lin_ref, x_ref, k_before, v_before, k_own, v_own, soft_ref, *refs
+    heads, block, rounds, place_ref, table_ref, q_ref, lin_ref, x_ref, before_ref, sums_ref, top_ref, *refs
 ):
     state_refs = refs[:rounds]
-    out_hbm, mixed, packed, cross, out_sems = refs[rounds:]
-    pairs = heads // 2 if heads % 2 == 0 else heads
-    together = heads // pairs
-    cross[...] = jnp.zeros_like(cross)
+    out_hbm, mixed, packed, cross, k_before, v_before, stage, raw, in_sem, out_sems = refs[rounds:]
     tok = q_ref.shape[0]
-    half = tok // 2
+    load = pltpu.make_async_copy(before_ref, raw, in_sem)
+    load.start()
     place = place_ref[0]
     first = place == 0
     stride = 2 * heads
     local_bits = tok.bit_length() - 1
-    masks = edge_masks(block)
-    stores = []
+    pairs = heads // 2 if heads % 2 == 0 else heads
+    together = heads // pairs
+    cross[...] = jnp.zeros_like(cross)
     for h in range(heads):
         total = jnp.zeros((HD, HD), F32)
         for bit, ref in enumerate(state_refs):
             earlier = jnp.bitwise_and(jnp.right_shift(place, bit), 1) == 1
             factor = jnp.where(earlier, table_ref[h, local_bits + bit + 1], 0.0)
             total = total + factor * ref[h].astype(F32)
-        at = slice(h % together * HD, (h % together + 1) * HD)
+        at = lanes(h % together)
         cross[h // together, at, at] = total.astype(BF16)
-
-    def linear_rows(start):
+    for start in range(0, tok, block):
         rows = slice(start, start + block)
         for pair in range(pairs):
             wide = slice(pair * together * HD, (pair + 1) * together * HD)
@@ -286,49 +250,61 @@
             for i in range(together):
                 total = both[:, lanes(i)]
                 norm = total * lax.rsqrt(jnp.mean(total * total, axis=1, keepdims=True) + 1e-06)
-                mixed[2 * (pair * together + i)] = norm
-
-    def send(start):
+                mixed[start // block, 2 * (pair * together + i)] = norm
+
+    load.wait()
+    take_apart(raw[...], stage, k_before, v_before)
+    row = lax.broadcasted_iota(jnp.int32, (block, block), 0)
+    col = lax.broadcasted_iota(jnp.int32, (block, block), 1)
+    mask = jnp.where(col >= row, 0.0, NEG).astype(F32)
+    stores = []
+    for start in range(0, tok, block):
+        index = start // block
+        for h in range(heads):
+            q = q_ref[start : start + block, lanes(h)]
+            scores = nt_dot(jnp.concatenate([q, q], axis=1), k_before[start:, :])
+            edge = scores[:, :block] + mask
+            scores = jnp.concatenate([edge, scores[:, block:]], axis=1) if start + block < tok else edge
+            top = jnp.max(scores, axis=1, keepdims=True)
+            top_own = top_ref[h, start : start + block, 0:1]
+            both = jnp.where(first, top_own, jnp.maximum(top, top_own))
+            probs = jnp.exp2(scores - jnp.where(first, FAR, both)).astype(BF16)
+            sums = jnp.dot(probs, v_before[start:, :], preferred_element_type=F32)
+            sums = sums + sums_ref[h, start : start + block, :] * jnp.exp2(top_own - both)
+            mixed[index, 2 * h + 1] = sums[:, :HD] / sums[:, HD:]
         rows = pl.ds(start * stride, block * stride)
-        packed[rows, :] = jnp.swapaxes(mixed[...], 0, 1).reshape(block * stride, HD).astype(BF16)
-        store = pltpu.make_async_copy(packed.at[rows, :], out_hbm.at[rows, :], out_sems.at[start // block])
+        packed[rows, :] = jnp.swapaxes(mixed[index], 0, 1).reshape(block * stride, HD).astype(BF16)
+        store = pltpu.make_async_copy(packed.at[rows, :], out_hbm.at[rows, :], out_sems.at[index])
         store.start()
         stores.append(store)
-
-    for start in range(half, tok, block):
-        for h in range(heads):
-            mixed[2 * h + 1] = soft_ref[start - half : start - half + block, lanes(h)].astype(F32)
-        linear_rows(start)
-        send(start)
-    for start in range(0, half, block):
-        linear_rows(start)
-        for h in range(heads):
-            q = q_ref[start : start + block, lanes(h)]
-            mixed[2 * h + 1] = softmax_block(q, start, (k_before, v_before), (k_own, v_own), masks, first)
-        send(start)
     for store in stores:
         store.wait()
 
 
-def last_call(place, table, soft_q, partial, planes, before, own, soft_late, states, block):
+def last_call(place, table, soft_q, partial, planes, before, sums, top, states, block):
     tok, width = soft_q.shape
     heads = width // HD
     return pl.pallas_call(
         functools.partial(last_kernel, heads, block, len(states)),
-        in_specs=[SMEM, SMEM] + [VMEM] * (8 + len(states)),
+        in_specs=[SMEM, SMEM, VMEM, VMEM, VMEM, ANY, VMEM, VMEM] + [VMEM] * len(states),
         out_specs=ANY,
         out_shape=jax.ShapeDtypeStruct((tok * 2 * heads, HD), BF16),
         scratch_shapes=[
-            pltpu.VMEM((2 * heads, block, HD), F32),
+            pltpu.VMEM((tok // block, 2 * heads, block, HD), F32),
             pltpu.VMEM((tok * 2 * heads, HD), BF16),
             pltpu.VMEM((heads // 2, 2 * HD, 2 * HD) if heads % 2 == 0 else (heads, HD, HD), BF16),
+            pltpu.VMEM((tok, 2 * HD), BF16),
+            pltpu.VMEM((tok, 2 * HD), BF16),
+            pltpu.VMEM((2 * tok, HD), F32),
+            pltpu.VMEM((2 * tok, HD), BF16),
+            pltpu.SemaphoreType.DMA(()),
             pltpu.SemaphoreType.DMA((tok // block,)),
         ],
         compiler_params=PARAMS,
         cost_estimate=pl.CostEstimate(
-            flops=8 * tok * tok * width // 2, bytes_accessed=14 * tok * width, transcendentals=tok * tok * heads // 2
+            flops=4 * tok * tok * width, bytes_accessed=14 * tok * width, transcendentals=tok * tok * heads // 2
         ),
-    )(place, table, soft_q, partial, planes, *before, *own, soft_late, *states)
+    )(place, table, soft_q, partial, planes, before, sums, top, *states)
 
 
 def local(lin_qkv, level_weights, soft_q, soft_kv):
@@ -353,8 +329,8 @@
         if bit > 1:
             group_sum = (group_sum.astype(F32) + states[-1].astype(F32)).astype(BF16)
         states.append(partner_2(group_sum, "seq", bit))
-    soft_late, *earlier = late_call(place, soft_q, before, *own, block)
-    out = last_call(place, table, soft_q, partial, planes, earlier, own, soft_late, states, block)
+    sums, top = own_call(soft_q, *own, block)
+    out = last_call(place, table, soft_q, partial, planes, before, sums, top, states, block)
     out = out.reshape(tok, q_heads, 2, HD).transpose(0, 2, 1, 3)
     return out.reshape(tok, 2, q_heads * HD)
 

time: 25.4 us -> 25.9 us (1.020)
  Pallas kernels: 18.9 us -> 19.9 us
  waiting for transfers between devices: 2.2 us -> 1.67 us
    pallas_call x1, Pallas kernels: 7.01 us -> 9.38 us  [last_call(): pl.pallas_call(functools.partial(last_kernel, heads, block, len(states)),...]
    pallas_call x1, Pallas kernels: 5.56 us -> 4.24 us  [own_call(): pl.pallas_call(functools.partial(own_kernel, heads, block), in_specs=[VME...]
    ppermute x1, waiting for transfers between devices: 1.21 us -> 0.01 us  [passed_along(): return lax.ppermute(x, axis, pairs)]
    ppermute x2, waiting for transfers between devices: 0.99 us -> 1.67 us  [partner_2(): return lax.ppermute(value, axis, pairs)]
  transfers between devices with their start and end apart: 3 -> 3, of which waited for: 2 -> 2; matrix products, arithmetic and copies ran while one was open for 0% -> 0% of each run, Pallas kernels for 36% -> 30%
where the time goes in v6:
time: 25.9 us; the launch traced here: 25.7 us
  Pallas kernels  19.9 us (77%)
  starting transfers between devices  4.04 us (16%)
  waiting for transfers between devices  1.67 us (6%)
    pallas_call x1, Pallas kernels, last_call(): pl.pallas_call(functools.partial(last_kernel, heads, block, len(states)),...  9.38 us
    pallas_call x1, Pallas kernels, own_call(): pl.pallas_call(functools.partial(own_kernel, heads, block), in_specs=[VME...  4.24 us
    ppermute x2, starting transfers between devices, partner_2(): return lax.ppermute(value, axis, pairs)  3.49 us
    pallas_call x1, Pallas kernels, linear_call(): pl.pallas_call(functools.partial(linear_kernel, heads), in_specs=[SMEM, V...  3.39 us
    pallas_call x1, Pallas kernels, first_call(): pl.pallas_call(functools.partial(first_kernel, heads), in_specs=[SMEM, HB...  2.93 us
    ppermute x2, waiting for transfers between devices, partner_2(): return lax.ppermute(value, axis, pairs)  1.67 us
    ppermute x1, starting transfers between devices, passed_along(): return lax.ppermute(x, axis, pairs)  0.54 us
  transfers between devices with their start and end apart: 3, of which 2 were waited for; matrix products, arithmetic and copies ran while one was open for 0% of the time, Pallas kernels for 30%

profile of v6, /device:TPU:0, one launch (start us, length us, event | category | flops | bytes accessed | tf_op | source)
XLA Modules:
  0.0 25.7 jit_solution(1419027834494467962)
XLA Ops:
  0.0 0.0 copy-start.1
  0.0 2.9 %shard_map.46 = (bf16[1024,2,128]{2,1,0:T(2,128)(2,1)}, bf16[4,128,128]{2,1,0:T(8,128)(2,1)S(1)}, bf16[3,1024,512]{2,1,0:T(8,128)(2,1)S(1)}) custom-call(s32[1]{0:T(128)} %bitcast.2.index_ref, bf16[1024,2,2,128]{3,2,1,0:T(2,128)(2,1)} %bitcast.16, bf16[3,1024,512]{2,1,0:T(8,128)(2,1)} %bitcast.15), custom_call_target="tpu_custom_call" | custom-call | flops 134217728 | bytes 2097152 | tf_op jit(solution)/shard_map/pallas_call | solution.py:90
  2.9 0.5 %collective-permute-start.1 = (bf16[2048,128]{1,0:T(8,128)(2,1)}, bf16[2048,128]{1,0:T(8,128)(2,1)}, u32[]{:S(2)}, u32[]{:S(2)}) collective-permute-start(bf16[2048,128]{1,0:T(8,128)(2,1)} %bitcast.6.own_ref), channel_id=1, source_target_pairs={{0,4},{4,8},{8,12},{12,0},{1,5},{5,9},{9,13},{13,1},{2,6},{6,10},{... | collective-permute-start | bytes 1572872 | tf_op jit(solution)/shard_map/ppermute | solution.py:37
  3.5 2.6 %collective-permute-start = (bf16[4,128,128]{2,1,0:T(8,128)(2,1)S(1)}, bf16[4,128,128]{2,1,0:T(8,128)(2,1)S(1)}, u32[]{:S(2)}, u32[]{:S(2)}) collective-permute-start(bf16[4,128,128]{2,1,0:T(8,128)(2,1)S(1)} %get-tuple-element.16.mine_ref), channel_id=1, source_target_pairs={{0,4},{4,0},{8,12},{12,8},{1,5},{5,1},{9,13},{13,9},{2,6},{6,2},{1... | collective-permute-start | bytes 393224 | tf_op jit(solution)/shard_map/ppermute | solution.py:31
  6.1 0.0 copy-start
  6.1 1.0 %collective-permute-done.near_ref.refs_0_ = bf16[4,128,128]{2,1,0:T(8,128)(2,1)S(1)} collective-permute-done((bf16[4,128,128]{2,1,0:T(8,128)(2,1)S(1)}, bf16[4,128,128]{2,1,0:T(8,128)(2,1)S(1)}, u32[]{:S(2)}, u32[]{:S(2)}) %collective-permute-start) | collective-permute-done | bytes 131104 | tf_op jit(solution)/shard_map/ppermute | solution.py:31
  7.1 0.0 copy-done.1
  7.1 3.4 %shard_map.47 = (f32[1024,512]{1,0:T(8,128)S(1)}, bf16[4,128,128]{2,1,0:T(8,128)(2,1)S(1)}, bf16[1024,256]{1,0:T(8,128)(2,1)S(1)}, bf16[1024,256]{1,0:T(8,128)(2,1)S(1)}) custom-call(f32[4,16]{1,0:T(4,128)S(1)} %bitcast.13, bf16[3,1024,512]{2,1,0:T(8,128)(2,1)S(1)} %get-tuple-element.14.x_ref, bf16[2048,128]{1,0:T(8,128)(2,1)} %bitcast.6.own_ref, ...), custom_call_target="tpu_custom_call" | custom-call | flops 1073741824 | bytes 5242880 | tf_op jit(solution)/shard_map/pallas_call | solution.py:170
  10.5 0.9 %collective-permute-start.2 = (bf16[4,128,128]{2,1,0:T(8,128)(2,1)S(1)}, bf16[4,128,128]{2,1,0:T(8,128)(2,1)S(1)}, u32[]{:S(2)}, u32[]{:S(2)}) collective-permute-start(bf16[4,128,128]{2,1,0:T(8,128)(2,1)S(1)} %get-tuple-element.22), channel_id=1, source_target_pairs={{0,8},{4,12},{8,0},{12,4},{1,9},{5,13},{9,1},{13,5},{2,10},{6,14},... | collective-permute-start | bytes 393224 | tf_op jit(solution)/shard_map/ppermute | solution.py:31
  11.4 0.0 copy-done
  11.4 4.2 %shard_map.48 = (f32[4,1024,256]{2,1,0:T(8,128)S(1)}, f32[4,1024,128]{2,1,0:T(8,128)S(1)}) custom-call(bf16[1024,512]{1,0:T(8,128)(2,1)S(1)} %copy-done, bf16[1024,256]{1,0:T(8,128)(2,1)S(1)} %get-tuple-element.18.k_own, bf16[1024,256]{1,0:T(8,128)(2,1)S(1)} %get-tuple-element.19.v_own), custom_call_target="tpu_custom_call" | custom-call | flops 1610612736 | bytes 3145728 | tf_op jit(solution)/shard_map/pallas_call | solution.py:210
  15.6 0.7 %collective-permute-done.2.refs_1_ = bf16[4,128,128]{2,1,0:T(8,128)(2,1)S(1)} collective-permute-done((bf16[4,128,128]{2,1,0:T(8,128)(2,1)S(1)}, bf16[4,128,128]{2,1,0:T(8,128)(2,1)S(1)}, u32[]{:S(2)}, u32[]{:S(2)}) %collective-permute-start.2) | collective-permute-done | bytes 131104 | tf_op jit(solution)/shard_map/ppermute | solution.py:31
  16.3 0.0 collective-permute-done.1.before_ref
  16.3 9.4 %shard_map.49 = bf16[8192,128]{1,0:T(8,128)(2,1)} custom-call(s32[1]{0:T(128)} %bitcast.place_ref, f32[4,16]{1,0:T(4,128)S(1)} %bitcast.14, bf16[1024,512]{1,0:T(8,128)(2,1)S(1)} %copy-done, f32[1024,512]{1,0:T(8,128)S(1)} %get-tuple-element.17.lin_ref, bf16[3,1024,512]{2,1,0:T(8,128)(2,1)S(1)} %get-tuple-element.14.x_ref, ...), custom_call_target="tpu_custom_call" | custom-call | flops 2147483648 | bytes 7340032 | tf_op jit(solution)/shard_map/pallas_call | solution.py:287
Async XLA Ops:
  0.0 7.1 %copy-start.1 = (f32[16,4]{0,1:T(4,128)S(1)}, f32[16,4]{0,1:T(4,128)}, u32[]{:S(2)}) copy-start(f32[16,4]{0,1:T(4,128)} %param.5) | copy-start | bytes 772
  2.9 13.4 %collective-permute-start.1 = (bf16[2048,128]{1,0:T(8,128)(2,1)}, bf16[2048,128]{1,0:T(8,128)(2,1)}, u32[]{:S(2)}, u32[]{:S(2)}) collective-permute-start(bf16[2048,128]{1,0:T(8,128)(2,1)} %bitcast.6.own_ref), channel_id=1, source_target_pairs={{0,4},{4,8},{8,12},{12,0},{1,5},{5,9},{9,13},{13,1},{2,6},{6,10},{... | collective-permute-start | bytes 1572872 | tf_op jit(solution)/shard_map/ppermute | solution.py:37
  3.5 3.6 %collective-permute-start = (bf16[4,128,128]{2,1,0:T(8,128)(2,1)S(1)}, bf16[4,128,128]{2,1,0:T(8,128)(2,1)S(1)}, u32[]{:S(2)}, u32[]{:S(2)}) collective-permute-start(bf16[4,128,128]{2,1,0:T(8,128)(2,1)S(1)} %get-tuple-element.16.mine_ref), channel_id=1, source_target_pairs={{0,4},{4,0},{8,12},{12,8},{1,5},{5,1},{9,13},{13,9},{2,6},{6,2},{1... | collective-permute-start | bytes 393224 | tf_op jit(solution)/shard_map/ppermute | solution.py:31
  6.1 5.3 %copy-start = (bf16[1024,512]{1,0:T(8,128)(2,1)S(1)}, bf16[1024,512]{1,0:T(8,128)(2,1)}, u32[]{:S(2)}) copy-start(bf16[1024,512]{1,0:T(8,128)(2,1)} %q_ref.3) | copy-start | bytes 3145732
  10.5 5.8 %collective-permute-start.2 = (bf16[4,128,128]{2,1,0:T(8,128)(2,1)S(1)}, bf16[4,128,128]{2,1,0:T(8,128)(2,1)S(1)}, u32[]{:S(2)}, u32[]{:S(2)}) collective-permute-start(bf16[4,128,128]{2,1,0:T(8,128)(2,1)S(1)} %get-tuple-element.22), channel_id=1, source_target_pairs={{0,8},{4,12},{8,0},{12,4},{1,9},{5,13},{9,1},{13,5},{2,10},{6,14},... | collective-permute-start | bytes 393224 | tf_op jit(solution)/shard_map/ppermute | solution.py:31

commit v7 on v6

--- a/solution.py
+++ b/solution.py
@@ -185,45 +185,49 @@
     )(table, planes, own_kv, mine, near)
 
 
-def own_kernel(heads, block, q_ref, k_own, v_own, sums_ref, top_ref):
-    tok = q_ref.shape[0]
+def attend_own(q_ref, k_own, v_own, start, block, h, sums_ref, top_ref, at):
     row = lax.broadcasted_iota(jnp.int32, (block, block), 0)
     col = lax.broadcasted_iota(jnp.int32, (block, block), 1)
     mask = jnp.where(col <= row, 0.0, NEG).astype(F32)
-    for start in range(0, tok, block):
-        end = start + block
+    end = start + block
+    q = q_ref[start:end, lanes(h)]
+    scores = nt_dot(jnp.concatenate([q, q], axis=1), k_own[:end, :])
+    edge = scores[:, start:] + mask
+    scores = jnp.concatenate([scores[:, :start], edge], axis=1) if start else edge
+    top = jnp.max(scores, axis=1, keepdims=True)
+    sums_ref[h, at : at + block, :] = jnp.dot(
+        jnp.exp2(scores - top).astype(BF16), v_own[:end, :], preferred_element_type=F32
+    )
+    top_ref[h, at : at + block, :] = jnp.broadcast_to(top, (block, HD))
+
+
+def own_kernel(heads, block, q_ref, k_own, v_own, sums_ref, top_ref):
+    for start in range(0, sums_ref.shape[1], block):
         for h in range(heads):
-            q = q_ref[start:end, lanes(h)]
-            scores = nt_dot(jnp.concatenate([q, q], axis=1), k_own[:end, :])
-            edge = scores[:, start:] + mask
-            scores = jnp.concatenate([scores[:, :start], edge], axis=1) if start else edge
-            top = jnp.max(scores, axis=1, keepdims=True)
-            sums_ref[h, start:end, :] = jnp.dot(
-                jnp.exp2(scores - top).astype(BF16), v_own[:end, :], preferred_element_type=F32
-            )
-            top_ref[h, start:end, :] = jnp.broadcast_to(top, (block, HD))
+            attend_own(q_ref, k_own, v_own, start, block, h, sums_ref, top_ref, start)
 
 
 def own_call(soft_q, k_own, v_own, block):
     tok, width = soft_q.shape
     heads = width // HD
+    rows = tok - block
     return pl.pallas_call(
         functools.partial(own_kernel, heads, block),
         in_specs=[VMEM] * 3,
         out_specs=[VMEM] * 2,
-        out_shape=[pltpu.VMEM((heads, tok, 2 * HD), F32), pltpu.VMEM((heads, tok, HD), F32)],
+        out_shape=[pltpu.VMEM((heads, rows, 2 * HD), F32), pltpu.VMEM((heads, rows, HD), F32)],
         compiler_params=PARAMS,
         cost_estimate=pl.CostEstimate(
-            flops=3 * tok * tok * width, bytes_accessed=6 * tok * width, transcendentals=tok * tok * heads // 2
+            flops=2 * tok * tok * width, bytes_accessed=6 * tok * width, transcendentals=tok * tok * heads // 2
         ),
     )(soft_q, k_own, v_own)
 
 
 def last_kernel(
-    heads, block, rounds, place_ref, table_ref, q_ref, lin_ref, x_ref, before_ref, sums_ref, top_ref, *refs
+    heads, block, rounds, place_ref, table_ref, q_ref, lin_ref, x_ref, before_ref, k_own, v_own, sums_ref, top_ref, *refs
 ):
     state_refs = refs[:rounds]
-    out_hbm, mixed, packed, cross, k_before, v_before, stage, raw, in_sem, out_sems = refs[rounds:]
+    out_hbm, mixed, packed, cross, k_before, v_before, stage, raw, sums_end, top_end, in_sem, out_sems = refs[rounds:]
     tok = q_ref.shape[0]
     load = pltpu.make_async_copy(before_ref, raw, in_sem)
     load.start()
@@ -242,7 +246,8 @@
             total = total + factor * ref[h].astype(F32)
         at = lanes(h % together)
         cross[h // together, at, at] = total.astype(BF16)
-    for start in range(0, tok, block):
+
+    def linear_rows(start):
         rows = slice(start, start + block)
         for pair in range(pairs):
             wide = slice(pair * together * HD, (pair + 1) * together * HD)
@@ -250,53 +255,74 @@
             for i in range(together):
                 total = both[:, lanes(i)]
                 norm = total * lax.rsqrt(jnp.mean(total * total, axis=1, keepdims=True) + 1e-06)
-                mixed[start // block, 2 * (pair * together + i)] = norm
-
+                at = start * stride + 2 * (pair * together + i)
+                mixed[pl.ds(at, block, stride=stride), :] = norm
+
+    for h in range(heads):
+        attend_own(q_ref, k_own, v_own, tok - block, block, h, sums_end, top_end, 0)
     load.wait()
     take_apart(raw[...], stage, k_before, v_before)
     row = lax.broadcasted_iota(jnp.int32, (block, block), 0)
     col = lax.broadcasted_iota(jnp.int32, (block, block), 1)
     mask = jnp.where(col >= row, 0.0, NEG).astype(F32)
-    stores = []
-    for start in range(0, tok, block):
-        index = start // block
+
+    def copy_out(start):
+        rows = pl.ds(start * stride, block * stride)
+        return pltpu.make_async_copy(packed.at[rows, :], out_hbm.at[rows, :], out_sems.at[start // block])
+
+    def send(start):
+        rows = pl.ds(start * stride, block * stride)
+        packed[rows, :] = mixed[rows, :].astype(BF16)
+        copy_out(start).start()
+
+    def attend(start):
+        linear_rows(start)
         for h in range(heads):
             q = q_ref[start : start + block, lanes(h)]
             scores = nt_dot(jnp.concatenate([q, q], axis=1), k_before[start:, :])
             edge = scores[:, :block] + mask
             scores = jnp.concatenate([edge, scores[:, block:]], axis=1) if start + block < tok else edge
             top = jnp.max(scores, axis=1, keepdims=True)
-            top_own = top_ref[h, start : start + block, 0:1]
+            sums_own, top_own = (sums_end, top_end) if start + block == tok else (sums_ref, top_ref)
+            at = 0 if start + block == tok else start
+            sums_own, top_own = sums_own[h, at : at + block, :], top_own[h, at : at + block, :]
             both = jnp.where(first, top_own, jnp.maximum(top, top_own))
-            probs = jnp.exp2(scores - jnp.where(first, FAR, both)).astype(BF16)
+            off = jnp.where(first, FAR, both)
+            probs = jnp.exp2(scores - jnp.concatenate([off] * (scores.shape[1] // HD), axis=1)).astype(BF16)
             sums = jnp.dot(probs, v_before[start:, :], preferred_element_type=F32)
-            sums = sums + sums_ref[h, start : start + block, :] * jnp.exp2(top_own - both)
-            mixed[index, 2 * h + 1] = sums[:, :HD] / sums[:, HD:]
-        rows = pl.ds(start * stride, block * stride)
-        packed[rows, :] = jnp.swapaxes(mixed[index], 0, 1).reshape(block * stride, HD).astype(BF16)
-        store = pltpu.make_async_copy(packed.at[rows, :], out_hbm.at[rows, :], out_sems.at[index])
-        store.start()
-        stores.append(store)
-    for store in stores:
-        store.wait()
-
-
-def last_call(place, table, soft_q, partial, planes, before, sums, top, states, block):
+            factor = jnp.exp2(top_own - both)
+            sums = sums + sums_own * jnp.concatenate([factor, factor], axis=1)
+            mixed[pl.ds(start * stride + 2 * h + 1, block, stride=stride), :] = sums[:, :HD] / sums[:, HD:]
+
+    for start in range(0, tok, block):
+
+        if start:
+            send(start - block)
+        attend(start)
+
+    send(tok - block)
+    for start in range(0, tok, block):
+        copy_out(start).wait()
+
+
+def last_call(place, table, soft_q, partial, planes, before, own, sums, top, states, block):
     tok, width = soft_q.shape
     heads = width // HD
     return pl.pallas_call(
         functools.partial(last_kernel, heads, block, len(states)),
-        in_specs=[SMEM, SMEM, VMEM, VMEM, VMEM, ANY, VMEM, VMEM] + [VMEM] * len(states),
+        in_specs=[SMEM, SMEM, VMEM, VMEM, VMEM, ANY] + [VMEM] * (4 + len(states)),
         out_specs=ANY,
         out_shape=jax.ShapeDtypeStruct((tok * 2 * heads, HD), BF16),
         scratch_shapes=[
-            pltpu.VMEM((tok // block, 2 * heads, block, HD), F32),
+            pltpu.VMEM((tok * 2 * heads, HD), F32),
             pltpu.VMEM((tok * 2 * heads, HD), BF16),
             pltpu.VMEM((heads // 2, 2 * HD, 2 * HD) if heads % 2 == 0 else (heads, HD, HD), BF16),
             pltpu.VMEM((tok, 2 * HD), BF16),
             pltpu.VMEM((tok, 2 * HD), BF16),
             pltpu.VMEM((2 * tok, HD), F32),
             pltpu.VMEM((2 * tok, HD), BF16),
+            pltpu.VMEM((heads, block, 2 * HD), F32),
+            pltpu.VMEM((heads, block, HD), F32),
             pltpu.SemaphoreType.DMA(()),
             pltpu.SemaphoreType.DMA((tok // block,)),
         ],
@@ -304,7 +330,7 @@
         cost_estimate=pl.CostEstimate(
             flops=4 * tok * tok * width, bytes_accessed=14 * tok * width, transcendentals=tok * tok * heads // 2
         ),
-    )(place, table, soft_q, partial, planes, before, sums, top, *states)
+    )(place, table, soft_q, partial, planes, before, *own, sums, top, *states)
 
 
 def local(lin_qkv, level_weights, soft_q, soft_kv):
@@ -330,7 +356,7 @@
             group_sum = (group_sum.astype(F32) + states[-1].astype(F32)).astype(BF16)
         states.append(partner_2(group_sum, "seq", bit))
     sums, top = own_call(soft_q, *own, block)
-    out = last_call(place, table, soft_q, partial, planes, before, sums, top, states, block)
+    out = last_call(place, table, soft_q, partial, planes, before, own, sums, top, states, block)
     out = out.reshape(tok, q_heads, 2, HD).transpose(0, 2, 1, 3)
     return out.reshape(tok, 2, q_heads * HD)
 

time: 25.9 us -> 30 us (1.16)
  local copies, waits for them, and re-layouts: 0.01 us -> 6.41 us
  Pallas kernels: 19.9 us -> 18.3 us
  waiting for transfers between devices: 1.67 us -> 0.99 us
    unnamed x4 -> x16, local copies, waits for them, and re-layouts: 0.01 us -> 6.41 us
    pallas_call x1, Pallas kernels: 4.24 us -> 2.72 us  [own_call(): pl.pallas_call(functools.partial(own_kernel, heads, block), in_specs=[VME...]
    ppermute x2, waiting for transfers between devices: 1.67 us -> 0.99 us  [partner_2(): return lax.ppermute(value, axis, pairs)]
  transfers between devices with their start and end apart: 3 -> 3, of which waited for: 2 -> 1; matrix products, arithmetic and copies ran while one was open for 0% -> 0% of each run, Pallas kernels for 30% -> 21%
where the time goes in v7:
time: 30 us; the launch traced here: 29.7 us
  Pallas kernels  18.3 us (61%)
  local copies, waits for them, and re-layouts  6.41 us (21%)
  starting transfers between devices  3.97 us (13%)
  waiting for transfers between devices  0.99 us (3%)
    pallas_call x1, Pallas kernels, last_call(): pl.pallas_call(functools.partial(last_kernel, heads, block, len(states)),...  9.26 us
    unnamed x16, local copies, waits for them, and re-layouts  6.41 us
    ppermute x2, starting transfers between devices, partner_2(): return lax.ppermute(value, axis, pairs)  3.43 us
    pallas_call x1, Pallas kernels, linear_call(): pl.pallas_call(functools.partial(linear_kernel, heads), in_specs=[SMEM, V...  3.4 us
    pallas_call x1, Pallas kernels, first_call(): pl.pallas_call(functools.partial(first_kernel, heads), in_specs=[SMEM, HB...  2.93 us
    pallas_call x1, Pallas kernels, own_call(): pl.pallas_call(functools.partial(own_kernel, heads, block), in_specs=[VME...  2.72 us
    ppermute x2, waiting for transfers between devices, partner_2(): return lax.ppermute(value, axis, pairs)  0.99 us
  transfers between devices with their start and end apart: 3, of which 1 were waited for; matrix products, arithmetic and copies ran while one was open for 0% of the time, Pallas kernels for 21%

profile of v7, /device:TPU:0, one launch (start us, length us, event | category | flops | bytes accessed | tf_op | source)
XLA Modules:
  0.0 29.7 jit_solution(219300790628026074)
XLA Ops:
  0.0 0.0 copy-start.7
  0.0 2.9 %shard_map.46 = (bf16[1024,2,128]{2,1,0:T(2,128)(2,1)}, bf16[4,128,128]{2,1,0:T(8,128)(2,1)S(1)}, bf16[3,1024,512]{2,1,0:T(8,128)(2,1)S(1)}) custom-call(s32[1]{0:T(128)} %bitcast.2.index_ref, bf16[1024,2,2,128]{3,2,1,0:T(2,128)(2,1)} %bitcast.16, bf16[3,1024,512]{2,1,0:T(8,128)(2,1)} %bitcast.15), custom_call_target="tpu_custom_call" | custom-call | flops 134217728 | bytes 2097152 | tf_op jit(solution)/shard_map/pallas_call | solution.py:90
  2.9 0.5 %collective-permute-start.1 = (bf16[2048,128]{1,0:T(8,128)(2,1)}, bf16[2048,128]{1,0:T(8,128)(2,1)}, u32[]{:S(2)}, u32[]{:S(2)}) collective-permute-start(bf16[2048,128]{1,0:T(8,128)(2,1)} %bitcast.6.own_ref), channel_id=1, source_target_pairs={{0,4},{4,8},{8,12},{12,0},{1,5},{5,9},{9,13},{13,1},{2,6},{6,10},{... | collective-permute-start | bytes 1572872 | tf_op jit(solution)/shard_map/ppermute | solution.py:37
  3.5 2.6 %collective-permute-start = (bf16[4,128,128]{2,1,0:T(8,128)(2,1)S(1)}, bf16[4,128,128]{2,1,0:T(8,128)(2,1)S(1)}, u32[]{:S(2)}, u32[]{:S(2)}) collective-permute-start(bf16[4,128,128]{2,1,0:T(8,128)(2,1)S(1)} %get-tuple-element.16.mine_ref), channel_id=1, source_target_pairs={{0,4},{4,0},{8,12},{12,8},{1,5},{5,1},{9,13},{13,9},{2,6},{6,2},{1... | collective-permute-start | bytes 393224 | tf_op jit(solution)/shard_map/ppermute | solution.py:31
  6.1 1.0 %collective-permute-done.near_ref.refs_0_ = bf16[4,128,128]{2,1,0:T(8,128)(2,1)S(1)} collective-permute-done((bf16[4,128,128]{2,1,0:T(8,128)(2,1)S(1)}, bf16[4,128,128]{2,1,0:T(8,128)(2,1)S(1)}, u32[]{:S(2)}, u32[]{:S(2)}) %collective-permute-start) | collective-permute-done | bytes 131104 | tf_op jit(solution)/shard_map/ppermute | solution.py:31
  7.1 0.0 copy-done.7
  7.1 3.4 %shard_map.47 = (f32[1024,512]{1,0:T(8,128)S(1)}, bf16[4,128,128]{2,1,0:T(8,128)(2,1)S(1)}, bf16[1024,256]{1,0:T(8,128)(2,1)S(1)}, bf16[1024,256]{1,0:T(8,128)(2,1)S(1)}) custom-call(f32[4,16]{1,0:T(4,128)S(1)} %bitcast.13, bf16[3,1024,512]{2,1,0:T(8,128)(2,1)S(1)} %get-tuple-element.14.x_ref, bf16[2048,128]{1,0:T(8,128)(2,1)} %bitcast.6.own_ref, ...), custom_call_target="tpu_custom_call" | custom-call | flops 1073741824 | bytes 5242880 | tf_op jit(solution)/shard_map/pallas_call | solution.py:170
  10.5 0.0 copy-start
  10.5 1.3 %copy-done = f32[1024,512]{1,0:T(8,128)} copy-done((f32[1024,512]{1,0:T(8,128)}, f32[1024,512]{1,0:T(8,128)S(1)}, u32[]{:S(2)}) %copy-start) | copy-done | bytes 2097176
  11.8 0.0 copy-start.3
  11.8 0.8 %copy-done.3 = bf16[1024,256]{1,0:T(8,128)(2,1)} copy-done((bf16[1024,256]{1,0:T(8,128)(2,1)}, bf16[1024,256]{1,0:T(8,128)(2,1)S(1)}, u32[]{:S(2)}) %copy-start.3) | copy-done | bytes 524312
  12.6 0.0 copy-start.5
  12.6 0.8 %copy-done.5 = bf16[1024,256]{1,0:T(8,128)(2,1)} copy-done((bf16[1024,256]{1,0:T(8,128)(2,1)}, bf16[1024,256]{1,0:T(8,128)(2,1)S(1)}, u32[]{:S(2)}) %copy-start.5) | copy-done | bytes 524312
  13.4 0.8 %collective-permute-start.2 = (bf16[4,128,128]{2,1,0:T(8,128)(2,1)S(1)}, bf16[4,128,128]{2,1,0:T(8,128)(2,1)S(1)}, u32[]{:S(2)}, u32[]{:S(2)}) collective-permute-start(bf16[4,128,128]{2,1,0:T(8,128)(2,1)S(1)} %get-tuple-element.22), channel_id=1, source_target_pairs={{0,8},{4,12},{8,0},{12,4},{1,9},{5,13},{9,1},{13,5},{2,10},{6,14},... | collective-permute-start | bytes 393224 | tf_op jit(solution)/shard_map/ppermute | solution.py:31
  14.3 0.0 copy-start.1
  14.3 0.0 copy-start.2
  14.3 1.4 %copy-done.2 = bf16[1024,512]{1,0:T(8,128)(2,1)S(1)} copy-done((bf16[1024,512]{1,0:T(8,128)(2,1)S(1)}, bf16[1024,512]{1,0:T(8,128)(2,1)}, u32[]{:S(2)}) %copy-start.2) | copy-done | bytes 1048600
  15.6 0.0 copy-start.4
  15.6 1.0 %copy-done.4 = bf16[1024,256]{1,0:T(8,128)(2,1)S(1)} copy-done((bf16[1024,256]{1,0:T(8,128)(2,1)S(1)}, bf16[1024,256]{1,0:T(8,128)(2,1)}, u32[]{:S(2)}) %copy-start.4) | copy-done | bytes 524312
  16.7 0.0 copy-start.6
  16.7 1.0 %copy-done.6 = bf16[1024,256]{1,0:T(8,128)(2,1)S(1)} copy-done((bf16[1024,256]{1,0:T(8,128)(2,1)S(1)}, bf16[1024,256]{1,0:T(8,128)(2,1)}, u32[]{:S(2)}) %copy-start.6) | copy-done | bytes 524312
  17.7 2.7 %shard_map.48 = (f32[4,768,256]{2,1,0:T(8,128)S(1)}, f32[4,768,128]{2,1,0:T(8,128)S(1)}) custom-call(bf16[1024,512]{1,0:T(8,128)(2,1)S(1)} %copy-done.2, bf16[1024,256]{1,0:T(8,128)(2,1)S(1)} %copy-done.4, bf16[1024,256]{1,0:T(8,128)(2,1)S(1)} %copy-done.6), custom_call_target="tpu_custom_call" | custom-call | flops 1073741824 | bytes 3145728 | tf_op jit(solution)/shard_map/pallas_call | solution.py:214
  20.5 0.0 collective-permute-done.2.refs_1_
  20.5 0.0 collective-permute-done.1.before_ref
  20.5 0.0 copy-done.1
  20.5 9.3 %shard_map.49 = bf16[8192,128]{1,0:T(8,128)(2,1)} custom-call(s32[1]{0:T(128)} %bitcast.place_ref, f32[4,16]{1,0:T(4,128)S(1)} %bitcast.14, bf16[1024,512]{1,0:T(8,128)(2,1)S(1)} %copy-done.2, f32[1024,512]{1,0:T(8,128)S(1)} %copy-done.1, bf16[3,1024,512]{2,1,0:T(8,128)(2,1)S(1)} %get-tuple-element.14.x_ref, ...), custom_call_target="tpu_custom_call" | custom-call | flops 2147483648 | bytes 7340032 | tf_op jit(solution)/shard_map/pallas_call | solution.py:311
Async XLA Ops:
  0.0 7.1 %copy-start.7 = (f32[16,4]{0,1:T(4,128)S(1)}, f32[16,4]{0,1:T(4,128)}, u32[]{:S(2)}) copy-start(f32[16,4]{0,1:T(4,128)} %param.5) | copy-start | bytes 772
  2.9 17.5 %collective-permute-start.1 = (bf16[2048,128]{1,0:T(8,128)(2,1)}, bf16[2048,128]{1,0:T(8,128)(2,1)}, u32[]{:S(2)}, u32[]{:S(2)}) collective-permute-start(bf16[2048,128]{1,0:T(8,128)(2,1)} %bitcast.6.own_ref), channel_id=1, source_target_pairs={{0,4},{4,8},{8,12},{12,0},{1,5},{5,9},{9,13},{13,1},{2,6},{6,10},{... | collective-permute-start | bytes 1572872 | tf_op jit(solution)/shard_map/ppermute | solution.py:37
  3.5 3.6 %collective-permute-start = (bf16[4,128,128]{2,1,0:T(8,128)(2,1)S(1)}, bf16[4,128,128]{2,1,0:T(8,128)(2,1)S(1)}, u32[]{:S(2)}, u32[]{:S(2)}) collective-permute-start(bf16[4,128,128]{2,1,0:T(8,128)(2,1)S(1)} %get-tuple-element.16.mine_ref), channel_id=1, source_target_pairs={{0,4},{4,0},{8,12},{12,8},{1,5},{5,1},{9,13},{13,9},{2,6},{6,2},{1... | collective-permute-start | bytes 393224 | tf_op jit(solution)/shard_map/ppermute | solution.py:31
  10.5 1.3 %copy-start = (f32[1024,512]{1,0:T(8,128)}, f32[1024,512]{1,0:T(8,128)S(1)}, u32[]{:S(2)}) copy-start(f32[1024,512]{1,0:T(8,128)S(1)} %get-tuple-element.17.lin_ref) | copy-start | bytes 6291460
  11.8 0.8 %copy-start.3 = (bf16[1024,256]{1,0:T(8,128)(2,1)}, bf16[1024,256]{1,0:T(8,128)(2,1)S(1)}, u32[]{:S(2)}) copy-start(bf16[1024,256]{1,0:T(8,128)(2,1)S(1)} %get-tuple-element.18.k_own) | copy-start | bytes 1572868
  12.6 0.8 %copy-start.5 = (bf16[1024,256]{1,0:T(8,128)(2,1)}, bf16[1024,256]{1,0:T(8,128)(2,1)S(1)}, u32[]{:S(2)}) copy-start(bf16[1024,256]{1,0:T(8,128)(2,1)S(1)} %get-tuple-element.19.v_own) | copy-start | bytes 1572868
  13.4 7.0 %collective-permute-start.2 = (bf16[4,128,128]{2,1,0:T(8,128)(2,1)S(1)}, bf16[4,128,128]{2,1,0:T(8,128)(2,1)S(1)}, u32[]{:S(2)}, u32[]{:S(2)}) collective-permute-start(bf16[4,128,128]{2,1,0:T(8,128)(2,1)S(1)} %get-tuple-element.22), channel_id=1, source_target_pairs={{0,8},{4,12},{8,0},{12,4},{1,9},{5,13},{9,1},{13,5},{2,10},{6,14},... | collective-permute-start | bytes 393224 | tf_op jit(solution)/shard_map/ppermute | solution.py:31
  14.3 6.2 %copy-start.1 = (f32[1024,512]{1,0:T(8,128)S(1)}, f32[1024,512]{1,0:T(8,128)}, u32[]{:S(2)}) copy-start(f32[1024,512]{1,0:T(8,128)} %copy-done) | copy-start | bytes 6291460
  14.3 1.4 %copy-start.2 = (bf16[1024,512]{1,0:T(8,128)(2,1)S(1)}, bf16[1024,512]{1,0:T(8,128)(2,1)}, u32[]{:S(2)}) copy-start(bf16[1024,512]{1,0:T(8,128)(2,1)} %q_ref.3) | copy-start | bytes 3145732
  15.6 1.0 %copy-start.4 = (bf16[1024,256]{1,0:T(8,128)(2,1)S(1)}, bf16[1024,256]{1,0:T(8,128)(2,1)}, u32[]{:S(2)}) copy-start(bf16[1024,256]{1,0:T(8,128)(2,1)} %copy-done.3) | copy-start | bytes 1572868
  16.7 1.0 %copy-start.6 = (bf16[1024,256]{1,0:T(8,128)(2,1)S(1)}, bf16[1024,256]{1,0:T(8,128)(2,1)}, u32[]{:S(2)}) copy-start(bf16[1024,256]{1,0:T(8,128)(2,1)} %copy-done.5) | copy-start | bytes 1572868

commit v8 on v6

--- a/solution.py
+++ b/solution.py
@@ -242,7 +242,8 @@
             total = total + factor * ref[h].astype(F32)
         at = lanes(h % together)
         cross[h // together, at, at] = total.astype(BF16)
-    for start in range(0, tok, block):
+
+    def linear_rows(start):
         rows = slice(start, start + block)
         for pair in range(pairs):
             wide = slice(pair * together * HD, (pair + 1) * together * HD)
@@ -250,35 +251,54 @@
             for i in range(together):
                 total = both[:, lanes(i)]
                 norm = total * lax.rsqrt(jnp.mean(total * total, axis=1, keepdims=True) + 1e-06)
-                mixed[start // block, 2 * (pair * together + i)] = norm
+                at = start * stride + 2 * (pair * together + i)
+                mixed[pl.ds(at, block, stride=stride), :] = norm
+
+    for start in range(0, tok // 2, block):
+        linear_rows(start)
 
     load.wait()
     take_apart(raw[...], stage, k_before, v_before)
     row = lax.broadcasted_iota(jnp.int32, (block, block), 0)
     col = lax.broadcasted_iota(jnp.int32, (block, block), 1)
     mask = jnp.where(col >= row, 0.0, NEG).astype(F32)
-    stores = []
-    for start in range(0, tok, block):
-        index = start // block
+
+    def copy_out(start):
+        rows = pl.ds(start * stride, block * stride)
+        return pltpu.make_async_copy(packed.at[rows, :], out_hbm.at[rows, :], out_sems.at[start // block])
+
+    def send(start):
+        rows = pl.ds(start * stride, block * stride)
+        packed[rows, :] = mixed[rows, :].astype(BF16)
+        copy_out(start).start()
+
+    def attend(start):
+        if start >= tok // 2:
+            linear_rows(start)
         for h in range(heads):
             q = q_ref[start : start + block, lanes(h)]
             scores = nt_dot(jnp.concatenate([q, q], axis=1), k_before[start:, :])
             edge = scores[:, :block] + mask
             scores = jnp.concatenate([edge, scores[:, block:]], axis=1) if start + block < tok else edge
             top = jnp.max(scores, axis=1, keepdims=True)
-            top_own = top_ref[h, start : start + block, 0:1]
+            top_own = top_ref[h, start : start + block, :]
             both = jnp.where(first, top_own, jnp.maximum(top, top_own))
-            probs = jnp.exp2(scores - jnp.where(first, FAR, both)).astype(BF16)
+            off = jnp.where(first, FAR, both)
+            probs = jnp.exp2(scores - jnp.concatenate([off] * (scores.shape[1] // HD), axis=1)).astype(BF16)
             sums = jnp.dot(probs, v_before[start:, :], preferred_element_type=F32)
-            sums = sums + sums_ref[h, start : start + block, :] * jnp.exp2(top_own - both)
-            mixed[index, 2 * h + 1] = sums[:, :HD] / sums[:, HD:]
-        rows = pl.ds(start * stride, block * stride)
-        packed[rows, :] = jnp.swapaxes(mixed[index], 0, 1).reshape(block * stride, HD).astype(BF16)
-        store = pltpu.make_async_copy(packed.at[rows, :], out_hbm.at[rows, :], out_sems.at[index])
-        store.start()
-        stores.append(store)
-    for store in stores:
-        store.wait()
+            factor = jnp.exp2(top_own - both)
+            sums = sums + sums_ref[h, start : start + block, :] * jnp.concatenate([factor, factor], axis=1)
+            mixed[pl.ds(start * stride + 2 * h + 1, block, stride=stride), :] = sums[:, :HD] / sums[:, HD:]
+
+    for start in range(0, tok, block):
+
+        if start:
+            send(start - block)
+        attend(start)
+
+    send(tok - block)
+    for start in range(0, tok, block):
+        copy_out(start).wait()
 
 
 def last_call(place, table, soft_q, partial, planes, before, sums, top, states, block):
@@ -290,7 +310,7 @@
         out_specs=ANY,
         out_shape=jax.ShapeDtypeStruct((tok * 2 * heads, HD), BF16),
         scratch_shapes=[
-            pltpu.VMEM((tok // block, 2 * heads, block, HD), F32),
+            pltpu.VMEM((tok * 2 * heads, HD), F32),
             pltpu.VMEM((tok * 2 * heads, HD), BF16),
             pltpu.VMEM((heads // 2, 2 * HD, 2 * HD) if heads % 2 == 0 else (heads, HD, HD), BF16),
             pltpu.VMEM((tok, 2 * HD), BF16),

time: 25.9 us -> 24 us (0.927)
  Pallas kernels: 19.9 us -> 18 us
    pallas_call x1, Pallas kernels: 9.38 us -> 7.46 us  [last_call(): pl.pallas_call(functools.partial(last_kernel, heads, block, len(states)),...]
  transfers between devices with their start and end apart: 3 -> 3, of which waited for: 2 -> 2; matrix products, arithmetic and copies ran while one was open for 0% -> 0% of each run, Pallas kernels for 30% -> 32%
where the time goes in v8:
time: 24 us; the launch traced here: 23.8 us
  Pallas kernels  18 us (75%)
  starting transfers between devices  4.04 us (17%)
  waiting for transfers between devices  1.67 us (7%)
    pallas_call x1, Pallas kernels, last_call(): pl.pallas_call(functools.partial(last_kernel, heads, block, len(states)),...  7.46 us
    pallas_call x1, Pallas kernels, own_call(): pl.pallas_call(functools.partial(own_kernel, heads, block), in_specs=[VME...  4.24 us
    ppermute x2, starting transfers between devices, partner_2(): return lax.ppermute(value, axis, pairs)  3.49 us
    pallas_call x1, Pallas kernels, linear_call(): pl.pallas_call(functools.partial(linear_kernel, heads), in_specs=[SMEM, V...  3.39 us
    pallas_call x1, Pallas kernels, first_call(): pl.pallas_call(functools.partial(first_kernel, heads), in_specs=[SMEM, HB...  2.93 us
    ppermute x2, waiting for transfers between devices, partner_2(): return lax.ppermute(value, axis, pairs)  1.67 us
    ppermute x1, starting transfers between devices, passed_along(): return lax.ppermute(x, axis, pairs)  0.54 us
  transfers between devices with their start and end apart: 3, of which 2 were waited for; matrix products, arithmetic and copies ran while one was open for 0% of the time, Pallas kernels for 32%

profile of v8, /device:TPU:0, one launch (start us, length us, event | category | flops | bytes accessed | tf_op | source)
XLA Modules:
  0.0 23.8 jit_solution(16775251922137549526)
XLA Ops:
  0.0 0.0 copy-start.1
  0.0 2.9 %shard_map.46 = (bf16[1024,2,128]{2,1,0:T(2,128)(2,1)}, bf16[4,128,128]{2,1,0:T(8,128)(2,1)S(1)}, bf16[3,1024,512]{2,1,0:T(8,128)(2,1)S(1)}) custom-call(s32[1]{0:T(128)} %bitcast.2.index_ref, bf16[1024,2,2,128]{3,2,1,0:T(2,128)(2,1)} %bitcast.16, bf16[3,1024,512]{2,1,0:T(8,128)(2,1)} %bitcast.15), custom_call_target="tpu_custom_call" | custom-call | flops 134217728 | bytes 2097152 | tf_op jit(solution)/shard_map/pallas_call | solution.py:90
  2.9 0.5 %collective-permute-start.1 = (bf16[2048,128]{1,0:T(8,128)(2,1)}, bf16[2048,128]{1,0:T(8,128)(2,1)}, u32[]{:S(2)}, u32[]{:S(2)}) collective-permute-start(bf16[2048,128]{1,0:T(8,128)(2,1)} %bitcast.6.own_ref), channel_id=1, source_target_pairs={{0,4},{4,8},{8,12},{12,0},{1,5},{5,9},{9,13},{13,1},{2,6},{6,10},{... | collective-permute-start | bytes 1572872 | tf_op jit(solution)/shard_map/ppermute | solution.py:37
  3.5 2.6 %collective-permute-start = (bf16[4,128,128]{2,1,0:T(8,128)(2,1)S(1)}, bf16[4,128,128]{2,1,0:T(8,128)(2,1)S(1)}, u32[]{:S(2)}, u32[]{:S(2)}) collective-permute-start(bf16[4,128,128]{2,1,0:T(8,128)(2,1)S(1)} %get-tuple-element.16.mine_ref), channel_id=1, source_target_pairs={{0,4},{4,0},{8,12},{12,8},{1,5},{5,1},{9,13},{13,9},{2,6},{6,2},{1... | collective-permute-start | bytes 393224 | tf_op jit(solution)/shard_map/ppermute | solution.py:31
  6.1 0.0 copy-start
  6.1 1.0 %collective-permute-done.near_ref.refs_0_ = bf16[4,128,128]{2,1,0:T(8,128)(2,1)S(1)} collective-permute-done((bf16[4,128,128]{2,1,0:T(8,128)(2,1)S(1)}, bf16[4,128,128]{2,1,0:T(8,128)(2,1)S(1)}, u32[]{:S(2)}, u32[]{:S(2)}) %collective-permute-start) | collective-permute-done | bytes 131104 | tf_op jit(solution)/shard_map/ppermute | solution.py:31
  7.1 0.0 copy-done.1
  7.1 3.4 %shard_map.47 = (f32[1024,512]{1,0:T(8,128)S(1)}, bf16[4,128,128]{2,1,0:T(8,128)(2,1)S(1)}, bf16[1024,256]{1,0:T(8,128)(2,1)S(1)}, bf16[1024,256]{1,0:T(8,128)(2,1)S(1)}) custom-call(f32[4,16]{1,0:T(4,128)S(1)} %bitcast.13, bf16[3,1024,512]{2,1,0:T(8,128)(2,1)S(1)} %get-tuple-element.14.x_ref, bf16[2048,128]{1,0:T(8,128)(2,1)} %bitcast.6.own_ref, ...), custom_call_target="tpu_custom_call" | custom-call | flops 1073741824 | bytes 5242880 | tf_op jit(solution)/shard_map/pallas_call | solution.py:170
  10.5 0.9 %collective-permute-start.2 = (bf16[4,128,128]{2,1,0:T(8,128)(2,1)S(1)}, bf16[4,128,128]{2,1,0:T(8,128)(2,1)S(1)}, u32[]{:S(2)}, u32[]{:S(2)}) collective-permute-start(bf16[4,128,128]{2,1,0:T(8,128)(2,1)S(1)} %get-tuple-element.22), channel_id=1, source_target_pairs={{0,8},{4,12},{8,0},{12,4},{1,9},{5,13},{9,1},{13,5},{2,10},{6,14},... | collective-permute-start | bytes 393224 | tf_op jit(solution)/shard_map/ppermute | solution.py:31
  11.4 0.0 copy-done
  11.4 4.2 %shard_map.48 = (f32[4,1024,256]{2,1,0:T(8,128)S(1)}, f32[4,1024,128]{2,1,0:T(8,128)S(1)}) custom-call(bf16[1024,512]{1,0:T(8,128)(2,1)S(1)} %copy-done, bf16[1024,256]{1,0:T(8,128)(2,1)S(1)} %get-tuple-element.18.k_own, bf16[1024,256]{1,0:T(8,128)(2,1)S(1)} %get-tuple-element.19.v_own), custom_call_target="tpu_custom_call" | custom-call | flops 1610612736 | bytes 3145728 | tf_op jit(solution)/shard_map/pallas_call | solution.py:210
  15.6 0.7 %collective-permute-done.2.refs_1_ = bf16[4,128,128]{2,1,0:T(8,128)(2,1)S(1)} collective-permute-done((bf16[4,128,128]{2,1,0:T(8,128)(2,1)S(1)}, bf16[4,128,128]{2,1,0:T(8,128)(2,1)S(1)}, u32[]{:S(2)}, u32[]{:S(2)}) %collective-permute-start.2) | collective-permute-done | bytes 131104 | tf_op jit(solution)/shard_map/ppermute | solution.py:31
  16.3 0.0 collective-permute-done.1.before_ref
  16.3 7.5 %shard_map.49 = bf16[8192,128]{1,0:T(8,128)(2,1)} custom-call(s32[1]{0:T(128)} %bitcast.place_ref, f32[4,16]{1,0:T(4,128)S(1)} %bitcast.14, bf16[1024,512]{1,0:T(8,128)(2,1)S(1)} %copy-done, f32[1024,512]{1,0:T(8,128)S(1)} %get-tuple-element.17.lin_ref, bf16[3,1024,512]{2,1,0:T(8,128)(2,1)S(1)} %get-tuple-element.14.x_ref, ...), custom_call_target="tpu_custom_call" | custom-call | flops 2147483648 | bytes 7340032 | tf_op jit(solution)/shard_map/pallas_call | solution.py:307
Async XLA Ops:
  0.0 7.1 %copy-start.1 = (f32[16,4]{0,1:T(4,128)S(1)}, f32[16,4]{0,1:T(4,128)}, u32[]{:S(2)}) copy-start(f32[16,4]{0,1:T(4,128)} %param.5) | copy-start | bytes 772
  2.9 13.4 %collective-permute-start.1 = (bf16[2048,128]{1,0:T(8,128)(2,1)}, bf16[2048,128]{1,0:T(8,128)(2,1)}, u32[]{:S(2)}, u32[]{:S(2)}) collective-permute-start(bf16[2048,128]{1,0:T(8,128)(2,1)} %bitcast.6.own_ref), channel_id=1, source_target_pairs={{0,4},{4,8},{8,12},{12,0},{1,5},{5,9},{9,13},{13,1},{2,6},{6,10},{... | collective-permute-start | bytes 1572872 | tf_op jit(solution)/shard_map/ppermute | solution.py:37
  3.5 3.6 %collective-permute-start = (bf16[4,128,128]{2,1,0:T(8,128)(2,1)S(1)}, bf16[4,128,128]{2,1,0:T(8,128)(2,1)S(1)}, u32[]{:S(2)}, u32[]{:S(2)}) collective-permute-start(bf16[4,128,128]{2,1,0:T(8,128)(2,1)S(1)} %get-tuple-element.16.mine_ref), channel_id=1, source_target_pairs={{0,4},{4,0},{8,12},{12,8},{1,5},{5,1},{9,13},{13,9},{2,6},{6,2},{1... | collective-permute-start | bytes 393224 | tf_op jit(solution)/shard_map/ppermute | solution.py:31
  6.1 5.3 %copy-start = (bf16[1024,512]{1,0:T(8,128)(2,1)S(1)}, bf16[1024,512]{1,0:T(8,128)(2,1)}, u32[]{:S(2)}) copy-start(bf16[1024,512]{1,0:T(8,128)(2,1)} %q_ref.3) | copy-start | bytes 3145732
  10.5 5.8 %collective-permute-start.2 = (bf16[4,128,128]{2,1,0:T(8,128)(2,1)S(1)}, bf16[4,128,128]{2,1,0:T(8,128)(2,1)S(1)}, u32[]{:S(2)}, u32[]{:S(2)}) collective-permute-start(bf16[4,128,128]{2,1,0:T(8,128)(2,1)S(1)} %get-tuple-element.22), channel_id=1, source_target_pairs={{0,8},{4,12},{8,0},{12,4},{1,9},{5,13},{9,1},{13,5},{2,10},{6,14},... | collective-permute-start | bytes 393224 | tf_op jit(solution)/shard_map/ppermute | solution.py:31

commit v9 on v8

--- a/solution.py
+++ b/solution.py
@@ -60,10 +60,11 @@
     v_out[:, HD : 2 * HD] = jnp.ones((count, HD), BF16)
 
 
-def first_kernel(heads, index_ref, kv_hbm, x_hbm, own_ref, state_ref, x_ref, sums, sems):
+def first_kernel(heads, index_ref, kv_hbm, x_hbm, own_hbm, state_ref, x_ref, raw, sums, sems):
     half = x_ref.shape[1] // 2
     pieces = [pl.ds(0, half), pl.ds(half, half)]
-    pick = pltpu.make_async_copy(kv_hbm.at[:, index_ref[0]], own_ref, sems.at[2])
+    pick = pltpu.make_async_copy(kv_hbm.at[:, index_ref[0]], raw, sems.at[2])
+    hand_on = pltpu.make_async_copy(raw, own_hbm, sems.at[4])
     pick.start()
     loads = [
         pltpu.make_async_copy(x_hbm.at[pl.ds(1, 2), rows, :], x_ref.at[pl.ds(1, 2), rows, :], sems.at[i])
@@ -72,6 +73,8 @@
     loads.append(pltpu.make_async_copy(x_hbm.at[0], x_ref.at[0], sems.at[3]))
     for load in loads:
         load.start()
+    pick.wait()
+    hand_on.start()
     loads[0].wait()
     for h in range(heads):
         sums[h] = tn_dot(x_ref[1, pieces[0], lanes(h)], x_ref[2, pieces[0], lanes(h)])
@@ -79,8 +82,8 @@
     for h in range(heads):
         total = sums[h] + tn_dot(x_ref[1, pieces[1], lanes(h)], x_ref[2, pieces[1], lanes(h)])
         state_ref[h] = total.astype(BF16)
-    pick.wait()
     loads[2].wait()
+    hand_on.wait()
 
 
 def first_call(index, kv, planes):
@@ -90,15 +93,16 @@
     return pl.pallas_call(
         functools.partial(first_kernel, heads),
         in_specs=[SMEM, HBM, HBM],
-        out_specs=[VMEM] * 3,
+        out_specs=[ANY, VMEM, VMEM],
         out_shape=[
-            pltpu.VMEM((tok, two, hd), BF16),
+            jax.ShapeDtypeStruct((tok, two, hd), BF16),
             pltpu.VMEM((heads, HD, HD), BF16),
             pltpu.VMEM(planes.shape, BF16),
         ],
         scratch_shapes=[
+            pltpu.VMEM((tok, two, hd), BF16),
             pltpu.VMEM((heads, HD, HD), F32),
-            pltpu.SemaphoreType.DMA((4,)),
+            pltpu.SemaphoreType.DMA((5,)),
         ],
         compiler_params=PARAMS,
         cost_estimate=pl.CostEstimate(

time: 24 us -> 23.2 us (0.967)
  Pallas kernels: 18 us -> 17.3 us
    pallas_call x1, Pallas kernels: 2.93 us -> 2.19 us  [first_call(): pl.pallas_call(functools.partial(first_kernel, heads), in_specs=[SMEM, HB...]
  transfers between devices with their start and end apart: 3 -> 3, of which waited for: 2 -> 2; matrix products, arithmetic and copies ran while one was open for 0% -> 0% of each run, Pallas kernels for 32% -> 33%
where the time goes in v9:
time: 23.2 us; the launch traced here: 23 us
  Pallas kernels  17.3 us (75%)
  starting transfers between devices  4.04 us (17%)
  waiting for transfers between devices  1.67 us (7%)
    pallas_call x1, Pallas kernels, last_call(): pl.pallas_call(functools.partial(last_kernel, heads, block, len(states)),...  7.46 us
    pallas_call x1, Pallas kernels, own_call(): pl.pallas_call(functools.partial(own_kernel, heads, block), in_specs=[VME...  4.24 us
    ppermute x2, starting transfers between devices, partner_2(): return lax.ppermute(value, axis, pairs)  3.5 us
    pallas_call x1, Pallas kernels, linear_call(): pl.pallas_call(functools.partial(linear_kernel, heads), in_specs=[SMEM, V...  3.4 us
    pallas_call x1, Pallas kernels, first_call(): pl.pallas_call(functools.partial(first_kernel, heads), in_specs=[SMEM, HB...  2.19 us
    ppermute x2, waiting for transfers between devices, partner_2(): return lax.ppermute(value, axis, pairs)  1.66 us
    ppermute x1, starting transfers between devices, passed_along(): return lax.ppermute(x, axis, pairs)  0.54 us
  transfers between devices with their start and end apart: 3, of which 2 were waited for; matrix products, arithmetic and copies ran while one was open for 0% of the time, Pallas kernels for 33%

profile of v9, /device:TPU:0, one launch (start us, length us, event | category | flops | bytes accessed | tf_op | source)
XLA Modules:
  0.0 23.0 jit_solution(11486239257208519914)
XLA Ops:
  0.0 0.0 copy-start.1
  0.0 2.2 %shard_map.46 = (bf16[1024,2,128]{2,1,0:T(2,128)(2,1)}, bf16[4,128,128]{2,1,0:T(8,128)(2,1)S(1)}, bf16[3,1024,512]{2,1,0:T(8,128)(2,1)S(1)}) custom-call(s32[1]{0:T(128)} %bitcast.2.index_ref, bf16[1024,2,2,128]{3,2,1,0:T(2,128)(2,1)} %bitcast.16, bf16[3,1024,512]{2,1,0:T(8,128)(2,1)} %bitcast.15), custom_call_target="tpu_custom_call" | custom-call | flops 134217728 | bytes 2097152 | tf_op jit(solution)/shard_map/pallas_call | solution.py:93
  2.2 0.5 %collective-permute-start.1 = (bf16[2048,128]{1,0:T(8,128)(2,1)}, bf16[2048,128]{1,0:T(8,128)(2,1)}, u32[]{:S(2)}, u32[]{:S(2)}) collective-permute-start(bf16[2048,128]{1,0:T(8,128)(2,1)} %bitcast.6.own_ref), channel_id=1, source_target_pairs={{0,4},{4,8},{8,12},{12,0},{1,5},{5,9},{9,13},{13,1},{2,6},{6,10},{... | collective-permute-start | bytes 1572872 | tf_op jit(solution)/shard_map/ppermute | solution.py:37
  2.7 2.6 %collective-permute-start = (bf16[4,128,128]{2,1,0:T(8,128)(2,1)S(1)}, bf16[4,128,128]{2,1,0:T(8,128)(2,1)S(1)}, u32[]{:S(2)}, u32[]{:S(2)}) collective-permute-start(bf16[4,128,128]{2,1,0:T(8,128)(2,1)S(1)} %get-tuple-element.16.mine_ref), channel_id=1, source_target_pairs={{0,4},{4,0},{8,12},{12,8},{1,5},{5,1},{9,13},{13,9},{2,6},{6,2},{1... | collective-permute-start | bytes 393224 | tf_op jit(solution)/shard_map/ppermute | solution.py:31
  5.3 0.0 copy-start
  5.3 1.0 %collective-permute-done.near_ref.refs_0_ = bf16[4,128,128]{2,1,0:T(8,128)(2,1)S(1)} collective-permute-done((bf16[4,128,128]{2,1,0:T(8,128)(2,1)S(1)}, bf16[4,128,128]{2,1,0:T(8,128)(2,1)S(1)}, u32[]{:S(2)}, u32[]{:S(2)}) %collective-permute-start) | collective-permute-done | bytes 131104 | tf_op jit(solution)/shard_map/ppermute | solution.py:31
  6.3 0.0 copy-done.1
  6.3 3.4 %shard_map.47 = (f32[1024,512]{1,0:T(8,128)S(1)}, bf16[4,128,128]{2,1,0:T(8,128)(2,1)S(1)}, bf16[1024,256]{1,0:T(8,128)(2,1)S(1)}, bf16[1024,256]{1,0:T(8,128)(2,1)S(1)}) custom-call(f32[4,16]{1,0:T(4,128)S(1)} %bitcast.13, bf16[3,1024,512]{2,1,0:T(8,128)(2,1)S(1)} %get-tuple-element.14.x_ref, bf16[2048,128]{1,0:T(8,128)(2,1)} %bitcast.6.own_ref, ...), custom_call_target="tpu_custom_call" | custom-call | flops 1073741824 | bytes 5242880 | tf_op jit(solution)/shard_map/pallas_call | solution.py:174
  9.7 0.9 %collective-permute-start.2 = (bf16[4,128,128]{2,1,0:T(8,128)(2,1)S(1)}, bf16[4,128,128]{2,1,0:T(8,128)(2,1)S(1)}, u32[]{:S(2)}, u32[]{:S(2)}) collective-permute-start(bf16[4,128,128]{2,1,0:T(8,128)(2,1)S(1)} %get-tuple-element.22), channel_id=1, source_target_pairs={{0,8},{4,12},{8,0},{12,4},{1,9},{5,13},{9,1},{13,5},{2,10},{6,14},... | collective-permute-start | bytes 393224 | tf_op jit(solution)/shard_map/ppermute | solution.py:31
  10.6 0.0 copy-done
  10.6 4.2 %shard_map.48 = (f32[4,1024,256]{2,1,0:T(8,128)S(1)}, f32[4,1024,128]{2,1,0:T(8,128)S(1)}) custom-call(bf16[1024,512]{1,0:T(8,128)(2,1)S(1)} %copy-done, bf16[1024,256]{1,0:T(8,128)(2,1)S(1)} %get-tuple-element.18.k_own, bf16[1024,256]{1,0:T(8,128)(2,1)S(1)} %get-tuple-element.19.v_own), custom_call_target="tpu_custom_call" | custom-call | flops 1610612736 | bytes 3145728 | tf_op jit(solution)/shard_map/pallas_call | solution.py:214
  14.9 0.7 %collective-permute-done.2.refs_1_ = bf16[4,128,128]{2,1,0:T(8,128)(2,1)S(1)} collective-permute-done((bf16[4,128,128]{2,1,0:T(8,128)(2,1)S(1)}, bf16[4,128,128]{2,1,0:T(8,128)(2,1)S(1)}, u32[]{:S(2)}, u32[]{:S(2)}) %collective-permute-start.2) | collective-permute-done | bytes 131104 | tf_op jit(solution)/shard_map/ppermute | solution.py:31
  15.6 0.0 collective-permute-done.1.before_ref
  15.6 7.5 %shard_map.49 = bf16[8192,128]{1,0:T(8,128)(2,1)} custom-call(s32[1]{0:T(128)} %bitcast.place_ref, f32[4,16]{1,0:T(4,128)S(1)} %bitcast.14, bf16[1024,512]{1,0:T(8,128)(2,1)S(1)} %copy-done, f32[1024,512]{1,0:T(8,128)S(1)} %get-tuple-element.17.lin_ref, bf16[3,1024,512]{2,1,0:T(8,128)(2,1)S(1)} %get-tuple-element.14.x_ref, ...), custom_call_target="tpu_custom_call" | custom-call | flops 2147483648 | bytes 7340032 | tf_op jit(solution)/shard_map/pallas_call | solution.py:311
Async XLA Ops:
  0.0 6.3 %copy-start.1 = (f32[16,4]{0,1:T(4,128)S(1)}, f32[16,4]{0,1:T(4,128)}, u32[]{:S(2)}) copy-start(f32[16,4]{0,1:T(4,128)} %param.5) | copy-start | bytes 772
  2.2 13.4 %collective-permute-start.1 = (bf16[2048,128]{1,0:T(8,128)(2,1)}, bf16[2048,128]{1,0:T(8,128)(2,1)}, u32[]{:S(2)}, u32[]{:S(2)}) collective-permute-start(bf16[2048,128]{1,0:T(8,128)(2,1)} %bitcast.6.own_ref), channel_id=1, source_target_pairs={{0,4},{4,8},{8,12},{12,0},{1,5},{5,9},{9,13},{13,1},{2,6},{6,10},{... | collective-permute-start | bytes 1572872 | tf_op jit(solution)/shard_map/ppermute | solution.py:37
  2.7 3.6 %collective-permute-start = (bf16[4,128,128]{2,1,0:T(8,128)(2,1)S(1)}, bf16[4,128,128]{2,1,0:T(8,128)(2,1)S(1)}, u32[]{:S(2)}, u32[]{:S(2)}) collective-permute-start(bf16[4,128,128]{2,1,0:T(8,128)(2,1)S(1)} %get-tuple-element.16.mine_ref), channel_id=1, source_target_pairs={{0,4},{4,0},{8,12},{12,8},{1,5},{5,1},{9,13},{13,9},{2,6},{6,2},{1... | collective-permute-start | bytes 393224 | tf_op jit(solution)/shard_map/ppermute | solution.py:31
  5.3 5.3 %copy-start = (bf16[1024,512]{1,0:T(8,128)(2,1)S(1)}, bf16[1024,512]{1,0:T(8,128)(2,1)}, u32[]{:S(2)}) copy-start(bf16[1024,512]{1,0:T(8,128)(2,1)} %q_ref.3) | copy-start | bytes 3145732
  9.7 5.8 %collective-permute-start.2 = (bf16[4,128,128]{2,1,0:T(8,128)(2,1)S(1)}, bf16[4,128,128]{2,1,0:T(8,128)(2,1)S(1)}, u32[]{:S(2)}, u32[]{:S(2)}) collective-permute-start(bf16[4,128,128]{2,1,0:T(8,128)(2,1)S(1)} %get-tuple-element.22), channel_id=1, source_target_pairs={{0,8},{4,12},{8,0},{12,4},{1,9},{5,13},{9,1},{13,5},{2,10},{6,14},... | collective-permute-start | bytes 393224 | tf_op jit(solution)/shard_map/ppermute | solution.py:31

commit v10 on v9

--- a/solution.py
+++ b/solution.py
@@ -194,18 +194,20 @@
     row = lax.broadcasted_iota(jnp.int32, (block, block), 0)
     col = lax.broadcasted_iota(jnp.int32, (block, block), 1)
     mask = jnp.where(col <= row, 0.0, NEG).astype(F32)
-    for start in range(0, tok, block):
+    mask = jnp.concatenate([mask] * heads, axis=0)
+    for start in reversed(range(0, tok, block)):
         end = start + block
+        q = jnp.concatenate([q_ref[start:end, lanes(h)] for h in range(heads)], axis=0)
+        scores = nt_dot(jnp.concatenate([q, q], axis=1), k_own[:end, :])
+        edge = scores[:, start:] + mask
+        scores = jnp.concatenate([scores[:, :start], edge], axis=1) if start else edge
+        top = jnp.max(scores, axis=1, keepdims=True)
+        sums = jnp.dot(jnp.exp2(scores - top).astype(BF16), v_own[:end, :], preferred_element_type=F32)
+        top = jnp.broadcast_to(top, (heads * block, HD))
         for h in range(heads):
-            q = q_ref[start:end, lanes(h)]
-            scores = nt_dot(jnp.concatenate([q, q], axis=1), k_own[:end, :])
-            edge = scores[:, start:] + mask
-            scores = jnp.concatenate([scores[:, :start], edge], axis=1) if start else edge
-            top = jnp.max(scores, axis=1, keepdims=True)
-            sums_ref[h, start:end, :] = jnp.dot(
-                jnp.exp2(scores - top).astype(BF16), v_own[:end, :], preferred_element_type=F32
-            )
-            top_ref[h, start:end, :] = jnp.broadcast_to(top, (block, HD))
+            rows = slice(h * block, (h + 1) * block)
+            sums_ref[h, start:end, :] = sums[rows]
+            top_ref[h, start:end, :] = top[rows]
 
 
 def own_call(soft_q, k_own, v_own, block):

time: 23.2 us -> 23.2 us (level)
  waiting for transfers between devices: 1.67 us -> 2.58 us
  Pallas kernels: 17.3 us -> 16.4 us
    pallas_call x1, Pallas kernels: 4.24 us -> 3.33 us  [own_call(): pl.pallas_call(functools.partial(own_kernel, heads, block), in_specs=[VME...]
    ppermute x2, waiting for transfers between devices: 1.66 us -> 2.57 us  [partner_2(): return lax.ppermute(value, axis, pairs)]
  transfers between devices with their start and end apart: 3 -> 3, of which waited for: 2 -> 2; matrix products, arithmetic and copies ran while one was open for 0% -> 0% of each run, Pallas kernels for 33% -> 29%
where the time goes in v10:
time: 23.2 us; the launch traced here: 23 us
  Pallas kernels  16.4 us (71%)
  starting transfers between devices  4.04 us (17%)
  waiting for transfers between devices  2.58 us (11%)
    pallas_call x1, Pallas kernels, last_call(): pl.pallas_call(functools.partial(last_kernel, heads, block, len(states)),...  7.46 us
    ppermute x2, starting transfers between devices, partner_2(): return lax.ppermute(value, axis, pairs)  3.5 us
    pallas_call x1, Pallas kernels, linear_call(): pl.pallas_call(functools.partial(linear_kernel, heads), in_specs=[SMEM, V...  3.4 us
    pallas_call x1, Pallas kernels, own_call(): pl.pallas_call(functools.partial(own_kernel, heads, block), in_specs=[VME...  3.33 us
    ppermute x2, waiting for transfers between devices, partner_2(): return lax.ppermute(value, axis, pairs)  2.57 us
    pallas_call x1, Pallas kernels, first_call(): pl.pallas_call(functools.partial(first_kernel, heads), in_specs=[SMEM, HB...  2.19 us
    ppermute x1, starting transfers between devices, passed_along(): return lax.ppermute(x, axis, pairs)  0.54 us
  transfers between devices with their start and end apart: 3, of which 2 were waited for; matrix products, arithmetic and copies ran while one was open for 0% of the time, Pallas kernels for 29%

profile of v10, /device:TPU:0, one launch (start us, length us, event | category | flops | bytes accessed | tf_op | source)
XLA Modules:
  0.0 23.0 jit_solution(11565751409196061998)
XLA Ops:
  0.0 0.0 copy-start.1
  0.0 2.2 %shard_map.46 = (bf16[1024,2,128]{2,1,0:T(2,128)(2,1)}, bf16[4,128,128]{2,1,0:T(8,128)(2,1)S(1)}, bf16[3,1024,512]{2,1,0:T(8,128)(2,1)S(1)}) custom-call(s32[1]{0:T(128)} %bitcast.2.index_ref, bf16[1024,2,2,128]{3,2,1,0:T(2,128)(2,1)} %bitcast.16, bf16[3,1024,512]{2,1,0:T(8,128)(2,1)} %bitcast.15), custom_call_target="tpu_custom_call" | custom-call | flops 134217728 | bytes 2097152 | tf_op jit(solution)/shard_map/pallas_call | solution.py:93
  2.2 0.5 %collective-permute-start.1 = (bf16[2048,128]{1,0:T(8,128)(2,1)}, bf16[2048,128]{1,0:T(8,128)(2,1)}, u32[]{:S(2)}, u32[]{:S(2)}) collective-permute-start(bf16[2048,128]{1,0:T(8,128)(2,1)} %bitcast.6.own_ref), channel_id=1, source_target_pairs={{0,4},{4,8},{8,12},{12,0},{1,5},{5,9},{9,13},{13,1},{2,6},{6,10},{... | collective-permute-start | bytes 1572872 | tf_op jit(solution)/shard_map/ppermute | solution.py:37
  2.7 2.6 %collective-permute-start = (bf16[4,128,128]{2,1,0:T(8,128)(2,1)S(1)}, bf16[4,128,128]{2,1,0:T(8,128)(2,1)S(1)}, u32[]{:S(2)}, u32[]{:S(2)}) collective-permute-start(bf16[4,128,128]{2,1,0:T(8,128)(2,1)S(1)} %get-tuple-element.16.mine_ref), channel_id=1, source_target_pairs={{0,4},{4,0},{8,12},{12,8},{1,5},{5,1},{9,13},{13,9},{2,6},{6,2},{1... | collective-permute-start | bytes 393224 | tf_op jit(solution)/shard_map/ppermute | solution.py:31
  5.3 0.0 copy-start
  5.3 1.0 %collective-permute-done.near_ref.refs_0_ = bf16[4,128,128]{2,1,0:T(8,128)(2,1)S(1)} collective-permute-done((bf16[4,128,128]{2,1,0:T(8,128)(2,1)S(1)}, bf16[4,128,128]{2,1,0:T(8,128)(2,1)S(1)}, u32[]{:S(2)}, u32[]{:S(2)}) %collective-permute-start) | collective-permute-done | bytes 131104 | tf_op jit(solution)/shard_map/ppermute | solution.py:31
  6.3 0.0 copy-done.1
  6.3 3.4 %shard_map.47 = (f32[1024,512]{1,0:T(8,128)S(1)}, bf16[4,128,128]{2,1,0:T(8,128)(2,1)S(1)}, bf16[1024,256]{1,0:T(8,128)(2,1)S(1)}, bf16[1024,256]{1,0:T(8,128)(2,1)S(1)}) custom-call(f32[4,16]{1,0:T(4,128)S(1)} %bitcast.13, bf16[3,1024,512]{2,1,0:T(8,128)(2,1)S(1)} %get-tuple-element.14.x_ref, bf16[2048,128]{1,0:T(8,128)(2,1)} %bitcast.6.own_ref, ...), custom_call_target="tpu_custom_call" | custom-call | flops 1073741824 | bytes 5242880 | tf_op jit(solution)/shard_map/pallas_call | solution.py:174
  9.7 0.9 %collective-permute-start.2 = (bf16[4,128,128]{2,1,0:T(8,128)(2,1)S(1)}, bf16[4,128,128]{2,1,0:T(8,128)(2,1)S(1)}, u32[]{:S(2)}, u32[]{:S(2)}) collective-permute-start(bf16[4,128,128]{2,1,0:T(8,128)(2,1)S(1)} %get-tuple-element.22), channel_id=1, source_target_pairs={{0,8},{4,12},{8,0},{12,4},{1,9},{5,13},{9,1},{13,5},{2,10},{6,14},... | collective-permute-start | bytes 393224 | tf_op jit(solution)/shard_map/ppermute | solution.py:31
  10.6 0.0 copy-done
  10.6 3.3 %shard_map.48 = (f32[4,1024,256]{2,1,0:T(8,128)S(1)}, f32[4,1024,128]{2,1,0:T(8,128)S(1)}) custom-call(bf16[1024,512]{1,0:T(8,128)(2,1)S(1)} %copy-done, bf16[1024,256]{1,0:T(8,128)(2,1)S(1)} %get-tuple-element.18.k_own, bf16[1024,256]{1,0:T(8,128)(2,1)S(1)} %get-tuple-element.19.v_own), custom_call_target="tpu_custom_call" | custom-call | flops 1610612736 | bytes 3145728 | tf_op jit(solution)/shard_map/pallas_call | solution.py:216
  14.0 1.6 %collective-permute-done.2.refs_1_ = bf16[4,128,128]{2,1,0:T(8,128)(2,1)S(1)} collective-permute-done((bf16[4,128,128]{2,1,0:T(8,128)(2,1)S(1)}, bf16[4,128,128]{2,1,0:T(8,128)(2,1)S(1)}, u32[]{:S(2)}, u32[]{:S(2)}) %collective-permute-start.2) | collective-permute-done | bytes 131104 | tf_op jit(solution)/shard_map/ppermute | solution.py:31
  15.6 0.0 collective-permute-done.1.before_ref
  15.6 7.5 %shard_map.49 = bf16[8192,128]{1,0:T(8,128)(2,1)} custom-call(s32[1]{0:T(128)} %bitcast.place_ref, f32[4,16]{1,0:T(4,128)S(1)} %bitcast.14, bf16[1024,512]{1,0:T(8,128)(2,1)S(1)} %copy-done, f32[1024,512]{1,0:T(8,128)S(1)} %get-tuple-element.17.lin_ref, bf16[3,1024,512]{2,1,0:T(8,128)(2,1)S(1)} %get-tuple-element.14.x_ref, ...), custom_call_target="tpu_custom_call" | custom-call | flops 2147483648 | bytes 7340032 | tf_op jit(solution)/shard_map/pallas_call | solution.py:313
Async XLA Ops:
  0.0 6.3 %copy-start.1 = (f32[16,4]{0,1:T(4,128)S(1)}, f32[16,4]{0,1:T(4,128)}, u32[]{:S(2)}) copy-start(f32[16,4]{0,1:T(4,128)} %param.5) | copy-start | bytes 772
  2.2 13.4 %collective-permute-start.1 = (bf16[2048,128]{1,0:T(8,128)(2,1)}, bf16[2048,128]{1,0:T(8,128)(2,1)}, u32[]{:S(2)}, u32[]{:S(2)}) collective-permute-start(bf16[2048,128]{1,0:T(8,128)(2,1)} %bitcast.6.own_ref), channel_id=1, source_target_pairs={{0,4},{4,8},{8,12},{12,0},{1,5},{5,9},{9,13},{13,1},{2,6},{6,10},{... | collective-permute-start | bytes 1572872 | tf_op jit(solution)/shard_map/ppermute | solution.py:37
  2.7 3.6 %collective-permute-start = (bf16[4,128,128]{2,1,0:T(8,128)(2,1)S(1)}, bf16[4,128,128]{2,1,0:T(8,128)(2,1)S(1)}, u32[]{:S(2)}, u32[]{:S(2)}) collective-permute-start(bf16[4,128,128]{2,1,0:T(8,128)(2,1)S(1)} %get-tuple-element.16.mine_ref), channel_id=1, source_target_pairs={{0,4},{4,0},{8,12},{12,8},{1,5},{5,1},{9,13},{13,9},{2,6},{6,2},{1... | collective-permute-start | bytes 393224 | tf_op jit(solution)/shard_map/ppermute | solution.py:31
  5.3 5.3 %copy-start = (bf16[1024,512]{1,0:T(8,128)(2,1)S(1)}, bf16[1024,512]{1,0:T(8,128)(2,1)}, u32[]{:S(2)}) copy-start(bf16[1024,512]{1,0:T(8,128)(2,1)} %q_ref.3) | copy-start | bytes 3145732
  9.7 5.8 %collective-permute-start.2 = (bf16[4,128,128]{2,1,0:T(8,128)(2,1)S(1)}, bf16[4,128,128]{2,1,0:T(8,128)(2,1)S(1)}, u32[]{:S(2)}, u32[]{:S(2)}) collective-permute-start(bf16[4,128,128]{2,1,0:T(8,128)(2,1)S(1)} %get-tuple-element.22), channel_id=1, source_target_pairs={{0,8},{4,12},{8,0},{12,4},{1,9},{5,13},{9,1},{13,5},{2,10},{6,14},... | collective-permute-start | bytes 393224 | tf_op jit(solution)/shard_map/ppermute | solution.py:31

commit v11 on v10

--- a/solution.py
+++ b/solution.py
@@ -225,14 +225,37 @@
     )(soft_q, k_own, v_own)
 
 
+def unpack_kernel(before_ref, k_out, v_out, stage, raw, sem):
+    load = pltpu.make_async_copy(before_ref, raw, sem)
+    load.start()
+    load.wait()
+    take_apart(raw[...], stage, k_out, v_out)
+
+
+def unpack_call(before):
+    rows = before.shape[0]
+    keys = pltpu.VMEM((rows // 2, 2 * HD), BF16)
+    return pl.pallas_call(
+        unpack_kernel,
+        in_specs=[ANY],
+        out_specs=[VMEM] * 2,
+        out_shape=[keys, keys],
+        scratch_shapes=[
+            pltpu.VMEM((rows, HD), F32),
+            pltpu.VMEM((rows, HD), BF16),
+            pltpu.SemaphoreType.DMA(()),
+        ],
+        compiler_params=PARAMS,
+        cost_estimate=pl.CostEstimate(flops=0, bytes_accessed=8 * rows * HD, transcendentals=0),
+    )(before)
+
+
 def last_kernel(
-    heads, block, rounds, place_ref, table_ref, q_ref, lin_ref, x_ref, before_ref, sums_ref, top_ref, *refs
+    heads, block, rounds, place_ref, table_ref, q_ref, lin_ref, x_ref, k_before, v_before, sums_ref, top_ref, *refs
 ):
     state_refs = refs[:rounds]
-    out_hbm, mixed, packed, cross, k_before, v_before, stage, raw, in_sem, out_sems = refs[rounds:]
+    out_hbm, mixed, packed, cross, out_sems = refs[rounds:]
     tok = q_ref.shape[0]
-    load = pltpu.make_async_copy(before_ref, raw, in_sem)
-    load.start()
     place = place_ref[0]
     first = place == 0
     stride = 2 * heads
@@ -260,11 +283,6 @@
                 at = start * stride + 2 * (pair * together + i)
                 mixed[pl.ds(at, block, stride=stride), :] = norm
 
-    for start in range(0, tok // 2, block):
-        linear_rows(start)
-
-    load.wait()
-    take_apart(raw[...], stage, k_before, v_before)
     row = lax.broadcasted_iota(jnp.int32, (block, block), 0)
     col = lax.broadcasted_iota(jnp.int32, (block, block), 1)
     mask = jnp.where(col >= row, 0.0, NEG).astype(F32)
@@ -279,8 +297,7 @@
         copy_out(start).start()
 
     def attend(start):
-        if start >= tok // 2:
-            linear_rows(start)
+        linear_rows(start)
         for h in range(heads):
             q = q_ref[start : start + block, lanes(h)]
             scores = nt_dot(jnp.concatenate([q, q], axis=1), k_before[start:, :])
@@ -307,30 +324,25 @@
         copy_out(start).wait()
 
 
-def last_call(place, table, soft_q, partial, planes, before, sums, top, states, block):
+def last_call(place, table, soft_q, partial, planes, earlier, sums, top, states, block):
     tok, width = soft_q.shape
     heads = width // HD
     return pl.pallas_call(
         functools.partial(last_kernel, heads, block, len(states)),
-        in_specs=[SMEM, SMEM, VMEM, VMEM, VMEM, ANY, VMEM, VMEM] + [VMEM] * len(states),
+        in_specs=[SMEM, SMEM] + [VMEM] * (7 + len(states)),
         out_specs=ANY,
         out_shape=jax.ShapeDtypeStruct((tok * 2 * heads, HD), BF16),
         scratch_shapes=[
             pltpu.VMEM((tok * 2 * heads, HD), F32),
             pltpu.VMEM((tok * 2 * heads, HD), BF16),
             pltpu.VMEM((heads // 2, 2 * HD, 2 * HD) if heads % 2 == 0 else (heads, HD, HD), BF16),
-            pltpu.VMEM((tok, 2 * HD), BF16),
-            pltpu.VMEM((tok, 2 * HD), BF16),
-            pltpu.VMEM((2 * tok, HD), F32),
-            pltpu.VMEM((2 * tok, HD), BF16),
-            pltpu.SemaphoreType.DMA(()),
             pltpu.SemaphoreType.DMA((tok // block,)),
         ],
         compiler_params=PARAMS,
         cost_estimate=pl.CostEstimate(
             flops=4 * tok * tok * width, bytes_accessed=14 * tok * width, transcendentals=tok * tok * heads // 2
         ),
-    )(place, table, soft_q, partial, planes, before, sums, top, *states)
+    )(place, table, soft_q, partial, planes, *earlier, sums, top, *states)
 
 
 def local(lin_qkv, level_weights, soft_q, soft_kv):
@@ -356,7 +368,8 @@
             group_sum = (group_sum.astype(F32) + states[-1].astype(F32)).astype(BF16)
         states.append(partner_2(group_sum, "seq", bit))
     sums, top = own_call(soft_q, *own, block)
-    out = last_call(place, table, soft_q, partial, planes, before, sums, top, states, block)
+    earlier = unpack_call(before)
+    out = last_call(place, table, soft_q, partial, planes, earlier, sums, top, states, block)
     out = out.reshape(tok, q_heads, 2, HD).transpose(0, 2, 1, 3)
     return out.reshape(tok, 2, q_heads * HD)
 

time: 23.2 us -> 22.4 us (0.966)
  waiting for transfers between devices: 2.58 us -> 1.32 us
  Pallas kernels: 16.4 us -> 16.8 us
    pallas_call x0 -> x1, Pallas kernels: none -> 1.37 us  [unpack_call(): pl.pallas_call(unpack_kernel, in_specs=[ANY], out_specs=[VMEM] * 2, out_s...]
    ppermute x2, waiting for transfers between devices: 2.57 us -> 1.32 us  [partner_2(): return lax.ppermute(value, axis, pairs)]
    pallas_call x1, Pallas kernels: 7.46 us -> 6.66 us  [last_call(): pl.pallas_call(functools.partial(last_kernel, heads, block, len(states)),...]
  transfers between devices with their start and end apart: 3 -> 3, of which waited for: 2 -> 2; matrix products, arithmetic and copies ran while one was open for 0% -> 0% of each run, Pallas kernels for 29% -> 36%
where the time goes in v11:
time: 22.4 us; the launch traced here: 22.2 us
  Pallas kernels  16.8 us (75%)
  starting transfers between devices  4.04 us (18%)
  waiting for transfers between devices  1.32 us (6%)
    pallas_call x1, Pallas kernels, last_call(): pl.pallas_call(functools.partial(last_kernel, heads, block, len(states)),...  6.66 us
    ppermute x2, starting transfers between devices, partner_2(): return lax.ppermute(value, axis, pairs)  3.5 us
    pallas_call x1, Pallas kernels, linear_call(): pl.pallas_call(functools.partial(linear_kernel, heads), in_specs=[SMEM, V...  3.4 us
    pallas_call x1, Pallas kernels, own_call(): pl.pallas_call(functools.partial(own_kernel, heads, block), in_specs=[VME...  3.2 us
    pallas_call x1, Pallas kernels, first_call(): pl.pallas_call(functools.partial(first_kernel, heads), in_specs=[SMEM, HB...  2.19 us
    pallas_call x1, Pallas kernels, unpack_call(): pl.pallas_call(unpack_kernel, in_specs=[ANY], out_specs=[VMEM] * 2, out_s...  1.37 us
    ppermute x2, waiting for transfers between devices, partner_2(): return lax.ppermute(value, axis, pairs)  1.32 us
    ppermute x1, starting transfers between devices, passed_along(): return lax.ppermute(x, axis, pairs)  0.54 us
  transfers between devices with their start and end apart: 3, of which 2 were waited for; matrix products, arithmetic and copies ran while one was open for 0% of the time, Pallas kernels for 36%

profile of v11, /device:TPU:0, one launch (start us, length us, event | category | flops | bytes accessed | tf_op | source)
XLA Modules:
  0.0 22.2 jit_solution(7057122910123149506)
XLA Ops:
  0.0 0.0 copy-start.1
  0.0 2.2 %shard_map.46 = (bf16[1024,2,128]{2,1,0:T(2,128)(2,1)}, bf16[4,128,128]{2,1,0:T(8,128)(2,1)S(1)}, bf16[3,1024,512]{2,1,0:T(8,128)(2,1)S(1)}) custom-call(s32[1]{0:T(128)} %bitcast.2.index_ref, bf16[1024,2,2,128]{3,2,1,0:T(2,128)(2,1)} %bitcast.16, bf16[3,1024,512]{2,1,0:T(8,128)(2,1)} %bitcast.15), custom_call_target="tpu_custom_call" | custom-call | flops 134217728 | bytes 2097152 | tf_op jit(solution)/shard_map/pallas_call | solution.py:93
  2.2 0.5 %collective-permute-start.1 = (bf16[2048,128]{1,0:T(8,128)(2,1)}, bf16[2048,128]{1,0:T(8,128)(2,1)}, u32[]{:S(2)}, u32[]{:S(2)}) collective-permute-start(bf16[2048,128]{1,0:T(8,128)(2,1)} %bitcast.6.own_ref), channel_id=1, source_target_pairs={{0,4},{4,8},{8,12},{12,0},{1,5},{5,9},{9,13},{13,1},{2,6},{6,10},{... | collective-permute-start | bytes 1572872 | tf_op jit(solution)/shard_map/ppermute | solution.py:37
  2.7 2.6 %collective-permute-start = (bf16[4,128,128]{2,1,0:T(8,128)(2,1)S(1)}, bf16[4,128,128]{2,1,0:T(8,128)(2,1)S(1)}, u32[]{:S(2)}, u32[]{:S(2)}) collective-permute-start(bf16[4,128,128]{2,1,0:T(8,128)(2,1)S(1)} %get-tuple-element.18.mine_ref), channel_id=1, source_target_pairs={{0,4},{4,0},{8,12},{12,8},{1,5},{5,1},{9,13},{13,9},{2,6},{6,2},{1... | collective-permute-start | bytes 393224 | tf_op jit(solution)/shard_map/ppermute | solution.py:31
  5.3 0.0 copy-start
  5.3 1.0 %collective-permute-done.near_ref.refs_0_ = bf16[4,128,128]{2,1,0:T(8,128)(2,1)S(1)} collective-permute-done((bf16[4,128,128]{2,1,0:T(8,128)(2,1)S(1)}, bf16[4,128,128]{2,1,0:T(8,128)(2,1)S(1)}, u32[]{:S(2)}, u32[]{:S(2)}) %collective-permute-start) | collective-permute-done | bytes 131104 | tf_op jit(solution)/shard_map/ppermute | solution.py:31
  6.3 0.0 copy-done.1
  6.3 3.4 %shard_map.47 = (f32[1024,512]{1,0:T(8,128)S(1)}, bf16[4,128,128]{2,1,0:T(8,128)(2,1)S(1)}, bf16[1024,256]{1,0:T(8,128)(2,1)S(1)}, bf16[1024,256]{1,0:T(8,128)(2,1)S(1)}) custom-call(f32[4,16]{1,0:T(4,128)S(1)} %bitcast.13, bf16[3,1024,512]{2,1,0:T(8,128)(2,1)S(1)} %get-tuple-element.16.x_ref, bf16[2048,128]{1,0:T(8,128)(2,1)} %bitcast.6.own_ref, ...), custom_call_target="tpu_custom_call" | custom-call | flops 1073741824 | bytes 5242880 | tf_op jit(solution)/shard_map/pallas_call | solution.py:174
  9.7 0.9 %collective-permute-start.2 = (bf16[4,128,128]{2,1,0:T(8,128)(2,1)S(1)}, bf16[4,128,128]{2,1,0:T(8,128)(2,1)S(1)}, u32[]{:S(2)}, u32[]{:S(2)}) collective-permute-start(bf16[4,128,128]{2,1,0:T(8,128)(2,1)S(1)} %get-tuple-element.26), channel_id=1, source_target_pairs={{0,8},{4,12},{8,0},{12,4},{1,9},{5,13},{9,1},{13,5},{2,10},{6,14},... | collective-permute-start | bytes 393224 | tf_op jit(solution)/shard_map/ppermute | solution.py:31
  10.6 0.0 copy-done
  10.6 3.2 %shard_map.49 = (f32[4,1024,256]{2,1,0:T(8,128)S(1)}, f32[4,1024,128]{2,1,0:T(8,128)S(1)}) custom-call(bf16[1024,512]{1,0:T(8,128)(2,1)S(1)} %copy-done, bf16[1024,256]{1,0:T(8,128)(2,1)S(1)} %get-tuple-element.22.k_own, bf16[1024,256]{1,0:T(8,128)(2,1)S(1)} %get-tuple-element.23.v_own), custom_call_target="tpu_custom_call" | custom-call | flops 1610612736 | bytes 3145728 | tf_op jit(solution)/shard_map/pallas_call | solution.py:216
  13.8 0.0 collective-permute-done.1.before_ref
  13.8 1.4 %shard_map.48 = (bf16[1024,256]{1,0:T(8,128)(2,1)S(1)}, bf16[1024,256]{1,0:T(8,128)(2,1)S(1)}) custom-call(bf16[2048,128]{1,0:T(8,128)(2,1)} %collective-permute-done.1.before_ref), custom_call_target="tpu_custom_call" | custom-call | bytes 2097152 | tf_op jit(solution)/shard_map/pallas_call | solution.py:238
  15.2 0.3 %collective-permute-done.2.refs_1_ = bf16[4,128,128]{2,1,0:T(8,128)(2,1)S(1)} collective-permute-done((bf16[4,128,128]{2,1,0:T(8,128)(2,1)S(1)}, bf16[4,128,128]{2,1,0:T(8,128)(2,1)S(1)}, u32[]{:S(2)}, u32[]{:S(2)}) %collective-permute-start.2) | collective-permute-done | bytes 131104 | tf_op jit(solution)/shard_map/ppermute | solution.py:31
  15.6 6.7 %shard_map.50 = bf16[8192,128]{1,0:T(8,128)(2,1)} custom-call(s32[1]{0:T(128)} %bitcast.place_ref, f32[4,16]{1,0:T(4,128)S(1)} %bitcast.14, bf16[1024,512]{1,0:T(8,128)(2,1)S(1)} %copy-done, f32[1024,512]{1,0:T(8,128)S(1)} %get-tuple-element.19.lin_ref, bf16[3,1024,512]{2,1,0:T(8,128)(2,1)S(1)} %get-tuple-element.16.x_ref, ...), custom_call_target="tpu_custom_call" | custom-call | flops 2147483648 | bytes 7340032 | tf_op jit(solution)/shard_map/pallas_call | solution.py:330
Async XLA Ops:
  0.0 6.3 %copy-start.1 = (f32[16,4]{0,1:T(4,128)S(1)}, f32[16,4]{0,1:T(4,128)}, u32[]{:S(2)}) copy-start(f32[16,4]{0,1:T(4,128)} %param.5) | copy-start | bytes 772
  2.2 11.6 %collective-permute-start.1 = (bf16[2048,128]{1,0:T(8,128)(2,1)}, bf16[2048,128]{1,0:T(8,128)(2,1)}, u32[]{:S(2)}, u32[]{:S(2)}) collective-permute-start(bf16[2048,128]{1,0:T(8,128)(2,1)} %bitcast.6.own_ref), channel_id=1, source_target_pairs={{0,4},{4,8},{8,12},{12,0},{1,5},{5,9},{9,13},{13,1},{2,6},{6,10},{... | collective-permute-start | bytes 1572872 | tf_op jit(solution)/shard_map/ppermute | solution.py:37
  2.7 3.6 %collective-permute-start = (bf16[4,128,128]{2,1,0:T(8,128)(2,1)S(1)}, bf16[4,128,128]{2,1,0:T(8,128)(2,1)S(1)}, u32[]{:S(2)}, u32[]{:S(2)}) collective-permute-start(bf16[4,128,128]{2,1,0:T(8,128)(2,1)S(1)} %get-tuple-element.18.mine_ref), channel_id=1, source_target_pairs={{0,4},{4,0},{8,12},{12,8},{1,5},{5,1},{9,13},{13,9},{2,6},{6,2},{1... | collective-permute-start | bytes 393224 | tf_op jit(solution)/shard_map/ppermute | solution.py:31
  5.3 5.3 %copy-start = (bf16[1024,512]{1,0:T(8,128)(2,1)S(1)}, bf16[1024,512]{1,0:T(8,128)(2,1)}, u32[]{:S(2)}) copy-start(bf16[1024,512]{1,0:T(8,128)(2,1)} %q_ref.3) | copy-start | bytes 3145732
  9.7 5.8 %collective-permute-start.2 = (bf16[4,128,128]{2,1,0:T(8,128)(2,1)S(1)}, bf16[4,128,128]{2,1,0:T(8,128)(2,1)S(1)}, u32[]{:S(2)}, u32[]{:S(2)}) collective-permute-start(bf16[4,128,128]{2,1,0:T(8,128)(2,1)S(1)} %get-tuple-element.26), channel_id=1, source_target_pairs={{0,8},{4,12},{8,0},{12,4},{1,9},{5,13},{9,1},{13,5},{2,10},{6,14},... | collective-permute-start | bytes 393224 | tf_op jit(solution)/shard_map/ppermute | solution.py:31

commit v12 on v11

--- a/solution.py
+++ b/solution.py
@@ -61,28 +61,31 @@
 
 
 def first_kernel(heads, index_ref, kv_hbm, x_hbm, own_hbm, state_ref, x_ref, raw, sums, sems):
-    half = x_ref.shape[1] // 2
-    pieces = [pl.ds(0, half), pl.ds(half, half)]
-    pick = pltpu.make_async_copy(kv_hbm.at[:, index_ref[0]], raw, sems.at[2])
-    hand_on = pltpu.make_async_copy(raw, own_hbm, sems.at[4])
+    count = 4
+    step = x_ref.shape[1] // count
+    pieces = [pl.ds(i * step, step) for i in range(count)]
+    pick = pltpu.make_async_copy(kv_hbm.at[:, index_ref[0]], raw, sems.at[count])
+    hand_on = pltpu.make_async_copy(raw, own_hbm, sems.at[count + 1])
     pick.start()
     loads = [
         pltpu.make_async_copy(x_hbm.at[pl.ds(1, 2), rows, :], x_ref.at[pl.ds(1, 2), rows, :], sems.at[i])
         for i, rows in enumerate(pieces)
     ]
-    loads.append(pltpu.make_async_copy(x_hbm.at[0], x_ref.at[0], sems.at[3]))
+    loads.append(pltpu.make_async_copy(x_hbm.at[0], x_ref.at[0], sems.at[count + 2]))
     for load in loads:
         load.start()
     pick.wait()
     hand_on.start()
-    loads[0].wait()
-    for h in range(heads):
-        sums[h] = tn_dot(x_ref[1, pieces[0], lanes(h)], x_ref[2, pieces[0], lanes(h)])
-    loads[1].wait()
-    for h in range(heads):
-        total = sums[h] + tn_dot(x_ref[1, pieces[1], lanes(h)], x_ref[2, pieces[1], lanes(h)])
-        state_ref[h] = total.astype(BF16)
-    loads[2].wait()
+    for i, rows in enumerate(pieces):
+        loads[i].wait()
+        for h in range(heads):
+            total = tn_dot(x_ref[1, rows, lanes(h)], x_ref[2, rows, lanes(h)])
+            total = total if i == 0 else sums[h] + total
+            if i < count - 1:
+                sums[h] = total
+            else:
+                state_ref[h] = total.astype(BF16)
+    loads[count].wait()
     hand_on.wait()
 
 
@@ -102,7 +105,7 @@
         scratch_shapes=[
             pltpu.VMEM((tok, two, hd), BF16),
             pltpu.VMEM((heads, HD, HD), F32),
-            pltpu.SemaphoreType.DMA((5,)),
+            pltpu.SemaphoreType.DMA((7,)),
         ],
         compiler_params=PARAMS,
         cost_estimate=pl.CostEstimate(
@@ -297,27 +300,33 @@
         copy_out(start).start()
 
     def attend(start):
-        linear_rows(start)
-        for h in range(heads):
-            q = q_ref[start : start + block, lanes(h)]
+        for pair in range(pairs):
+            group = range(pair * together, (pair + 1) * together)
+            here = slice(start, start + block)
+            q = jnp.concatenate([q_ref[here, lanes(h)] for h in group], axis=0)
             scores = nt_dot(jnp.concatenate([q, q], axis=1), k_before[start:, :])
-            edge = scores[:, :block] + mask
+            edge = scores[:, :block] + jnp.concatenate([mask] * len(group), axis=0)
             scores = jnp.concatenate([edge, scores[:, block:]], axis=1) if start + block < tok else edge
             top = jnp.max(scores, axis=1, keepdims=True)
-            top_own = top_ref[h, start : start + block, :]
+            top_own = jnp.concatenate([top_ref[h, here, :] for h in group], axis=0)
             both = jnp.where(first, top_own, jnp.maximum(top, top_own))
             off = jnp.where(first, FAR, both)
             probs = jnp.exp2(scores - jnp.concatenate([off] * (scores.shape[1] // HD), axis=1)).astype(BF16)
             sums = jnp.dot(probs, v_before[start:, :], preferred_element_type=F32)
             factor = jnp.exp2(top_own - both)
-            sums = sums + sums_ref[h, start : start + block, :] * jnp.concatenate([factor, factor], axis=1)
-            mixed[pl.ds(start * stride + 2 * h + 1, block, stride=stride), :] = sums[:, :HD] / sums[:, HD:]
+            own = jnp.concatenate([sums_ref[h, here, :] for h in group], axis=0)
+            sums = sums + own * jnp.concatenate([factor, factor], axis=1)
+            out = sums[:, :HD] / sums[:, HD:]
+            for i, h in enumerate(group):
+                at = start * stride + 2 * h + 1
+                mixed[pl.ds(at, block, stride=stride), :] = out[i * block : (i + 1) * block]
 
     for start in range(0, tok, block):
 
         if start:
             send(start - block)
         attend(start)
+        linear_rows(start)
 
     send(tok - block)
     for start in range(0, tok, block):

time: 22.4 us -> 22.6 us (level)
  no operation moved by 1% of the time
where the time goes in v12:
time: 22.6 us; the launch traced here: 22.4 us
  Pallas kernels  17 us (75%)
  starting transfers between devices  4.04 us (18%)
  waiting for transfers between devices  1.32 us (6%)
    pallas_call x1, Pallas kernels, last_call(): pl.pallas_call(functools.partial(last_kernel, heads, block, len(states)),...  6.63 us
    ppermute x2, starting transfers between devices, partner_2(): return lax.ppermute(value, axis, pairs)  3.5 us
    pallas_call x1, Pallas kernels, linear_call(): pl.pallas_call(functools.partial(linear_kernel, heads), in_specs=[SMEM, V...  3.4 us
    pallas_call x1, Pallas kernels, own_call(): pl.pallas_call(functools.partial(own_kernel, heads, block), in_specs=[VME...  3.2 us
    pallas_call x1, Pallas kernels, first_call(): pl.pallas_call(functools.partial(first_kernel, heads), in_specs=[SMEM, HB...  2.37 us
    pallas_call x1, Pallas kernels, unpack_call(): pl.pallas_call(unpack_kernel, in_specs=[ANY], out_specs=[VMEM] * 2, out_s...  1.37 us
    ppermute x2, waiting for transfers between devices, partner_2(): return lax.ppermute(value, axis, pairs)  1.32 us
    ppermute x1, starting transfers between devices, passed_along(): return lax.ppermute(x, axis, pairs)  0.54 us
  transfers between devices with their start and end apart: 3, of which 2 were waited for; matrix products, arithmetic and copies ran while one was open for 0% of the time, Pallas kernels for 36%

profile of v12, /device:TPU:0, one launch (start us, length us, event | category | flops | bytes accessed | tf_op | source)
XLA Modules:
  0.0 22.4 jit_solution(8224627915377161416)
XLA Ops:
  0.0 0.0 copy-start.1
  0.0 2.4 %shard_map.46 = (bf16[1024,2,128]{2,1,0:T(2,128)(2,1)}, bf16[4,128,128]{2,1,0:T(8,128)(2,1)S(1)}, bf16[3,1024,512]{2,1,0:T(8,128)(2,1)S(1)}) custom-call(s32[1]{0:T(128)} %bitcast.2.index_ref, bf16[1024,2,2,128]{3,2,1,0:T(2,128)(2,1)} %bitcast.16, bf16[3,1024,512]{2,1,0:T(8,128)(2,1)} %bitcast.15), custom_call_target="tpu_custom_call" | custom-call | flops 134217728 | bytes 2097152 | tf_op jit(solution)/shard_map/pallas_call | solution.py:96
  2.4 0.5 %collective-permute-start.1 = (bf16[2048,128]{1,0:T(8,128)(2,1)}, bf16[2048,128]{1,0:T(8,128)(2,1)}, u32[]{:S(2)}, u32[]{:S(2)}) collective-permute-start(bf16[2048,128]{1,0:T(8,128)(2,1)} %bitcast.6.own_ref), channel_id=1, source_target_pairs={{0,4},{4,8},{8,12},{12,0},{1,5},{5,9},{9,13},{13,1},{2,6},{6,10},{... | collective-permute-start | bytes 1572872 | tf_op jit(solution)/shard_map/ppermute | solution.py:37
  2.9 2.6 %collective-permute-start = (bf16[4,128,128]{2,1,0:T(8,128)(2,1)S(1)}, bf16[4,128,128]{2,1,0:T(8,128)(2,1)S(1)}, u32[]{:S(2)}, u32[]{:S(2)}) collective-permute-start(bf16[4,128,128]{2,1,0:T(8,128)(2,1)S(1)} %get-tuple-element.18.mine_ref), channel_id=1, source_target_pairs={{0,4},{4,0},{8,12},{12,8},{1,5},{5,1},{9,13},{13,9},{2,6},{6,2},{1... | collective-permute-start | bytes 393224 | tf_op jit(solution)/shard_map/ppermute | solution.py:31
  5.5 0.0 copy-start
  5.5 1.0 %collective-permute-done.near_ref.refs_0_ = bf16[4,128,128]{2,1,0:T(8,128)(2,1)S(1)} collective-permute-done((bf16[4,128,128]{2,1,0:T(8,128)(2,1)S(1)}, bf16[4,128,128]{2,1,0:T(8,128)(2,1)S(1)}, u32[]{:S(2)}, u32[]{:S(2)}) %collective-permute-start) | collective-permute-done | bytes 131104 | tf_op jit(solution)/shard_map/ppermute | solution.py:31
  6.5 0.0 copy-done.1
  6.5 3.4 %shard_map.47 = (f32[1024,512]{1,0:T(8,128)S(1)}, bf16[4,128,128]{2,1,0:T(8,128)(2,1)S(1)}, bf16[1024,256]{1,0:T(8,128)(2,1)S(1)}, bf16[1024,256]{1,0:T(8,128)(2,1)S(1)}) custom-call(f32[4,16]{1,0:T(4,128)S(1)} %bitcast.13, bf16[3,1024,512]{2,1,0:T(8,128)(2,1)S(1)} %get-tuple-element.16.x_ref, bf16[2048,128]{1,0:T(8,128)(2,1)} %bitcast.6.own_ref, ...), custom_call_target="tpu_custom_call" | custom-call | flops 1073741824 | bytes 5242880 | tf_op jit(solution)/shard_map/pallas_call | solution.py:177
  9.9 0.9 %collective-permute-start.2 = (bf16[4,128,128]{2,1,0:T(8,128)(2,1)S(1)}, bf16[4,128,128]{2,1,0:T(8,128)(2,1)S(1)}, u32[]{:S(2)}, u32[]{:S(2)}) collective-permute-start(bf16[4,128,128]{2,1,0:T(8,128)(2,1)S(1)} %get-tuple-element.26), channel_id=1, source_target_pairs={{0,8},{4,12},{8,0},{12,4},{1,9},{5,13},{9,1},{13,5},{2,10},{6,14},... | collective-permute-start | bytes 393224 | tf_op jit(solution)/shard_map/ppermute | solution.py:31
  10.8 0.0 copy-done
  10.8 3.2 %shard_map.49 = (f32[4,1024,256]{2,1,0:T(8,128)S(1)}, f32[4,1024,128]{2,1,0:T(8,128)S(1)}) custom-call(bf16[1024,512]{1,0:T(8,128)(2,1)S(1)} %copy-done, bf16[1024,256]{1,0:T(8,128)(2,1)S(1)} %get-tuple-element.22.k_own, bf16[1024,256]{1,0:T(8,128)(2,1)S(1)} %get-tuple-element.23.v_own), custom_call_target="tpu_custom_call" | custom-call | flops 1610612736 | bytes 3145728 | tf_op jit(solution)/shard_map/pallas_call | solution.py:219
  14.0 0.0 collective-permute-done.1.before_ref
  14.0 1.4 %shard_map.48 = (bf16[1024,256]{1,0:T(8,128)(2,1)S(1)}, bf16[1024,256]{1,0:T(8,128)(2,1)S(1)}) custom-call(bf16[2048,128]{1,0:T(8,128)(2,1)} %collective-permute-done.1.before_ref), custom_call_target="tpu_custom_call" | custom-call | bytes 2097152 | tf_op jit(solution)/shard_map/pallas_call | solution.py:241
  15.4 0.3 %collective-permute-done.2.refs_1_ = bf16[4,128,128]{2,1,0:T(8,128)(2,1)S(1)} collective-permute-done((bf16[4,128,128]{2,1,0:T(8,128)(2,1)S(1)}, bf16[4,128,128]{2,1,0:T(8,128)(2,1)S(1)}, u32[]{:S(2)}, u32[]{:S(2)}) %collective-permute-start.2) | collective-permute-done | bytes 131104 | tf_op jit(solution)/shard_map/ppermute | solution.py:31
  15.7 6.6 %shard_map.50 = bf16[8192,128]{1,0:T(8,128)(2,1)} custom-call(s32[1]{0:T(128)} %bitcast.place_ref, f32[4,16]{1,0:T(4,128)S(1)} %bitcast.14, bf16[1024,512]{1,0:T(8,128)(2,1)S(1)} %copy-done, f32[1024,512]{1,0:T(8,128)S(1)} %get-tuple-element.19.lin_ref, bf16[3,1024,512]{2,1,0:T(8,128)(2,1)S(1)} %get-tuple-element.16.x_ref, ...), custom_call_target="tpu_custom_call" | custom-call | flops 2147483648 | bytes 7340032 | tf_op jit(solution)/shard_map/pallas_call | solution.py:339
Async XLA Ops:
  0.0 6.5 %copy-start.1 = (f32[16,4]{0,1:T(4,128)S(1)}, f32[16,4]{0,1:T(4,128)}, u32[]{:S(2)}) copy-start(f32[16,4]{0,1:T(4,128)} %param.5) | copy-start | bytes 772
  2.4 11.6 %collective-permute-start.1 = (bf16[2048,128]{1,0:T(8,128)(2,1)}, bf16[2048,128]{1,0:T(8,128)(2,1)}, u32[]{:S(2)}, u32[]{:S(2)}) collective-permute-start(bf16[2048,128]{1,0:T(8,128)(2,1)} %bitcast.6.own_ref), channel_id=1, source_target_pairs={{0,4},{4,8},{8,12},{12,0},{1,5},{5,9},{9,13},{13,1},{2,6},{6,10},{... | collective-permute-start | bytes 1572872 | tf_op jit(solution)/shard_map/ppermute | solution.py:37
  2.9 3.6 %collective-permute-start = (bf16[4,128,128]{2,1,0:T(8,128)(2,1)S(1)}, bf16[4,128,128]{2,1,0:T(8,128)(2,1)S(1)}, u32[]{:S(2)}, u32[]{:S(2)}) collective-permute-start(bf16[4,128,128]{2,1,0:T(8,128)(2,1)S(1)} %get-tuple-element.18.mine_ref), channel_id=1, source_target_pairs={{0,4},{4,0},{8,12},{12,8},{1,5},{5,1},{9,13},{13,9},{2,6},{6,2},{1... | collective-permute-start | bytes 393224 | tf_op jit(solution)/shard_map/ppermute | solution.py:31
  5.5 5.3 %copy-start = (bf16[1024,512]{1,0:T(8,128)(2,1)S(1)}, bf16[1024,512]{1,0:T(8,128)(2,1)}, u32[]{:S(2)}) copy-start(bf16[1024,512]{1,0:T(8,128)(2,1)} %q_ref.3) | copy-start | bytes 3145732
  9.9 5.8 %collective-permute-start.2 = (bf16[4,128,128]{2,1,0:T(8,128)(2,1)S(1)}, bf16[4,128,128]{2,1,0:T(8,128)(2,1)S(1)}, u32[]{:S(2)}, u32[]{:S(2)}) collective-permute-start(bf16[4,128,128]{2,1,0:T(8,128)(2,1)S(1)} %get-tuple-element.26), channel_id=1, source_target_pairs={{0,8},{4,12},{8,0},{12,4},{1,9},{5,13},{9,1},{13,5},{2,10},{6,14},... | collective-permute-start | bytes 393224 | tf_op jit(solution)/shard_map/ppermute | solution.py:31

commit v13 on v11

--- a/solution.py
+++ b/solution.py
@@ -287,14 +287,17 @@
     col = lax.broadcasted_iota(jnp.int32, (block, block), 1)
     mask = jnp.where(col >= row, 0.0, NEG).astype(F32)
 
+    half = block // 2
+
     def copy_out(start):
-        rows = pl.ds(start * stride, block * stride)
-        return pltpu.make_async_copy(packed.at[rows, :], out_hbm.at[rows, :], out_sems.at[start // block])
+        rows = pl.ds(start * stride, half * stride)
+        return pltpu.make_async_copy(packed.at[rows, :], out_hbm.at[rows, :], out_sems.at[start // half])
 
     def send(start):
-        rows = pl.ds(start * stride, block * stride)
-        packed[rows, :] = mixed[rows, :].astype(BF16)
-        copy_out(start).start()
+        for at in (start, start + half):
+            rows = pl.ds(at * stride, half * stride)
+            packed[rows, :] = mixed[rows, :].astype(BF16)
+            copy_out(at).start()
 
     def attend(start):
         linear_rows(start)
@@ -320,7 +323,7 @@
         attend(start)
 
     send(tok - block)
-    for start in range(0, tok, block):
+    for start in range(0, tok, half):
         copy_out(start).wait()
 
 
@@ -336,7 +339,7 @@
             pltpu.VMEM((tok * 2 * heads, HD), F32),
             pltpu.VMEM((tok * 2 * heads, HD), BF16),
             pltpu.VMEM((heads // 2, 2 * HD, 2 * HD) if heads % 2 == 0 else (heads, HD, HD), BF16),
-            pltpu.SemaphoreType.DMA((tok // block,)),
+            pltpu.SemaphoreType.DMA((2 * tok // block,)),
         ],
         compiler_params=PARAMS,
         cost_estimate=pl.CostEstimate(

time: 22.4 us -> 22.4 us (level)
  no operation moved by 1% of the time
where the time goes in v13:
time: 22.4 us; the launch traced here: 22.2 us
  Pallas kernels  16.8 us (75%)
  starting transfers between devices  4.04 us (18%)
  waiting for transfers between devices  1.32 us (6%)
    pallas_call x1, Pallas kernels, last_call(): pl.pallas_call(functools.partial(last_kernel, heads, block, len(states)),...  6.62 us
    ppermute x2, starting transfers between devices, partner_2(): return lax.ppermute(value, axis, pairs)  3.5 us
    pallas_call x1, Pallas kernels, linear_call(): pl.pallas_call(functools.partial(linear_kernel, heads), in_specs=[SMEM, V...  3.4 us
    pallas_call x1, Pallas kernels, own_call(): pl.pallas_call(functools.partial(own_kernel, heads, block), in_specs=[VME...  3.2 us
    pallas_call x1, Pallas kernels, first_call(): pl.pallas_call(functools.partial(first_kernel, heads), in_specs=[SMEM, HB...  2.19 us
    pallas_call x1, Pallas kernels, unpack_call(): pl.pallas_call(unpack_kernel, in_specs=[ANY], out_specs=[VMEM] * 2, out_s...  1.37 us
    ppermute x2, waiting for transfers between devices, partner_2(): return lax.ppermute(value, axis, pairs)  1.32 us
    ppermute x1, starting transfers between devices, passed_along(): return lax.ppermute(x, axis, pairs)  0.54 us
  transfers between devices with their start and end apart: 3, of which 2 were waited for; matrix products, arithmetic and copies ran while one was open for 0% of the time, Pallas kernels for 36%

profile of v13, /device:TPU:0, one launch (start us, length us, event | category | flops | bytes accessed | tf_op | source)
XLA Modules:
  0.0 22.2 jit_solution(13442095824750605340)
XLA Ops:
  0.0 0.0 copy-start.1
  0.0 2.2 %shard_map.46 = (bf16[1024,2,128]{2,1,0:T(2,128)(2,1)}, bf16[4,128,128]{2,1,0:T(8,128)(2,1)S(1)}, bf16[3,1024,512]{2,1,0:T(8,128)(2,1)S(1)}) custom-call(s32[1]{0:T(128)} %bitcast.2.index_ref, bf16[1024,2,2,128]{3,2,1,0:T(2,128)(2,1)} %bitcast.16, bf16[3,1024,512]{2,1,0:T(8,128)(2,1)} %bitcast.15), custom_call_target="tpu_custom_call" | custom-call | flops 134217728 | bytes 2097152 | tf_op jit(solution)/shard_map/pallas_call | solution.py:93
  2.2 0.5 %collective-permute-start.1 = (bf16[2048,128]{1,0:T(8,128)(2,1)}, bf16[2048,128]{1,0:T(8,128)(2,1)}, u32[]{:S(2)}, u32[]{:S(2)}) collective-permute-start(bf16[2048,128]{1,0:T(8,128)(2,1)} %bitcast.6.own_ref), channel_id=1, source_target_pairs={{0,4},{4,8},{8,12},{12,0},{1,5},{5,9},{9,13},{13,1},{2,6},{6,10},{... | collective-permute-start | bytes 1572872 | tf_op jit(solution)/shard_map/ppermute | solution.py:37
  2.7 2.6 %collective-permute-start = (bf16[4,128,128]{2,1,0:T(8,128)(2,1)S(1)}, bf16[4,128,128]{2,1,0:T(8,128)(2,1)S(1)}, u32[]{:S(2)}, u32[]{:S(2)}) collective-permute-start(bf16[4,128,128]{2,1,0:T(8,128)(2,1)S(1)} %get-tuple-element.18.mine_ref), channel_id=1, source_target_pairs={{0,4},{4,0},{8,12},{12,8},{1,5},{5,1},{9,13},{13,9},{2,6},{6,2},{1... | collective-permute-start | bytes 393224 | tf_op jit(solution)/shard_map/ppermute | solution.py:31
  5.3 0.0 copy-start
  5.3 1.0 %collective-permute-done.near_ref.refs_0_ = bf16[4,128,128]{2,1,0:T(8,128)(2,1)S(1)} collective-permute-done((bf16[4,128,128]{2,1,0:T(8,128)(2,1)S(1)}, bf16[4,128,128]{2,1,0:T(8,128)(2,1)S(1)}, u32[]{:S(2)}, u32[]{:S(2)}) %collective-permute-start) | collective-permute-done | bytes 131104 | tf_op jit(solution)/shard_map/ppermute | solution.py:31
  6.3 0.0 copy-done.1
  6.3 3.4 %shard_map.47 = (f32[1024,512]{1,0:T(8,128)S(1)}, bf16[4,128,128]{2,1,0:T(8,128)(2,1)S(1)}, bf16[1024,256]{1,0:T(8,128)(2,1)S(1)}, bf16[1024,256]{1,0:T(8,128)(2,1)S(1)}) custom-call(f32[4,16]{1,0:T(4,128)S(1)} %bitcast.13, bf16[3,1024,512]{2,1,0:T(8,128)(2,1)S(1)} %get-tuple-element.16.x_ref, bf16[2048,128]{1,0:T(8,128)(2,1)} %bitcast.6.own_ref, ...), custom_call_target="tpu_custom_call" | custom-call | flops 1073741824 | bytes 5242880 | tf_op jit(solution)/shard_map/pallas_call | solution.py:174
  9.7 0.9 %collective-permute-start.2 = (bf16[4,128,128]{2,1,0:T(8,128)(2,1)S(1)}, bf16[4,128,128]{2,1,0:T(8,128)(2,1)S(1)}, u32[]{:S(2)}, u32[]{:S(2)}) collective-permute-start(bf16[4,128,128]{2,1,0:T(8,128)(2,1)S(1)} %get-tuple-element.26), channel_id=1, source_target_pairs={{0,8},{4,12},{8,0},{12,4},{1,9},{5,13},{9,1},{13,5},{2,10},{6,14},... | collective-permute-start | bytes 393224 | tf_op jit(solution)/shard_map/ppermute | solution.py:31
  10.6 0.0 copy-done
  10.6 3.2 %shard_map.49 = (f32[4,1024,256]{2,1,0:T(8,128)S(1)}, f32[4,1024,128]{2,1,0:T(8,128)S(1)}) custom-call(bf16[1024,512]{1,0:T(8,128)(2,1)S(1)} %copy-done, bf16[1024,256]{1,0:T(8,128)(2,1)S(1)} %get-tuple-element.22.k_own, bf16[1024,256]{1,0:T(8,128)(2,1)S(1)} %get-tuple-element.23.v_own), custom_call_target="tpu_custom_call" | custom-call | flops 1610612736 | bytes 3145728 | tf_op jit(solution)/shard_map/pallas_call | solution.py:216
  13.8 0.0 collective-permute-done.1.before_ref
  13.8 1.4 %shard_map.48 = (bf16[1024,256]{1,0:T(8,128)(2,1)S(1)}, bf16[1024,256]{1,0:T(8,128)(2,1)S(1)}) custom-call(bf16[2048,128]{1,0:T(8,128)(2,1)} %collective-permute-done.1.before_ref), custom_call_target="tpu_custom_call" | custom-call | bytes 2097152 | tf_op jit(solution)/shard_map/pallas_call | solution.py:238
  15.2 0.3 %collective-permute-done.2.refs_1_ = bf16[4,128,128]{2,1,0:T(8,128)(2,1)S(1)} collective-permute-done((bf16[4,128,128]{2,1,0:T(8,128)(2,1)S(1)}, bf16[4,128,128]{2,1,0:T(8,128)(2,1)S(1)}, u32[]{:S(2)}, u32[]{:S(2)}) %collective-permute-start.2) | collective-permute-done | bytes 131104 | tf_op jit(solution)/shard_map/ppermute | solution.py:31
  15.6 6.6 %shard_map.50 = bf16[8192,128]{1,0:T(8,128)(2,1)} custom-call(s32[1]{0:T(128)} %bitcast.place_ref, f32[4,16]{1,0:T(4,128)S(1)} %bitcast.14, bf16[1024,512]{1,0:T(8,128)(2,1)S(1)} %copy-done, f32[1024,512]{1,0:T(8,128)S(1)} %get-tuple-element.19.lin_ref, bf16[3,1024,512]{2,1,0:T(8,128)(2,1)S(1)} %get-tuple-element.16.x_ref, ...), custom_call_target="tpu_custom_call" | custom-call | flops 2147483648 | bytes 7340032 | tf_op jit(solution)/shard_map/pallas_call | solution.py:333
Async XLA Ops:
  0.0 6.3 %copy-start.1 = (f32[16,4]{0,1:T(4,128)S(1)}, f32[16,4]{0,1:T(4,128)}, u32[]{:S(2)}) copy-start(f32[16,4]{0,1:T(4,128)} %param.5) | copy-start | bytes 772
  2.2 11.6 %collective-permute-start.1 = (bf16[2048,128]{1,0:T(8,128)(2,1)}, bf16[2048,128]{1,0:T(8,128)(2,1)}, u32[]{:S(2)}, u32[]{:S(2)}) collective-permute-start(bf16[2048,128]{1,0:T(8,128)(2,1)} %bitcast.6.own_ref), channel_id=1, source_target_pairs={{0,4},{4,8},{8,12},{12,0},{1,5},{5,9},{9,13},{13,1},{2,6},{6,10},{... | collective-permute-start | bytes 1572872 | tf_op jit(solution)/shard_map/ppermute | solution.py:37
  2.7 3.6 %collective-permute-start = (bf16[4,128,128]{2,1,0:T(8,128)(2,1)S(1)}, bf16[4,128,128]{2,1,0:T(8,128)(2,1)S(1)}, u32[]{:S(2)}, u32[]{:S(2)}) collective-permute-start(bf16[4,128,128]{2,1,0:T(8,128)(2,1)S(1)} %get-tuple-element.18.mine_ref), channel_id=1, source_target_pairs={{0,4},{4,0},{8,12},{12,8},{1,5},{5,1},{9,13},{13,9},{2,6},{6,2},{1... | collective-permute-start | bytes 393224 | tf_op jit(solution)/shard_map/ppermute | solution.py:31
  5.3 5.3 %copy-start = (bf16[1024,512]{1,0:T(8,128)(2,1)S(1)}, bf16[1024,512]{1,0:T(8,128)(2,1)}, u32[]{:S(2)}) copy-start(bf16[1024,512]{1,0:T(8,128)(2,1)} %q_ref.3) | copy-start | bytes 3145732
  9.7 5.8 %collective-permute-start.2 = (bf16[4,128,128]{2,1,0:T(8,128)(2,1)S(1)}, bf16[4,128,128]{2,1,0:T(8,128)(2,1)S(1)}, u32[]{:S(2)}, u32[]{:S(2)}) collective-permute-start(bf16[4,128,128]{2,1,0:T(8,128)(2,1)S(1)} %get-tuple-element.26), channel_id=1, source_target_pairs={{0,8},{4,12},{8,0},{12,4},{1,9},{5,13},{9,1},{13,5},{2,10},{6,14},... | collective-permute-start | bytes 393224 | tf_op jit(solution)/shard_map/ppermute | solution.py:31

commit v14 on v13

--- a/solution.py
+++ b/solution.py
@@ -287,15 +287,15 @@
     col = lax.broadcasted_iota(jnp.int32, (block, block), 1)
     mask = jnp.where(col >= row, 0.0, NEG).astype(F32)
 
-    half = block // 2
+    part = block // 4
 
     def copy_out(start):
-        rows = pl.ds(start * stride, half * stride)
-        return pltpu.make_async_copy(packed.at[rows, :], out_hbm.at[rows, :], out_sems.at[start // half])
+        rows = pl.ds(start * stride, part * stride)
+        return pltpu.make_async_copy(packed.at[rows, :], out_hbm.at[rows, :], out_sems.at[start // part])
 
     def send(start):
-        for at in (start, start + half):
-            rows = pl.ds(at * stride, half * stride)
+        for at in range(start, start + block, part):
+            rows = pl.ds(at * stride, part * stride)
             packed[rows, :] = mixed[rows, :].astype(BF16)
             copy_out(at).start()
 
@@ -323,7 +323,7 @@
         attend(start)
 
     send(tok - block)
-    for start in range(0, tok, half):
+    for start in range(0, tok, part):
         copy_out(start).wait()
 
 
@@ -339,7 +339,7 @@
             pltpu.VMEM((tok * 2 * heads, HD), F32),
             pltpu.VMEM((tok * 2 * heads, HD), BF16),
             pltpu.VMEM((heads // 2, 2 * HD, 2 * HD) if heads % 2 == 0 else (heads, HD, HD), BF16),
-            pltpu.SemaphoreType.DMA((2 * tok // block,)),
+            pltpu.SemaphoreType.DMA((4 * tok // block,)),
         ],
         compiler_params=PARAMS,
         cost_estimate=pl.CostEstimate(

time: 22.4 us -> 22.4 us (level)
  no operation moved by 1% of the time
where the time goes in v14:
time: 22.4 us; the launch traced here: 22.2 us
  Pallas kernels  16.8 us (75%)
  starting transfers between devices  4.04 us (18%)
  waiting for transfers between devices  1.32 us (6%)
    pallas_call x1, Pallas kernels, last_call(): pl.pallas_call(functools.partial(last_kernel, heads, block, len(states)),...  6.66 us
    ppermute x2, starting transfers between devices, partner_2(): return lax.ppermute(value, axis, pairs)  3.5 us
    pallas_call x1, Pallas kernels, linear_call(): pl.pallas_call(functools.partial(linear_kernel, heads), in_specs=[SMEM, V...  3.4 us
    pallas_call x1, Pallas kernels, own_call(): pl.pallas_call(functools.partial(own_kernel, heads, block), in_specs=[VME...  3.2 us
    pallas_call x1, Pallas kernels, first_call(): pl.pallas_call(functools.partial(first_kernel, heads), in_specs=[SMEM, HB...  2.19 us
    pallas_call x1, Pallas kernels, unpack_call(): pl.pallas_call(unpack_kernel, in_specs=[ANY], out_specs=[VMEM] * 2, out_s...  1.37 us
    ppermute x2, waiting for transfers between devices, partner_2(): return lax.ppermute(value, axis, pairs)  1.32 us
    ppermute x1, starting transfers between devices, passed_along(): return lax.ppermute(x, axis, pairs)  0.54 us
  transfers between devices with their start and end apart: 3, of which 2 were waited for; matrix products, arithmetic and copies ran while one was open for 0% of the time, Pallas kernels for 36%

profile of v14, /device:TPU:0, one launch (start us, length us, event | category | flops | bytes accessed | tf_op | source)
XLA Modules:
  0.0 22.2 jit_solution(14536001947597229042)
XLA Ops:
  0.0 0.0 copy-start.1
  0.0 2.2 %shard_map.46 = (bf16[1024,2,128]{2,1,0:T(2,128)(2,1)}, bf16[4,128,128]{2,1,0:T(8,128)(2,1)S(1)}, bf16[3,1024,512]{2,1,0:T(8,128)(2,1)S(1)}) custom-call(s32[1]{0:T(128)} %bitcast.2.index_ref, bf16[1024,2,2,128]{3,2,1,0:T(2,128)(2,1)} %bitcast.16, bf16[3,1024,512]{2,1,0:T(8,128)(2,1)} %bitcast.15), custom_call_target="tpu_custom_call" | custom-call | flops 134217728 | bytes 2097152 | tf_op jit(solution)/shard_map/pallas_call | solution.py:93
  2.2 0.5 %collective-permute-start.1 = (bf16[2048,128]{1,0:T(8,128)(2,1)}, bf16[2048,128]{1,0:T(8,128)(2,1)}, u32[]{:S(2)}, u32[]{:S(2)}) collective-permute-start(bf16[2048,128]{1,0:T(8,128)(2,1)} %bitcast.6.own_ref), channel_id=1, source_target_pairs={{0,4},{4,8},{8,12},{12,0},{1,5},{5,9},{9,13},{13,1},{2,6},{6,10},{... | collective-permute-start | bytes 1572872 | tf_op jit(solution)/shard_map/ppermute | solution.py:37
  2.7 2.6 %collective-permute-start = (bf16[4,128,128]{2,1,0:T(8,128)(2,1)S(1)}, bf16[4,128,128]{2,1,0:T(8,128)(2,1)S(1)}, u32[]{:S(2)}, u32[]{:S(2)}) collective-permute-start(bf16[4,128,128]{2,1,0:T(8,128)(2,1)S(1)} %get-tuple-element.18.mine_ref), channel_id=1, source_target_pairs={{0,4},{4,0},{8,12},{12,8},{1,5},{5,1},{9,13},{13,9},{2,6},{6,2},{1... | collective-permute-start | bytes 393224 | tf_op jit(solution)/shard_map/ppermute | solution.py:31
  5.3 0.0 copy-start
  5.3 1.0 %collective-permute-done.near_ref.refs_0_ = bf16[4,128,128]{2,1,0:T(8,128)(2,1)S(1)} collective-permute-done((bf16[4,128,128]{2,1,0:T(8,128)(2,1)S(1)}, bf16[4,128,128]{2,1,0:T(8,128)(2,1)S(1)}, u32[]{:S(2)}, u32[]{:S(2)}) %collective-permute-start) | collective-permute-done | bytes 131104 | tf_op jit(solution)/shard_map/ppermute | solution.py:31
  6.3 0.0 copy-done.1
  6.3 3.4 %shard_map.47 = (f32[1024,512]{1,0:T(8,128)S(1)}, bf16[4,128,128]{2,1,0:T(8,128)(2,1)S(1)}, bf16[1024,256]{1,0:T(8,128)(2,1)S(1)}, bf16[1024,256]{1,0:T(8,128)(2,1)S(1)}) custom-call(f32[4,16]{1,0:T(4,128)S(1)} %bitcast.13, bf16[3,1024,512]{2,1,0:T(8,128)(2,1)S(1)} %get-tuple-element.16.x_ref, bf16[2048,128]{1,0:T(8,128)(2,1)} %bitcast.6.own_ref, ...), custom_call_target="tpu_custom_call" | custom-call | flops 1073741824 | bytes 5242880 | tf_op jit(solution)/shard_map/pallas_call | solution.py:174
  9.7 0.9 %collective-permute-start.2 = (bf16[4,128,128]{2,1,0:T(8,128)(2,1)S(1)}, bf16[4,128,128]{2,1,0:T(8,128)(2,1)S(1)}, u32[]{:S(2)}, u32[]{:S(2)}) collective-permute-start(bf16[4,128,128]{2,1,0:T(8,128)(2,1)S(1)} %get-tuple-element.26), channel_id=1, source_target_pairs={{0,8},{4,12},{8,0},{12,4},{1,9},{5,13},{9,1},{13,5},{2,10},{6,14},... | collective-permute-start | bytes 393224 | tf_op jit(solution)/shard_map/ppermute | solution.py:31
  10.6 0.0 copy-done
  10.6 3.2 %shard_map.49 = (f32[4,1024,256]{2,1,0:T(8,128)S(1)}, f32[4,1024,128]{2,1,0:T(8,128)S(1)}) custom-call(bf16[1024,512]{1,0:T(8,128)(2,1)S(1)} %copy-done, bf16[1024,256]{1,0:T(8,128)(2,1)S(1)} %get-tuple-element.22.k_own, bf16[1024,256]{1,0:T(8,128)(2,1)S(1)} %get-tuple-element.23.v_own), custom_call_target="tpu_custom_call" | custom-call | flops 1610612736 | bytes 3145728 | tf_op jit(solution)/shard_map/pallas_call | solution.py:216
  13.8 0.0 collective-permute-done.1.before_ref
  13.8 1.4 %shard_map.48 = (bf16[1024,256]{1,0:T(8,128)(2,1)S(1)}, bf16[1024,256]{1,0:T(8,128)(2,1)S(1)}) custom-call(bf16[2048,128]{1,0:T(8,128)(2,1)} %collective-permute-done.1.before_ref), custom_call_target="tpu_custom_call" | custom-call | bytes 2097152 | tf_op jit(solution)/shard_map/pallas_call | solution.py:238
  15.2 0.3 %collective-permute-done.2.refs_1_ = bf16[4,128,128]{2,1,0:T(8,128)(2,1)S(1)} collective-permute-done((bf16[4,128,128]{2,1,0:T(8,128)(2,1)S(1)}, bf16[4,128,128]{2,1,0:T(8,128)(2,1)S(1)}, u32[]{:S(2)}, u32[]{:S(2)}) %collective-permute-start.2) | collective-permute-done | bytes 131104 | tf_op jit(solution)/shard_map/ppermute | solution.py:31
  15.6 6.7 %shard_map.50 = bf16[8192,128]{1,0:T(8,128)(2,1)} custom-call(s32[1]{0:T(128)} %bitcast.place_ref, f32[4,16]{1,0:T(4,128)S(1)} %bitcast.14, bf16[1024,512]{1,0:T(8,128)(2,1)S(1)} %copy-done, f32[1024,512]{1,0:T(8,128)S(1)} %get-tuple-element.19.lin_ref, bf16[3,1024,512]{2,1,0:T(8,128)(2,1)S(1)} %get-tuple-element.16.x_ref, ...), custom_call_target="tpu_custom_call" | custom-call | flops 2147483648 | bytes 7340032 | tf_op jit(solution)/shard_map/pallas_call | solution.py:333
Async XLA Ops:
  0.0 6.3 %copy-start.1 = (f32[16,4]{0,1:T(4,128)S(1)}, f32[16,4]{0,1:T(4,128)}, u32[]{:S(2)}) copy-start(f32[16,4]{0,1:T(4,128)} %param.5) | copy-start | bytes 772
  2.2 11.6 %collective-permute-start.1 = (bf16[2048,128]{1,0:T(8,128)(2,1)}, bf16[2048,128]{1,0:T(8,128)(2,1)}, u32[]{:S(2)}, u32[]{:S(2)}) collective-permute-start(bf16[2048,128]{1,0:T(8,128)(2,1)} %bitcast.6.own_ref), channel_id=1, source_target_pairs={{0,4},{4,8},{8,12},{12,0},{1,5},{5,9},{9,13},{13,1},{2,6},{6,10},{... | collective-permute-start | bytes 1572872 | tf_op jit(solution)/shard_map/ppermute | solution.py:37
  2.7 3.6 %collective-permute-start = (bf16[4,128,128]{2,1,0:T(8,128)(2,1)S(1)}, bf16[4,128,128]{2,1,0:T(8,128)(2,1)S(1)}, u32[]{:S(2)}, u32[]{:S(2)}) collective-permute-start(bf16[4,128,128]{2,1,0:T(8,128)(2,1)S(1)} %get-tuple-element.18.mine_ref), channel_id=1, source_target_pairs={{0,4},{4,0},{8,12},{12,8},{1,5},{5,1},{9,13},{13,9},{2,6},{6,2},{1... | collective-permute-start | bytes 393224 | tf_op jit(solution)/shard_map/ppermute | solution.py:31
  5.3 5.3 %copy-start = (bf16[1024,512]{1,0:T(8,128)(2,1)S(1)}, bf16[1024,512]{1,0:T(8,128)(2,1)}, u32[]{:S(2)}) copy-start(bf16[1024,512]{1,0:T(8,128)(2,1)} %q_ref.3) | copy-start | bytes 3145732
  9.7 5.8 %collective-permute-start.2 = (bf16[4,128,128]{2,1,0:T(8,128)(2,1)S(1)}, bf16[4,128,128]{2,1,0:T(8,128)(2,1)S(1)}, u32[]{:S(2)}, u32[]{:S(2)}) collective-permute-start(bf16[4,128,128]{2,1,0:T(8,128)(2,1)S(1)} %get-tuple-element.26), channel_id=1, source_target_pairs={{0,8},{4,12},{8,0},{12,4},{1,9},{5,13},{9,1},{13,5},{2,10},{6,14},... | collective-permute-start | bytes 393224 | tf_op jit(solution)/shard_map/ppermute | solution.py:31
